TPU v7x, 512 devices: a whole 4x8x8 slice. The times are simulated.
512 devices in a mesh: stn: 16 (over z, core), chan: 32 (over y, x).
Axes of the slice: x: 4, y: 8, z: 8, core: 2. Of those that a mesh axis runs over, the one named last changes fastest.
Arguments:
- voltages: bfloat16 [256, 2048, 512], P('stn', 'chan'), may hold values from -6 to 6
- block_facet: int32 [32, 16, 2048, 1], P('chan', 'stn'), may hold values from 0 to 15; in each aligned block of 2048 rows (0 to 2047, 2048 to 4095, ..., all dimensions but the last counted through in order) at most 192 rows name the same one
- block_tile: int32 [32, 16, 2048], P('chan', 'stn'), may hold values from 0 to 15
- vis_offset: int32 [32, 16, 2048, 128], P('chan', 'stn'), may hold values from 0 to 624
- kernel_taps: bfloat16 [2, 8], replicated, may hold values from 0.19921875 to 1
Outputs:
- image: float32 [2, 2048, 128], P(None, ('stn', 'chan'))
Inputs may be any that keep to these rules, and one draw needn't show every extreme that they name: `block_facet`: among the blocks of one device (one index of the first two dimensions) at most 192 name one facet; in every draw some facet is named by exactly 192 of some device's blocks.
All inputs are finite; a program needn't handle non-finite values.
Results may differ from a plain program's by a relative error of at most 0.0041.
Values may be sent and summed in bfloat16 or wider, within the bound.
A program may use at most 64 MiB of HBM per device.

v0:
```python
import math

import jax
import jax.numpy as jnp
from jax import lax
from jax.sharding import PartitionSpec as P

VB = 128
TILE = 32
KT = 8
TS = 4
TT = 16
OFFS = 25


def kernel_rows(offsets, taps_row):
    cell_ids = jnp.arange(TILE, dtype=jnp.int32)
    distance = cell_ids[None, :, None] - offsets[:, None, :]
    weights_sum = jnp.zeros(distance.shape, jnp.float32)
    for tap_index in range(KT):
        weights_sum = weights_sum + jnp.where(
            distance == tap_index, taps_row[tap_index].astype(jnp.float32), jnp.float32(0.0)
        )
    return weights_sum.astype(jnp.bfloat16)


def block_tiles(values, offsets, kernel_taps):
    along_u = kernel_rows(offsets // OFFS, kernel_taps[0])
    along_v = kernel_rows(offsets % OFFS, kernel_taps[1])
    weighted = (
        values[:, :, None, :].astype(jnp.float32) * along_v[:, None, :, :].astype(jnp.float32)
    ).astype(jnp.bfloat16)
    weighted = weighted.reshape(values.shape[0], 2 * TILE, values.shape[2])
    return jnp.einsum("nux,nwx->nuw", along_u, weighted, preferred_element_type=jnp.float32)


def grid_blocks(values, offsets, target_ids, kernel_taps, segments):
    slot_count = values.shape[0]
    group_size = math.gcd(slot_count, 256)
    tile_width = 2 * TILE * TILE
    segment_ids = jnp.arange(segments, dtype=jnp.int32)

    def accumulate(grids, turn_index):
        first_row = turn_index * group_size
        part_values = lax.dynamic_slice_in_dim(values, first_row, group_size, 0)
        part_offsets = lax.dynamic_slice_in_dim(offsets, first_row, group_size, 0)
        part_targets = lax.dynamic_slice_in_dim(target_ids, first_row, group_size, 0)
        tile_sums = block_tiles(part_values, part_offsets, kernel_taps).reshape(
            group_size, tile_width
        )
        placing = (segment_ids[:, None] == part_targets[None, :]).astype(jnp.float32)
        grids = grids + jnp.dot(
            placing, tile_sums, precision=lax.Precision.HIGHEST, preferred_element_type=jnp.float32
        )
        return (grids, None)

    start_grids = jnp.zeros((segments, tile_width), jnp.float32)
    grids, leftover = lax.scan(accumulate, start_grids, jnp.arange(slot_count // group_size))
    return grids


def facet_grid(tile_grid):
    shaped = tile_grid.reshape(TS, TS, TILE, 2, TILE)
    return jnp.transpose(shaped, (3, 0, 2, 1, 4)).reshape(2, TS * TILE, TS * TILE)


def dft_tables(side):
    index_ids = jnp.arange(side, dtype=jnp.int32)
    phases = index_ids[:, None] * index_ids[None, :] % side
    angles = phases.astype(jnp.float32) * (2.0 * math.pi / side)
    return (jnp.cos(angles), jnp.sin(angles))


def column_pass(grid, cosine, sine):
    high = lax.Precision.HIGHEST
    real_cols = jnp.dot(grid[0], cosine, precision=high) + jnp.dot(grid[1], sine, precision=high)
    imag_cols = jnp.dot(grid[1], cosine, precision=high) - jnp.dot(grid[0], sine, precision=high)
    return (real_cols, imag_cols)


def row_pass(real_cols, imag_cols, cosine_rows, sine_rows):
    high = lax.Precision.HIGHEST
    real_rows = jnp.dot(cosine_rows, real_cols, precision=high) + jnp.dot(
        sine_rows, imag_cols, precision=high
    )
    imag_rows = jnp.dot(cosine_rows, imag_cols, precision=high) - jnp.dot(
        sine_rows, real_cols, precision=high
    )
    return (real_rows, imag_rows)


def body(voltages, block_facet, block_tile, vis_offset, kernel_taps):
    facets = lax.axis_size("stn")
    chan_count = lax.axis_size("chan")
    panels = lax.all_to_all(voltages, "stn", split_axis=1, concat_axis=0, tiled=True)
    stations = panels.shape[0]
    local_channels = panels.shape[1]
    samples = panels.shape[2] // 2
    swapped = jnp.concatenate([panels[:, :, samples:], -panels[:, :, :samples]], axis=2)
    stacked = jnp.concatenate([panels, swapped], axis=0)
    products = jnp.einsum("aks,jks->kaj", stacked, panels, preferred_element_type=jnp.float32)
    station_ids = jnp.arange(stations, dtype=jnp.int32)
    off_diagonal = (station_ids[:, None] != station_ids[None, :]).astype(jnp.float32)
    scale = 1.0 / math.sqrt(samples)
    real_vis = (products[:, :stations, :] * scale * off_diagonal).astype(jnp.bfloat16)
    imag_vis = (products[:, stations:, :] * scale * off_diagonal).astype(jnp.bfloat16)
    block_values = jnp.stack([real_vis.reshape(-1, VB), imag_vis.reshape(-1, VB)], axis=1)
    block_count = block_values.shape[0]
    offsets = vis_offset.reshape(block_count, VB)
    tile_ids = block_tile.reshape(block_count)
    facet_ids = block_facet.reshape(block_count)
    capacity = 3 * block_count // (2 * facets)
    facet_range = jnp.arange(facets, dtype=jnp.int32)
    member = (facet_ids[:, None] == facet_range[None, :]).astype(jnp.int32)
    earlier = jnp.cumsum(member, axis=0) - member
    position = jnp.sum(earlier * member, axis=1)
    slot_ids = facet_ids * capacity + position
    send_values = jnp.zeros((facets * capacity, 2, VB), jnp.bfloat16).at[slot_ids].set(block_values)
    send_offsets = jnp.zeros((facets * capacity, VB), jnp.int32).at[slot_ids].set(offsets)
    send_tiles = jnp.zeros((facets * capacity,), jnp.int32).at[slot_ids].set(tile_ids)
    got_values, got_offsets, got_tiles = (
        lax.all_to_all(send_values, "stn", split_axis=0, concat_axis=0, tiled=True),
        lax.all_to_all(send_offsets, "stn", split_axis=0, concat_axis=0, tiled=True),
        lax.all_to_all(send_tiles, "stn", split_axis=0, concat_axis=0, tiled=True),
    )
    tile_grid = grid_blocks(got_values, got_offsets, got_tiles, kernel_taps, TT)
    grid = facet_grid(tile_grid)
    side = grid.shape[1]
    row_count = side // chan_count
    channels_all = local_channels * facets * chan_count
    norm_factor = 1.0 / math.sqrt(channels_all * stations * stations * KT * KT / facets)
    cosine, sine = dft_tables(side)
    summed = lax.psum(grid, "chan")
    real_cols, imag_cols = column_pass(summed, cosine, sine)
    first_row = lax.axis_index("chan") * row_count
    cosine_rows = lax.dynamic_slice_in_dim(cosine, first_row, row_count, 0)
    sine_rows = lax.dynamic_slice_in_dim(sine, first_row, row_count, 0)
    real_rows, imag_rows = row_pass(real_cols, imag_cols, cosine_rows, sine_rows)
    image = jnp.stack([real_rows, imag_rows], axis=0) * norm_factor
    return image


def solution(mesh):
    placed = (
        P("stn", "chan", None),
        P("chan", "stn", None, None),
        P("chan", "stn", None),
        P("chan", "stn", None, None),
        P(),
    )
    return jax.shard_map(
        body, mesh=mesh, in_specs=placed, out_specs=P(None, ("stn", "chan"), None), check_vma=False
    )
```

profile of v0, /device:TPU:1, one launch (start us, length us, event | category | flops | bytes accessed | tf_op | source)
XLA Modules:
  0.0 873.3 jit_solution(455187938880387183)
XLA Ops:
  7.3 4.5 reduce-window.6
  14.1 8.2 scatter_custom_fusion
  23.0 11.8 %all-to-all-start = ((s32[16,192,1]{1,2,0:T(1,128)}), s32[16,192,1]{1,2,0:T(1,128)S(1)}, u32[]{:S(2)}, u32[]{:S(2)}) async-start(s32[16,192,1]{1,2,0:T(1,128)} %all_to_all.43), calls=%async_computation | async-start | bytes 32768 | tf_op jit(solution)/shard_map/all_to_all | solution.py:124
  37.6 4.6 all-to-all-done
  42.2 3.8 all-to-all-start.2
  46.0 6.8 scatter_custom_fusion.1
  52.9 21.1 %all-to-all-done.2 = bf16[16,64,512]{2,0,1:T(8,128)(2,1)S(1)} async-done(((bf16[16,64,512]{2,0,1:T(8,128)(2,1)}), bf16[16,64,512]{2,0,1:T(8,128)(2,1)S(1)}, u32[]{:S(2)}, u32[]{:S(2)}) %all-to-all-start.2) | async-done | bytes 1048608 | tf_op jit(solution)/shard_map/all_to_all | solution.py:95
  74.0 4.3 all-to-all-start.1
  86.8 185.9 %scatter_fusion = bf16[3072,2,128]{2,1,0:T(2,128)(2,1)} fusion(bf16[3072,2,128]{2,1,0:T(2,128)(2,1)} %broadcast_in_dim.128, s32[2048]{0:T(1024)S(1)} %bitcast.146, bf16[2048,2,128]{2,1,0:T(2,128)(2,1)S(1)} %pad_maximum_fusion), kind=kCustom, calls=%fused_computation.2 | custom fusion | bytes 3153920 | tf_op jit(solution)/shard_map/scatter | solution.py:118
  272.8 6.5 all-to-all-start.3
  279.6 38.2 %all-to-all-done.3 = bf16[3072,2,128]{2,1,0:T(2,128)(2,1)} async-done(((bf16[3072,2,128]{2,1,0:T(2,128)(2,1)}), bf16[3072,2,128]{2,1,0:T(2,128)(2,1)}, u32[]{:S(2)}, u32[]{:S(2)}) %all-to-all-start.3) | async-done | bytes 1572896 | tf_op jit(solution)/shard_map/all_to_all | solution.py:122
  317.8 394.3 %while.13 = (s32[]{:T(128)}, f32[16,2048]{1,0:T(8,128)S(1)}, s32[12]{0:T(128)S(1)}, s32[3072]{0:T(1024)S(1)}, s32[3072,128]{1,0:T(8,128)}, /*index=5*/bf16[2,8]{...) while((s32[]{:T(128)}, f32[16,2048]{1,0:T(8,128)S(1)}, ...), condition=%wide.region_7.8_spmd.clone, body=%wide.region_6.7_spmd.clone.sunk | while | flops 293081088 | bytes 26742172 | solution.py:58
  338.3 7.6 fusion.128
  346.0 3.5 copy.26
  371.2 7.6 fusion.128
  378.8 3.5 copy.26
  404.0 7.6 fusion.128
  411.7 3.5 copy.26
  436.9 7.6 fusion.128
  444.5 3.5 copy.26
  469.7 7.6 fusion.128
  477.3 3.5 copy.26
  502.6 7.6 fusion.128
  535.4 7.6 fusion.128
  568.3 7.6 fusion.128
  601.1 7.6 fusion.128
  634.0 7.6 fusion.128
  641.6 3.5 copy.26
  666.8 7.6 fusion.128
  699.6 7.6 fusion.128
  707.3 3.5 copy.26
  714.4 145.6 %all-reduce.2.cloned.1.call-done = f32[2,128,128]{2,1,0:T(8,128)} async-done(((f32[2,128,128]{2,1,0:T(8,128)}), f32[2,128,128]{2,1,0:T(8,128)}) %all-reduce.2.cloned.1.call-update) | async-done | bytes 131088 | tf_op jit(solution)/shard_map/psum | solution.py:133
  (143 shorter events, 173.9 us)
Async XLA Ops:
  6.5 39.5 %copy-start = (s32[1,1,2048,128]{3,2,1,0:T(8,128)S(1)}, s32[1,1,2048,128]{3,2,1,0:T(8,128)}, u32[]{:S(2)}) copy-start(s32[1,1,2048,128]{3,2,1,0:T(8,128)} %param.10) | copy-start | bytes 3145732
  23.0 19.2 %all-to-all-start = ((s32[16,192,1]{1,2,0:T(1,128)}), s32[16,192,1]{1,2,0:T(1,128)S(1)}, u32[]{:S(2)}, u32[]{:S(2)}) async-start(s32[16,192,1]{1,2,0:T(1,128)} %all_to_all.43), calls=%async_computation | async-start | bytes 32768 | tf_op jit(solution)/shard_map/all_to_all | solution.py:124
  42.2 31.8 %all-to-all-start.2 = ((bf16[16,64,512]{2,0,1:T(8,128)(2,1)}), bf16[16,64,512]{2,0,1:T(8,128)(2,1)S(1)}, u32[]{:S(2)}, u32[]{:S(2)}) async-start(bf16[16,64,512]{2,0,1:T(8,128)(2,1)} %copy.16), calls=%async_computation.2 | async-start | bytes 2097152 | tf_op jit(solution)/shard_map/all_to_all | solution.py:95
  74.0 198.8 %all-to-all-start.1 = ((s32[16,192,128]{2,1,0:T(8,128)}), s32[16,192,128]{2,1,0:T(8,128)}, u32[]{:S(2)}, u32[]{:S(2)}) async-start(s32[16,192,128]{2,1,0:T(8,128)} %bitcast.8), calls=%async_computation.1 | async-start | bytes 3145728 | tf_op jit(solution)/shard_map/all_to_all | solution.py:123
  84.7 233.2 %copy-start.1 = (bf16[2,8]{1,0:T(2,128)(2,1)S(1)}, bf16[2,8]{1,0:T(2,128)(2,1)}, u32[]{:S(2)}) copy-start(bf16[2,8]{1,0:T(2,128)(2,1)} %param.11) | copy-start | bytes 100
  272.8 45.0 %all-to-all-start.3 = ((bf16[3072,2,128]{2,1,0:T(2,128)(2,1)}), bf16[3072,2,128]{2,1,0:T(2,128)(2,1)}, u32[]{:S(2)}, u32[]{:S(2)}) async-start(bf16[3072,2,128]{2,1,0:T(2,128)(2,1)} %scatter_fusion), calls=%async_computation.3 | async-start | bytes 3145728 | tf_op jit(solution)/shard_map/all_to_all | solution.py:122
  279.3 580.7 %all-reduce.2.cloned.1.call-start = ((), (), s32[]{:S(2)}) async-start(), calls=%async_computation.4 | async-start | bytes 262144 | tf_op jit(solution)/shard_map/psum | solution.py:133
Sparse Core Ops, SparseCore 0:
  714.0 145.9 all-reduce.1
where the time goes:
time: 881 us; the launch traced here: 873 us
  local copies, waits for them, and re-layouts  271 us (31%)
  waiting for transfers between devices  209 us (24%)
  loops' own time  128 us (15%)
  other arithmetic  114 us (13%)
  matrix products  111 us (13%)
  starting transfers between devices  26.7 us (3%)
  between operations  13.6 us (2%)
    scatter x1, local copies, waits for them, and re-layouts, body(): jnp.zeros((facets * capacity, 2, VB), jnp.bfloat16).at[slot_ids]  186 us
    psum x1, waiting for transfers between devices, body(): summed = lax.psum(grid, 'chan')  146 us
    another operation x1, loops' own time, grid_blocks(): lax.scan(accumulate, start_grids, jnp.arange(slot_count // group_size))  128 us
    dot_general x12, matrix products, block_tiles(): jnp.einsum('nux,nwx->nuw', along_u, weighted, preferred_element_type=jnp....  91.5 us
    dot_general x12, local copies, waits for them, and re-layouts, block_tiles(): jnp.einsum('nux,nwx->nuw', along_u, weighted, preferred_element_type=jnp....  42.5 us
    convert_element_type x12, other arithmetic, block_tiles(): along_v[:, None, :, :].astype(jnp.float32)  38.9 us
    convert_element_type x12, other arithmetic, block_tiles(): weighted = (values[:, :, None, :].astype(jnp.float32) * along_v[:, None,...  38.3 us
    all_to_all x1, waiting for transfers between devices, body(): lax.all_to_all(send_values, 'stn', split_axis=0, concat_axis=0, tiled=True)  38.2 us
  transfers between devices with their start and end apart: 5, of which 4 were waited for; matrix products, arithmetic and copies ran while one was open for 23% of the time, Pallas kernels for 0%

commit v1 on v0

v1 whole, which is shorter than its diff:
```python
import functools
import math

import jax
import jax.numpy as jnp
from jax import lax
from jax.experimental import pallas as pl
from jax.experimental.pallas import tpu as pltpu
from jax.sharding import PartitionSpec as P

VB = 128
TILE = 32
KT = 8
TS = 4
TT = 16
OFFS = 25
CHUNK = 256


def grid_kernel(seg_ref, du_ref, dv_ref, re_ref, im_ref, out_ref):
    step = pl.program_id(0)

    @pl.when(step == 0)
    def _():
        out_ref[...] = jnp.zeros_like(out_ref)

    cells = lax.broadcasted_iota(jnp.int32, (TILE, VB), 0)

    def one_block(b, carry):
        du = du_ref[pl.ds(b, 1), :]
        dv = dv_ref[pl.ds(b, 1), :]
        re = re_ref[pl.ds(b, 1), :]
        im = im_ref[pl.ds(b, 1), :]
        along_u = (cells == du).astype(jnp.float32).astype(jnp.bfloat16)
        hit_v = cells == dv
        weighted = jnp.concatenate(
            [jnp.where(hit_v, re, 0.0), jnp.where(hit_v, im, 0.0)], axis=0
        ).astype(jnp.bfloat16)
        tile_sum = lax.dot_general(
            along_u, weighted, (((1,), (1,)), ((), ())), preferred_element_type=jnp.float32
        )
        seg = seg_ref[step * CHUNK + b]
        out_ref[seg] += tile_sum
        return carry

    lax.fori_loop(0, CHUNK, one_block, 0, unroll=8)


def grid_blocks(seg_ids, du, dv, re, im, segments):
    blocks = du.shape[0]
    row_spec = pl.BlockSpec((CHUNK, VB), lambda i, seg: (i, 0))
    return pl.pallas_call(
        grid_kernel,
        out_shape=jax.ShapeDtypeStruct((segments, TILE, 2 * TILE), jnp.float32),
        grid_spec=pltpu.PrefetchScalarGridSpec(
            num_scalar_prefetch=1,
            grid=(blocks // CHUNK,),
            in_specs=[row_spec] * 4,
            out_specs=pl.BlockSpec((segments, TILE, 2 * TILE), lambda i, seg: (0, 0, 0)),
        ),
        cost_estimate=pl.CostEstimate(
            flops=blocks * TILE * VB * 2 * TILE * 2,
            bytes_accessed=blocks * VB * 16 + segments * TILE * 2 * TILE * 4,
            transcendentals=0,
        ),
    )(seg_ids, du, dv, re, im)


def dft_tables(side):
    index_ids = jnp.arange(side, dtype=jnp.int32)
    phases = index_ids[:, None] * index_ids[None, :] % side
    angles = phases.astype(jnp.float32) * (2.0 * math.pi / side)
    return (jnp.cos(angles), jnp.sin(angles))


def taps_transform(taps_row, side):
    index_ids = jnp.arange(side, dtype=jnp.int32)
    tap_ids = jnp.arange(KT, dtype=jnp.int32)
    phases = index_ids[:, None] * tap_ids[None, :] % side
    angles = phases.astype(jnp.float32) * (2.0 * math.pi / side)
    taps = taps_row.astype(jnp.float32)
    return (jnp.sum(jnp.cos(angles) * taps, axis=1), -jnp.sum(jnp.sin(angles) * taps, axis=1))


def body(voltages, block_facet, block_tile, vis_offset, kernel_taps):
    facets = lax.axis_size("stn")
    chan_count = lax.axis_size("chan")
    high = lax.Precision.HIGHEST
    panels = lax.all_to_all(voltages, "stn", split_axis=1, concat_axis=0, tiled=True)
    stations = panels.shape[0]
    local_channels = panels.shape[1]
    samples = panels.shape[2] // 2
    swapped = jnp.concatenate([panels[:, :, samples:], -panels[:, :, :samples]], axis=2)
    stacked = jnp.concatenate([panels, swapped], axis=0)
    products = jnp.einsum("aks,jks->kaj", stacked, panels, preferred_element_type=jnp.float32)
    station_ids = jnp.arange(stations, dtype=jnp.int32)
    off_diagonal = (station_ids[:, None] != station_ids[None, :]).astype(jnp.float32)
    scale = 1.0 / math.sqrt(samples)
    real_vis = (products[:, :stations, :] * scale * off_diagonal).astype(jnp.bfloat16)
    imag_vis = (products[:, stations:, :] * scale * off_diagonal).astype(jnp.bfloat16)
    re = real_vis.reshape(-1, VB).astype(jnp.float32)
    im = imag_vis.reshape(-1, VB).astype(jnp.float32)
    block_count = re.shape[0]
    offsets = vis_offset.reshape(block_count, VB)
    du = offsets // OFFS
    dv = offsets % OFFS
    seg_ids = block_facet.reshape(block_count) * TT + block_tile.reshape(block_count)
    tiles = grid_blocks(seg_ids, du, dv, re, im, facets * TT)
    side = TS * TILE
    delta = tiles.reshape(facets, TS, TS, TILE, 2, TILE)
    delta = jnp.transpose(delta, (0, 4, 1, 3, 2, 5)).reshape(facets, 2, side, side)
    cosine, sine = dft_tables(side)
    along_x = jnp.stack(
        [jnp.stack([cosine, sine], axis=1), jnp.stack([-sine, cosine], axis=1)], axis=1
    )
    rows = jnp.einsum("xqpu,fpuv->fxqv", along_x, delta, precision=high)
    rows = rows.reshape(facets * side, 2, side)
    mine = lax.psum_scatter(rows, ("stn", "chan"), scatter_dimension=0, tiled=True)
    row_count = mine.shape[0]
    along_y = jnp.stack(
        [jnp.stack([cosine, -sine], axis=1), jnp.stack([sine, cosine], axis=1)], axis=0
    )
    spectrum = jnp.einsum("rqv,qvsy->rsy", mine, along_y, precision=high)
    first_row = lax.axis_index("chan") * row_count
    u_re, u_im = taps_transform(kernel_taps[0], side)
    v_re, v_im = taps_transform(kernel_taps[1], side)
    u_re = lax.dynamic_slice_in_dim(u_re, first_row, row_count, 0)[:, None]
    u_im = lax.dynamic_slice_in_dim(u_im, first_row, row_count, 0)[:, None]
    k_re = u_re * v_re[None, :] - u_im * v_im[None, :]
    k_im = u_re * v_im[None, :] + u_im * v_re[None, :]
    s_re = spectrum[:, 0, :]
    s_im = spectrum[:, 1, :]
    channels_all = local_channels * facets * chan_count
    norm_factor = 1.0 / math.sqrt(channels_all * stations * stations * KT * KT / facets)
    image_re = (s_re * k_re - s_im * k_im) * norm_factor
    image_im = (s_re * k_im + s_im * k_re) * norm_factor
    return jnp.stack([image_re, image_im], axis=0)


def solution(mesh):
    placed = (
        P("stn", "chan", None),
        P("chan", "stn", None, None),
        P("chan", "stn", None),
        P("chan", "stn", None, None),
        P(),
    )
    return jax.shard_map(
        body, mesh=mesh, in_specs=placed, out_specs=P(None, ("stn", "chan"), None), check_vma=False
    )
```

time: 881 us -> 423 us (0.48)
  local copies, waits for them, and re-layouts: 271 us -> 35.1 us
  loops' own time: 128 us -> 0 us
  other arithmetic: 114 us -> 4.63 us
  matrix products: 111 us -> 3.65 us
  waiting for transfers between devices: 209 us -> 300 us
  Pallas kernels: 0 us -> 52.8 us
  starting transfers between devices: 26.7 us -> 12 us
    unnamed x1 -> x2, waiting for transfers between devices: 0.02 us -> 276 us
    scatter x3 -> x0, local copies, waits for them, and re-layouts: 201 us -> none  [the longest x1 186 us: body(): jnp.zeros((facets * capacity, 2, VB), jnp.bfloat16).at[slot_ids]]
    psum x1 -> x0, waiting for transfers between devices: 146 us -> none  [body(): summed = lax.psum(grid, 'chan')]
    another operation x1 -> x0, loops' own time: 128 us -> none  [grid_blocks(): lax.scan(accumulate, start_grids, jnp.arange(slot_count // group_size))]
    dot_general x32 -> x2, matrix products: 110 us -> 2.91 us  [the longest x1 2.02 us: body(): rows = jnp.einsum('xqpu,fpuv->fxqv', along_x, delta, precision=high)]
    convert_element_type x38 -> x1, other arithmetic: 90.4 us -> 0.16 us  [body(): im = imag_vis.reshape(-1, VB).astype(jnp.float32)]
    pallas_call x0 -> x1, Pallas kernels: none -> 52.8 us  [grid_blocks(): pl.pallas_call(grid_kernel, out_shape=jax.ShapeDtypeStruct((segments, TIL...]
    all_to_all x3 -> x0, waiting for transfers between devices: 42.7 us -> none  [the longest x1 38.2 us: body(): lax.all_to_all(send_values, 'stn', split_axis=0, concat_axis=0, tiled=True)]
  transfers between devices with their start and end apart: 5 -> 2, of which waited for: 4 -> 2; matrix products, arithmetic and copies ran while one was open for 23% -> 1% of each run, Pallas kernels for 0% -> 0%
where the time goes in v1:
time: 423 us; the launch traced here: 422 us
  waiting for transfers between devices  300 us (71%)
  Pallas kernels  52.8 us (12%)
  local copies, waits for them, and re-layouts  35.1 us (8%)
  between operations  13.5 us (3%)
  starting transfers between devices  12 us (3%)
  other arithmetic  4.63 us (1%)
    unnamed x2, waiting for transfers between devices  276 us
    pallas_call x1, Pallas kernels, grid_blocks(): pl.pallas_call(grid_kernel, out_shape=jax.ShapeDtypeStruct((segments, TIL...  52.8 us
    all_to_all x1, waiting for transfers between devices, body(): lax.all_to_all(voltages, 'stn', split_axis=1, concat_axis=0, tiled=True)  24.3 us
    transpose x1, local copies, waits for them, and re-layouts, body(): jnp.transpose(delta, (0, 4, 1, 3, 2, 5)).reshape(facets, 2, side, side)  12.2 us
    all_to_all x1, starting transfers between devices, body(): lax.all_to_all(voltages, 'stn', split_axis=1, concat_axis=0, tiled=True)  12 us
    reshape x1, local copies, waits for them, and re-layouts, body(): delta = tiles.reshape(facets, TS, TS, TILE, 2, TILE)  9.16 us
  transfers between devices with their start and end apart: 2, of which 2 were waited for; matrix products, arithmetic and copies ran while one was open for 1% of the time, Pallas kernels for 0%

profile of v1, /device:TPU:1, one launch (start us, length us, event | category | flops | bytes accessed | tf_op | source)
XLA Modules:
  0.0 422.0 jit_solution(6164785644236662602)
XLA Ops:
  6.5 2.8 copy.21
  9.4 12.0 %all-to-all-start = ((bf16[16,64,512]{2,0,1:T(8,128)(2,1)}), bf16[16,64,512]{2,0,1:T(8,128)(2,1)S(1)}, u32[]{:S(2)}, u32[]{:S(2)}) async-start(bf16[16,64,512]{2,0,1:T(8,128)(2,1)} %copy.21), calls=%async_computation | async-start | bytes 2097152 | tf_op jit(solution)/shard_map/all_to_all | solution.py:89
  21.3 0.0 all-reduce.3.cloned.1.call-start
  21.4 0.0 copy-done.2
  21.4 0.0 copy-done.1
  21.4 0.6 add.89.seg_ref
  22.0 0.3 fusion.36
  22.3 0.3 fusion.34
  22.6 2.3 add_select_fusion
  24.9 24.3 %all-to-all-done = bf16[16,64,512]{2,0,1:T(8,128)(2,1)S(1)} async-done(((bf16[16,64,512]{2,0,1:T(8,128)(2,1)}), bf16[16,64,512]{2,0,1:T(8,128)(2,1)S(1)}, u32[]{:S(2)}, u32[]{:S(2)}) %all-to-all-start) | async-done | bytes 1048608 | tf_op jit(solution)/shard_map/all_to_all | solution.py:89
  49.3 0.1 copy.22
  49.3 0.1 fusion.51
  49.4 0.7 fusion
  50.2 0.2 fusion.17
  50.3 1.1 reshape.492.re_ref
  51.4 1.1 reshape.493.im_ref
  52.4 52.8 %shard_map.55 = f32[256,32,64]{2,1,0:T(8,128)} custom-call(s32[2048]{0:T(1024)} %add.89.seg_ref, s32[2048,128]{1,0:T(8,128)} %get-tuple-element.14.du_ref, s32[2048,128]{1,0:T(8,128)} %get-tuple-element.13.dv_ref, f32[2048,128]{1,0:T(8,128)} %reshape.492.re_ref, f32[2048,128]{1,0:T(8,128)} %reshape.493.im_ref), custom_call_target="tpu_custom_call" | custom-call | flops 1073741824 | bytes 6291456 | tf_op jit(solution)/shard_map/pallas_call | solution.py:52
  105.3 9.2 %reshape.489 = f32[16,4,4,32,2,32]{5,4,3,2,1,0:T(2,128)} reshape(f32[256,32,64]{2,1,0:T(8,128)} %shard_map.55) | data formatting | bytes 4194304 | tf_op jit(solution)/shard_map/reshape | solution.py:110
  114.4 12.2 %copy.23 = f32[16,2,4,32,4,32]{5,4,3,2,1,0:T(4,128)} copy(f32[16,2,4,32,4,32]{5,1,3,4,2,0:T(2,128)} %bitcast.78) | data formatting | bytes 4194304 | tf_op jit(solution)/shard_map/transpose | solution.py:111
  126.6 6.5 %reshape.496 = f32[16,2,128,128,1]{3,2,1,0,4:T(8,128)S(1)} reshape(f32[16,2,4,32,4,32]{5,4,3,2,1,0:T(4,128)} %copy.23) | data formatting | bytes 4194304 | tf_op jit(solution)/shard_map/reshape | solution.py:111
  133.2 2.0 fusion.8
  135.2 1.5 copy.24
  136.6 0.0 all-reduce.3.cloned.1.call-update
  136.7 0.6 copy-done.3
  137.3 0.1 multiply_reduce_fusion.3
  137.4 0.1 dynamic_slice.7
  137.5 0.1 dynamic_slice.6
  137.5 0.1 multiply_reduce_fusion.2
  137.6 275.9 %all-reduce.3.cloned.1.call-done = f32[2048,2,128]{2,0,1:T(8,128)} async-done(((f32[2048,2,128]{2,0,1:T(8,128)}), f32[2048,2,128]{2,0,1:T(8,128)}) %all-reduce.3.cloned.1.call-update) | async-done | bytes 2097168
  413.6 0.9 convolution_bitcast_fusion
  414.4 0.1 subtract_multiply_fusion
  414.6 0.6 pad_maximum_fusion.4
  (11 shorter events, 0.1 us)
Async XLA Ops:
  6.5 14.8 %copy-start.2 = (s32[1,1,2048,1]{2,3,1,0:T(1,128)S(1)}, s32[1,1,2048,1]{2,3,1,0:T(1,128)}, u32[]{:S(2)}) copy-start(s32[1,1,2048,1]{2,3,1,0:T(1,128)} %param.6) | copy-start | bytes 24580
  6.5 14.9 %copy-start.1 = (s32[1,1,2048]{2,1,0:T(1,128)S(1)}, s32[1,1,2048]{2,1,0:T(1,128)}, u32[]{:S(2)}) copy-start(s32[1,1,2048]{2,1,0:T(1,128)} %param.7) | copy-start | bytes 24580
  9.4 13.3 %copy-start = (s32[1,1,2048,128]{3,2,1,0:T(8,128)S(1)}, s32[1,1,2048,128]{3,2,1,0:T(8,128)}, u32[]{:S(2)}) copy-start(s32[1,1,2048,128]{3,2,1,0:T(8,128)} %param.8) | copy-start | bytes 3145732
  9.4 39.9 %all-to-all-start = ((bf16[16,64,512]{2,0,1:T(8,128)(2,1)}), bf16[16,64,512]{2,0,1:T(8,128)(2,1)S(1)}, u32[]{:S(2)}, u32[]{:S(2)}) async-start(bf16[16,64,512]{2,0,1:T(8,128)(2,1)} %copy.21), calls=%async_computation | async-start | bytes 2097152 | tf_op jit(solution)/shard_map/all_to_all | solution.py:89
  21.3 392.2 %all-reduce.3.cloned.1.call-start = ((), (), s32[]{:S(2)}) async-start(), calls=%async_computation.1 | async-start | bytes 4194304
  136.6 0.7 copy-start.3
Sparse Core Ops, SparseCore 0:
  136.8 276.7 all-reduce.2

commit v2 on v1

--- a/solution.py
+++ b/solution.py
@@ -108,17 +108,24 @@
     tiles = grid_blocks(seg_ids, du, dv, re, im, facets * TT)
     side = TS * TILE
     delta = tiles.reshape(facets, TS, TS, TILE, 2, TILE)
-    delta = jnp.transpose(delta, (0, 4, 1, 3, 2, 5)).reshape(facets, 2, side, side)
+    delta = delta[..., :OFFS]
+    delta = jnp.transpose(delta, (0, 4, 1, 3, 2, 5)).reshape(facets, 2, side, TS * OFFS)
     cosine, sine = dft_tables(side)
     along_x = jnp.stack(
         [jnp.stack([cosine, sine], axis=1), jnp.stack([-sine, cosine], axis=1)], axis=1
     )
     rows = jnp.einsum("xqpu,fpuv->fxqv", along_x, delta, precision=high)
-    rows = rows.reshape(facets * side, 2, side)
-    mine = lax.psum_scatter(rows, ("stn", "chan"), scatter_dimension=0, tiled=True)
-    row_count = mine.shape[0]
+    row_count = side // chan_count
+    rows = rows.reshape(facets, chan_count, row_count, 2, TS * OFFS)
+    rows = jnp.transpose(rows, (1, 0, 2, 3, 4)).reshape(chan_count * facets * row_count, 2, TS * OFFS)
+    rows = lax.psum_scatter(rows, "chan", scatter_dimension=0, tiled=True)
+    mine = lax.psum_scatter(rows, "stn", scatter_dimension=0, tiled=True)
+    used = jnp.arange(TS * OFFS, dtype=jnp.int32)
+    used = (used // OFFS) * TILE + used % OFFS
+    cos_used = cosine[used]
+    sin_used = sine[used]
     along_y = jnp.stack(
-        [jnp.stack([cosine, -sine], axis=1), jnp.stack([sine, cosine], axis=1)], axis=0
+        [jnp.stack([cos_used, -sin_used], axis=1), jnp.stack([sin_used, cos_used], axis=1)], axis=0
     )
     spectrum = jnp.einsum("rqv,qvsy->rsy", mine, along_y, precision=high)
     first_row = lax.axis_index("chan") * row_count

time: 423 us -> 421 us (level)
  waiting for transfers between devices: 300 us -> 234 us
  blocking collectives: 0 us -> 49.6 us
  local copies, waits for them, and re-layouts: 35.1 us -> 47.6 us
    unnamed x2 -> x1, waiting for transfers between devices: 276 us -> 0.02 us
    reduce_scatter x0 -> x1, waiting for transfers between devices: none -> 210 us  [body(): rows = lax.psum_scatter(rows, 'chan', scatter_dimension=0, tiled=True)]
    unnamed x0 -> x1, blocking collectives: none -> 49.6 us
    reshape x1 -> x2, local copies, waits for them, and re-layouts: 6.52 us -> 18.3 us  [body(): jnp.transpose(delta, (0, 4, 1, 3, 2, 5)).reshape(facets, 2, side, TS * OFFS)]
    transpose x1 -> x2, local copies, waits for them, and re-layouts: 12.2 us -> 10.1 us  [the longest x1 7.39 us: body(): jnp.transpose(delta, (0, 4, 1, 3, 2, 5)).reshape(facets, 2, side, TS * OFFS)]
  transfers between devices with their start and end apart: 2 -> 2, of which waited for: 2 -> 2; matrix products, arithmetic and copies ran while one was open for 1% -> 2% of each run, Pallas kernels for 0% -> 0%
where the time goes in v2:
time: 421 us; the launch traced here: 419 us
  waiting for transfers between devices  234 us (56%)
  Pallas kernels  52.6 us (12%)
  blocking collectives  49.6 us (12%)
  local copies, waits for them, and re-layouts  47.6 us (11%)
  between operations  14.2 us (3%)
  starting transfers between devices  11.9 us (3%)
  other arithmetic  5.18 us (1%)
    reduce_scatter x1, waiting for transfers between devices, body(): rows = lax.psum_scatter(rows, 'chan', scatter_dimension=0, tiled=True)  210 us
    pallas_call x1, Pallas kernels, grid_blocks(): pl.pallas_call(grid_kernel, out_shape=jax.ShapeDtypeStruct((segments, TIL...  52.6 us
    unnamed x1, blocking collectives  49.6 us
    all_to_all x1, waiting for transfers between devices, body(): lax.all_to_all(voltages, 'stn', split_axis=1, concat_axis=0, tiled=True)  24.3 us
    reshape x2, local copies, waits for them, and re-layouts, body(): jnp.transpose(delta, (0, 4, 1, 3, 2, 5)).reshape(facets, 2, side, TS * OFFS)  18.3 us
    all_to_all x1, starting transfers between devices, body(): lax.all_to_all(voltages, 'stn', split_axis=1, concat_axis=0, tiled=True)  11.8 us
    reshape x1, local copies, waits for them, and re-layouts, body(): delta = tiles.reshape(facets, TS, TS, TILE, 2, TILE)  9.14 us
  transfers between devices with their start and end apart: 2, of which 2 were waited for; matrix products, arithmetic and copies ran while one was open for 2% of the time, Pallas kernels for 0%

profile of v2, /device:TPU:1, one launch (start us, length us, event | category | flops | bytes accessed | tf_op | source)
XLA Modules:
  0.0 418.7 jit_solution(14324126553127827226)
XLA Ops:
  6.5 2.9 copy.28
  9.4 11.8 %all-to-all-start = ((bf16[16,64,512]{2,0,1:T(8,128)(2,1)}), bf16[16,64,512]{2,0,1:T(8,128)(2,1)S(1)}, u32[]{:S(2)}, u32[]{:S(2)}) async-start(bf16[16,64,512]{2,0,1:T(8,128)(2,1)} %copy.28), calls=%async_computation | async-start | bytes 2097152 | tf_op jit(solution)/shard_map/all_to_all | solution.py:89
  21.3 0.6 add.135.seg_ref
  21.9 0.3 fusion.40
  22.2 0.3 fusion.38
  22.5 2.3 add_select_fusion
  24.9 24.3 %all-to-all-done = bf16[16,64,512]{2,0,1:T(8,128)(2,1)S(1)} async-done(((bf16[16,64,512]{2,0,1:T(8,128)(2,1)}), bf16[16,64,512]{2,0,1:T(8,128)(2,1)S(1)}, u32[]{:S(2)}, u32[]{:S(2)}) %all-to-all-start) | async-done | bytes 1048608 | tf_op jit(solution)/shard_map/all_to_all | solution.py:89
  49.3 0.7 fusion
  50.1 0.2 fusion.17
  50.2 1.1 reshape.564.re_ref
  51.3 1.0 reshape.565.im_ref
  52.3 52.6 %shard_map.55 = f32[256,32,64]{2,1,0:T(8,128)} custom-call(s32[2048]{0:T(1024)} %add.135.seg_ref, s32[2048,128]{1,0:T(8,128)} %get-tuple-element.14.du_ref, s32[2048,128]{1,0:T(8,128)} %get-tuple-element.13.dv_ref, f32[2048,128]{1,0:T(8,128)} %reshape.564.re_ref, f32[2048,128]{1,0:T(8,128)} %reshape.565.im_ref), custom_call_target="tpu_custom_call" | custom-call | flops 1073741824 | bytes 6291456 | tf_op jit(solution)/shard_map/pallas_call | solution.py:52
  105.0 9.1 %reshape.560 = f32[16,4,4,32,2,32]{5,4,3,2,1,0:T(2,128)} reshape(f32[256,32,64]{2,1,0:T(8,128)} %shard_map.55) | data formatting | bytes 4194304 | tf_op jit(solution)/shard_map/reshape | solution.py:110
  114.1 7.4 %slice_bitcast_fusion = f32[16,2,4,32,4,25]{5,1,3,4,2,0:T(2,128)} fusion(f32[16,4,4,32,2,32]{5,4,3,2,1,0:T(2,128)} %reshape.560), kind=kLoop, calls=%fused_computation.2 | loop fusion | bytes 3276800 | tf_op jit(solution)/shard_map/transpose | solution.py:112
  121.5 13.2 %copy.38 = f32[16,2,4,32,4,25]{3,2,5,4,1,0:T(4,128)} copy(f32[16,2,4,32,4,25]{5,1,3,4,2,0:T(2,128)} %slice_bitcast_fusion) | data formatting | bytes 3276800 | tf_op jit(solution)/shard_map/reshape | solution.py:112
  134.7 5.1 %reshape.584 = f32[16,2,128,100,1]{2,3,1,0,4:T(8,128)S(1)} reshape(f32[16,2,4,32,4,25]{3,2,5,4,1,0:T(4,128)} %copy.38) | data formatting | bytes 3276800 | tf_op jit(solution)/shard_map/reshape | solution.py:112
  139.8 2.7 fusion.8
  142.6 2.4 copy.32
  144.9 2.7 copy.33
  147.7 0.3 fusion.36
  148.0 0.6 gather_fusion.1
  148.6 0.3 fusion.37
  148.8 0.6 gather_fusion
  149.5 0.1 multiply_reduce_fusion.3
  149.6 0.1 dynamic_slice.7
  149.7 0.1 multiply_reduce_fusion.2
  149.8 1.3 dynamic-slice
  151.8 209.5 %reduce-scatter.3.cloned.1.call-done = f32[64,2,100]{2,0,1:T(8,128)} async-done(((f32[2048,2,100]{2,0,1:T(8,128)}), f32[64,2,100]{2,0,1:T(8,128)}) %reduce-scatter.3.cloned.1.call-update) | async-done | bytes 51216 | tf_op jit(solution)/shard_map/reduce_scatter | solution.py:121
  361.3 49.6 %all-reduce = f32[64,2,100]{2,0,1:T(8,128)S(1)} all-reduce(f32[64,2,100]{2,0,1:T(8,128)} %reduce-scatter.3.cloned.1.call-done), channel_id=3, replica_groups=mesh['stn'=16,'chan'=32] {'stn'}, use_global_device_ids=true, to_apply=%region_1.2.clone | all-reduce | flops 12800 | bytes 102400
  410.9 0.2 convolution_bitcast_fusion
  411.1 0.1 subtract_multiply_fusion
  411.2 0.6 pad_maximum_fusion
  (23 shorter events, 0.4 us)
Async XLA Ops:
  6.5 14.8 %copy-start.2 = (s32[1,1,2048,1]{2,3,1,0:T(1,128)S(1)}, s32[1,1,2048,1]{2,3,1,0:T(1,128)}, u32[]{:S(2)}) copy-start(s32[1,1,2048,1]{2,3,1,0:T(1,128)} %param.6) | copy-start | bytes 24580
  6.5 14.8 %copy-start.1 = (s32[1,1,2048]{2,1,0:T(1,128)S(1)}, s32[1,1,2048]{2,1,0:T(1,128)}, u32[]{:S(2)}) copy-start(s32[1,1,2048]{2,1,0:T(1,128)} %param.7) | copy-start | bytes 24580
  6.5 16.0 %copy-start = (s32[1,1,2048,128]{3,2,1,0:T(8,128)S(1)}, s32[1,1,2048,128]{3,2,1,0:T(8,128)}, u32[]{:S(2)}) copy-start(s32[1,1,2048,128]{3,2,1,0:T(8,128)} %param.8) | copy-start | bytes 3145732
  9.4 39.8 %all-to-all-start = ((bf16[16,64,512]{2,0,1:T(8,128)(2,1)}), bf16[16,64,512]{2,0,1:T(8,128)(2,1)S(1)}, u32[]{:S(2)}, u32[]{:S(2)}) async-start(bf16[16,64,512]{2,0,1:T(8,128)(2,1)} %copy.28), calls=%async_computation | async-start | bytes 2097152 | tf_op jit(solution)/shard_map/all_to_all | solution.py:89
  21.3 340.0 %reduce-scatter.3.cloned.1.call-start = ((), (), s32[]{:S(2)}) async-start(), calls=%async_computation.2 | async-start | bytes 2162688 | tf_op jit(solution)/shard_map/reduce_scatter | solution.py:121
  147.6 1.8 copy-start.3
Sparse Core Ops, SparseCore 0:
  147.8 213.4 reduce-scatter.2

commit v3 on v2

--- a/solution.py
+++ b/solution.py
@@ -118,8 +118,10 @@
     row_count = side // chan_count
     rows = rows.reshape(facets, chan_count, row_count, 2, TS * OFFS)
     rows = jnp.transpose(rows, (1, 0, 2, 3, 4)).reshape(chan_count * facets * row_count, 2, TS * OFFS)
-    rows = lax.psum_scatter(rows, "chan", scatter_dimension=0, tiled=True)
-    mine = lax.psum_scatter(rows, "stn", scatter_dimension=0, tiled=True)
+    rows = lax.all_to_all(rows, "chan", split_axis=0, concat_axis=0, tiled=True)
+    rows = jnp.sum(rows.reshape(chan_count, facets * row_count, 2, TS * OFFS), axis=0)
+    rows = lax.all_to_all(rows, "stn", split_axis=0, concat_axis=0, tiled=True)
+    mine = jnp.sum(rows.reshape(facets, row_count, 2, TS * OFFS), axis=0)
     used = jnp.arange(TS * OFFS, dtype=jnp.int32)
     used = (used // OFFS) * TILE + used % OFFS
     cos_used = cosine[used]

time: 421 us -> 224 us (0.53)
  waiting for transfers between devices: 234 us -> 80.7 us
  blocking collectives: 49.6 us -> 0 us
  between operations: 14.2 us -> 0.17 us
  starting transfers between devices: 11.9 us -> 25.2 us
  local copies, waits for them, and re-layouts: 47.6 us -> 53.8 us
    reduce_scatter x1 -> x0, waiting for transfers between devices: 210 us -> none  [body(): rows = lax.psum_scatter(rows, 'chan', scatter_dimension=0, tiled=True)]
    all_to_all x0 -> x2, waiting for transfers between devices: none -> 56.3 us  [the longest x1 48.5 us: body(): rows = lax.all_to_all(rows, 'chan', split_axis=0, concat_axis=0, tiled=True)]
    unnamed x1 -> x0, blocking collectives: 49.6 us -> none
    all_to_all x0 -> x2, starting transfers between devices: none -> 13.4 us  [the longest x1 9.81 us: body(): rows = lax.all_to_all(rows, 'chan', split_axis=0, concat_axis=0, tiled=True)]
    reshape x0 -> x1, local copies, waits for them, and re-layouts: none -> 8.78 us  [body(): jnp.transpose(rows, (1, 0, 2, 3, 4))]
  transfers between devices with their start and end apart: 2 -> 3, of which waited for: 2 -> 3; matrix products, arithmetic and copies ran while one was open for 2% -> 3% of each run, Pallas kernels for 0% -> 0%
where the time goes in v3:
time: 224 us; the launch traced here: 223 us
  waiting for transfers between devices  80.7 us (36%)
  local copies, waits for them, and re-layouts  53.8 us (24%)
  Pallas kernels  52.6 us (23%)
  starting transfers between devices  25.2 us (11%)
  other arithmetic  6.87 us (3%)
  matrix products  3.64 us (2%)
    pallas_call x1, Pallas kernels, grid_blocks(): pl.pallas_call(grid_kernel, out_shape=jax.ShapeDtypeStruct((segments, TIL...  52.6 us
    all_to_all x1, waiting for transfers between devices, body(): rows = lax.all_to_all(rows, 'chan', split_axis=0, concat_axis=0, tiled=True)  48.5 us
    all_to_all x1, waiting for transfers between devices, body(): lax.all_to_all(voltages, 'stn', split_axis=1, concat_axis=0, tiled=True)  24.4 us
    reshape x2, local copies, waits for them, and re-layouts, body(): jnp.transpose(delta, (0, 4, 1, 3, 2, 5)).reshape(facets, 2, side, TS * OFFS)  18.3 us
    all_to_all x1, starting transfers between devices, body(): lax.all_to_all(voltages, 'stn', split_axis=1, concat_axis=0, tiled=True)  11.8 us
    all_to_all x1, starting transfers between devices, body(): rows = lax.all_to_all(rows, 'chan', split_axis=0, concat_axis=0, tiled=True)  9.81 us
    reshape x1, local copies, waits for them, and re-layouts, body(): delta = tiles.reshape(facets, TS, TS, TILE, 2, TILE)  9.15 us
    reshape x1, local copies, waits for them, and re-layouts, body(): jnp.transpose(rows, (1, 0, 2, 3, 4))  8.78 us
  transfers between devices with their start and end apart: 3, of which 3 were waited for; matrix products, arithmetic and copies ran while one was open for 3% of the time, Pallas kernels for 0%

profile of v3, /device:TPU:1, one launch (start us, length us, event | category | flops | bytes accessed | tf_op | source)
XLA Modules:
  0.0 223.0 jit_solution(6080201266339694279)
XLA Ops:
  0.0 2.9 %copy.45 = bf16[16,64,512]{2,0,1:T(8,128)(2,1)} copy(bf16[16,64,512]{2,1,0:T(8,128)(2,1)} %param.5) | data formatting | bytes 2097152 | tf_op args[0]
  2.9 11.8 %all-to-all-start = ((bf16[16,64,512]{2,0,1:T(8,128)(2,1)}), bf16[16,64,512]{2,0,1:T(8,128)(2,1)S(1)}, u32[]{:S(2)}, u32[]{:S(2)}) async-start(bf16[16,64,512]{2,0,1:T(8,128)(2,1)} %copy.45), calls=%async_computation | async-start | bytes 2097152 | tf_op jit(solution)/shard_map/all_to_all | solution.py:89
  14.8 0.6 add.131.seg_ref
  15.4 0.3 fusion.40
  15.6 0.3 fusion.38
  16.0 2.3 %add_select_fusion = (s32[2048,128]{1,0:T(8,128)}, s32[2048,128]{1,0:T(8,128)}) fusion(s32[1,1,2048,128]{3,2,1,0:T(8,128)S(1)} %copy-done), kind=kLoop, calls=%fused_computation.11 | loop fusion | flops 3145728 | bytes 3145728 | tf_op jit(solution)/shard_map/jit(remainder)/select_n | solution.py:106
  18.3 24.4 %all-to-all-done = bf16[16,64,512]{2,0,1:T(8,128)(2,1)S(1)} async-done(((bf16[16,64,512]{2,0,1:T(8,128)(2,1)}), bf16[16,64,512]{2,0,1:T(8,128)(2,1)S(1)}, u32[]{:S(2)}, u32[]{:S(2)}) %all-to-all-start) | async-done | bytes 1048608 | tf_op jit(solution)/shard_map/all_to_all | solution.py:89
  42.8 0.7 fusion
  43.6 0.2 fusion.17
  43.7 1.1 reshape.572.re_ref
  44.8 1.0 reshape.573.im_ref
  45.8 52.6 %shard_map.55 = f32[256,32,64]{2,1,0:T(8,128)} custom-call(s32[2048]{0:T(1024)} %add.131.seg_ref, s32[2048,128]{1,0:T(8,128)} %get-tuple-element.14.du_ref, s32[2048,128]{1,0:T(8,128)} %get-tuple-element.13.dv_ref, f32[2048,128]{1,0:T(8,128)} %reshape.572.re_ref, f32[2048,128]{1,0:T(8,128)} %reshape.573.im_ref), custom_call_target="tpu_custom_call" | custom-call | flops 1073741824 | bytes 6291456 | tf_op jit(solution)/shard_map/pallas_call | solution.py:52
  98.5 9.2 %reshape.566 = f32[16,4,4,32,2,32]{5,4,3,2,1,0:T(2,128)} reshape(f32[256,32,64]{2,1,0:T(8,128)} %shard_map.55) | data formatting | bytes 4194304 | tf_op jit(solution)/shard_map/reshape | solution.py:110
  107.6 7.4 %slice_bitcast_fusion = f32[16,2,4,32,4,25]{5,1,3,4,2,0:T(2,128)} fusion(f32[16,4,4,32,2,32]{5,4,3,2,1,0:T(2,128)} %reshape.566), kind=kLoop, calls=%fused_computation.2 | loop fusion | bytes 3276800 | tf_op jit(solution)/shard_map/transpose | solution.py:112
  115.0 13.2 %copy.59 = f32[16,2,4,32,4,25]{3,2,5,4,1,0:T(4,128)} copy(f32[16,2,4,32,4,25]{5,1,3,4,2,0:T(2,128)} %slice_bitcast_fusion) | data formatting | bytes 3276800 | tf_op jit(solution)/shard_map/reshape | solution.py:112
  128.2 5.1 %reshape.592 = f32[16,2,128,100,1]{2,3,1,0,4:T(8,128)S(1)} reshape(f32[16,2,4,32,4,25]{3,2,5,4,1,0:T(4,128)} %copy.59) | data formatting | bytes 3276800 | tf_op jit(solution)/shard_map/reshape | solution.py:112
  133.3 2.7 %fusion.8 = f32[16,128,2,100]{1,3,2,0:T(8,128)} fusion(f32[16,2,128,100,1]{2,3,1,0,4:T(8,128)S(1)} %reshape.592, f32[128,1,2,128]{3,0,2,1:T(8,128)S(1)} %get-tuple-element.16, f32[128,1,2,128]{3,0,2,1:T(8,128)S(1)} %get-tuple-element.15), kind=kOutput, calls=%fused_computation.13 | convolution fusion | flops 1258356736 | bytes 3538944 | tf_op jit(solution)/shard_map/xqpu,fpuv->fxqv/dot_general | solution.py:117
  136.1 2.4 %copy.49 = f32[16,128,2,100]{3,0,2,1:T(8,128)S(1)} copy(f32[16,128,2,100]{1,3,2,0:T(8,128)} %fusion.8) | data formatting | bytes 3276800 | tf_op jit(solution)/shard_map/xqpu,fpuv->fxqv/transpose | solution.py:117
  138.4 1.4 copy.50
  139.8 8.8 %copy.51 = f32[2048,2,100]{2,1,0:T(2,128)} copy(f32[2048,2,100]{2,0,1:T(8,128)S(1)} %bitcast.91) | data formatting | bytes 3276800 | tf_op jit(solution)/shard_map/reshape | solution.py:120
  148.6 9.8 %all-to-all-start.1 = ((f32[2048,2,100]{2,1,0:T(2,128)}), f32[2048,2,100]{2,1,0:T(2,128)S(1)}, u32[]{:S(2)}, u32[]{:S(2)}) async-start(f32[2048,2,100]{2,1,0:T(2,128)} %copy.51), calls=%async_computation.1 | async-start | bytes 4194304 | tf_op jit(solution)/shard_map/all_to_all | solution.py:121
  158.4 0.3 fusion.36
  158.7 0.6 gather_fusion.1
  159.3 0.3 fusion.37
  159.6 0.6 gather_fusion
  160.6 48.5 %all-to-all-done.1 = f32[2048,2,100]{2,1,0:T(2,128)S(1)} async-done(((f32[2048,2,100]{2,1,0:T(2,128)}), f32[2048,2,100]{2,1,0:T(2,128)S(1)}, u32[]{:S(2)}, u32[]{:S(2)}) %all-to-all-start.1) | async-done | bytes 1638432 | tf_op jit(solution)/shard_map/all_to_all | solution.py:121
  209.1 1.6 reduce_sum.54
  210.7 3.6 %all-to-all-start.2 = ((f32[64,2,100]{2,1,0:T(2,128)}), f32[64,2,100]{2,1,0:T(2,128)S(1)}, u32[]{:S(2)}, u32[]{:S(2)}) async-start(f32[64,2,100]{2,1,0:T(2,128)} %reduce_sum.54), calls=%async_computation.2 | async-start | bytes 131072 | tf_op jit(solution)/shard_map/all_to_all | solution.py:123
  214.3 7.8 %all-to-all-done.2 = f32[64,2,100]{2,1,0:T(2,128)S(1)} async-done(((f32[64,2,100]{2,1,0:T(2,128)}), f32[64,2,100]{2,1,0:T(2,128)S(1)}, u32[]{:S(2)}, u32[]{:S(2)}) %all-to-all-start.2) | async-done | bytes 51232 | tf_op jit(solution)/shard_map/all_to_all | solution.py:123
  222.2 0.2 convolution_bitcast_fusion
  222.3 0.1 subtract_multiply_fusion
  222.4 0.6 pad_maximum_fusion
  (25 shorter events, 0.6 us)
Async XLA Ops:
  0.0 14.7 %copy-start.2 = (s32[1,1,2048,1]{2,3,1,0:T(1,128)S(1)}, s32[1,1,2048,1]{2,3,1,0:T(1,128)}, u32[]{:S(2)}) copy-start(s32[1,1,2048,1]{2,3,1,0:T(1,128)} %param.6) | copy-start | bytes 24580
  0.0 14.8 %copy-start.1 = (s32[1,1,2048]{2,1,0:T(1,128)S(1)}, s32[1,1,2048]{2,1,0:T(1,128)}, u32[]{:S(2)}) copy-start(s32[1,1,2048]{2,1,0:T(1,128)} %param.7) | copy-start | bytes 24580
  0.0 16.0 %copy-start = (s32[1,1,2048,128]{3,2,1,0:T(8,128)S(1)}, s32[1,1,2048,128]{3,2,1,0:T(8,128)}, u32[]{:S(2)}) copy-start(s32[1,1,2048,128]{3,2,1,0:T(8,128)} %param.8) | copy-start | bytes 3145732
  2.9 39.8 %all-to-all-start = ((bf16[16,64,512]{2,0,1:T(8,128)(2,1)}), bf16[16,64,512]{2,0,1:T(8,128)(2,1)S(1)}, u32[]{:S(2)}, u32[]{:S(2)}) async-start(bf16[16,64,512]{2,0,1:T(8,128)(2,1)} %copy.45), calls=%async_computation | async-start | bytes 2097152 | tf_op jit(solution)/shard_map/all_to_all | solution.py:89
  148.6 11.6 %copy-start.3 = (bf16[2,8]{1,0:T(2,128)(2,1)S(1)}, bf16[2,8]{1,0:T(2,128)(2,1)}, u32[]{:S(2)}) copy-start(bf16[2,8]{1,0:T(2,128)(2,1)} %param.9) | copy-start | bytes 100
  148.6 60.5 %all-to-all-start.1 = ((f32[2048,2,100]{2,1,0:T(2,128)}), f32[2048,2,100]{2,1,0:T(2,128)S(1)}, u32[]{:S(2)}, u32[]{:S(2)}) async-start(f32[2048,2,100]{2,1,0:T(2,128)} %copy.51), calls=%async_computation.1 | async-start | bytes 4194304 | tf_op jit(solution)/shard_map/all_to_all | solution.py:121
  210.7 11.4 %all-to-all-start.2 = ((f32[64,2,100]{2,1,0:T(2,128)}), f32[64,2,100]{2,1,0:T(2,128)S(1)}, u32[]{:S(2)}, u32[]{:S(2)}) async-start(f32[64,2,100]{2,1,0:T(2,128)} %reduce_sum.54), calls=%async_computation.2 | async-start | bytes 131072 | tf_op jit(solution)/shard_map/all_to_all | solution.py:123

commit v4 on v1

--- a/solution.py
+++ b/solution.py
@@ -19,48 +19,52 @@
 
 def grid_kernel(seg_ref, du_ref, dv_ref, re_ref, im_ref, out_ref):
     step = pl.program_id(0)
+    side = TS * TILE
 
     @pl.when(step == 0)
     def _():
         out_ref[...] = jnp.zeros_like(out_ref)
-
     cells = lax.broadcasted_iota(jnp.int32, (TILE, VB), 0)
-
+    lines = lax.broadcasted_iota(jnp.int32, (side, VB), 0)
     def one_block(b, carry):
         du = du_ref[pl.ds(b, 1), :]
         dv = dv_ref[pl.ds(b, 1), :]
         re = re_ref[pl.ds(b, 1), :]
         im = im_ref[pl.ds(b, 1), :]
+        seg = seg_ref[step * CHUNK + b]
+        facet = seg // TT
+        tile = seg % TT
+        first_u = pl.multiple_of((tile // TS) * TILE, TILE)
+        first_v = (tile % TS) * TILE
         along_u = (cells == du).astype(jnp.float32).astype(jnp.bfloat16)
-        hit_v = cells == dv
-        weighted = jnp.concatenate(
+        hit_v = lines == (dv + first_v)
+        spread = jnp.concatenate(
             [jnp.where(hit_v, re, 0.0), jnp.where(hit_v, im, 0.0)], axis=0
         ).astype(jnp.bfloat16)
         tile_sum = lax.dot_general(
-            along_u, weighted, (((1,), (1,)), ((), ())), preferred_element_type=jnp.float32
+            along_u, spread, (((1,), (1,)), ((), ())), preferred_element_type=jnp.float32
         )
-        seg = seg_ref[step * CHUNK + b]
-        out_ref[seg] += tile_sum
+        out_ref[facet, pl.ds(first_u, TILE), :] += tile_sum
         return carry
-
     lax.fori_loop(0, CHUNK, one_block, 0, unroll=8)
 
 
-def grid_blocks(seg_ids, du, dv, re, im, segments):
+def grid_blocks(seg_ids, du, dv, re, im, facets):
     blocks = du.shape[0]
+    side = TS * TILE
     row_spec = pl.BlockSpec((CHUNK, VB), lambda i, seg: (i, 0))
     return pl.pallas_call(
         grid_kernel,
-        out_shape=jax.ShapeDtypeStruct((segments, TILE, 2 * TILE), jnp.float32),
+        out_shape=jax.ShapeDtypeStruct((facets, side, 2 * side), jnp.float32),
         grid_spec=pltpu.PrefetchScalarGridSpec(
             num_scalar_prefetch=1,
             grid=(blocks // CHUNK,),
             in_specs=[row_spec] * 4,
-            out_specs=pl.BlockSpec((segments, TILE, 2 * TILE), lambda i, seg: (0, 0, 0)),
+            out_specs=pl.BlockSpec((facets, side, 2 * side), lambda i, seg: (0, 0, 0)),
         ),
         cost_estimate=pl.CostEstimate(
-            flops=blocks * TILE * VB * 2 * TILE * 2,
-            bytes_accessed=blocks * VB * 16 + segments * TILE * 2 * TILE * 4,
+            flops=blocks * TILE * VB * 2 * side * 2,
+            bytes_accessed=blocks * VB * 16 + facets * side * 2 * side * 4,
             transcendentals=0,
         ),
     )(seg_ids, du, dv, re, im)
@@ -105,18 +109,20 @@
     du = offsets // OFFS
     dv = offsets % OFFS
     seg_ids = block_facet.reshape(block_count) * TT + block_tile.reshape(block_count)
-    tiles = grid_blocks(seg_ids, du, dv, re, im, facets * TT)
+    delta = grid_blocks(seg_ids, du, dv, re, im, facets)
     side = TS * TILE
-    delta = tiles.reshape(facets, TS, TS, TILE, 2, TILE)
-    delta = jnp.transpose(delta, (0, 4, 1, 3, 2, 5)).reshape(facets, 2, side, side)
+    row_count = side // chan_count
     cosine, sine = dft_tables(side)
     along_x = jnp.stack(
-        [jnp.stack([cosine, sine], axis=1), jnp.stack([-sine, cosine], axis=1)], axis=1
-    )
-    rows = jnp.einsum("xqpu,fpuv->fxqv", along_x, delta, precision=high)
-    rows = rows.reshape(facets * side, 2, side)
-    mine = lax.psum_scatter(rows, ("stn", "chan"), scatter_dimension=0, tiled=True)
-    row_count = mine.shape[0]
+        [jnp.stack([cosine, sine], axis=2), jnp.stack([-sine, cosine], axis=2)], axis=1
+    ).reshape(2 * side, 2 * side)
+    rows = jnp.einsum("kc,fcv->kfv", along_x, delta.reshape(facets, 2 * side, side), precision=high)
+    rows = rows.reshape(chan_count * row_count * 2 * facets, side)
+    rows = lax.all_to_all(rows, "chan", split_axis=0, concat_axis=0, tiled=True)
+    rows = jnp.sum(rows.reshape(chan_count, row_count * 2, facets, side), axis=0)
+    rows = jnp.transpose(rows, (1, 0, 2)).reshape(facets * row_count * 2, side)
+    rows = lax.all_to_all(rows, "stn", split_axis=0, concat_axis=0, tiled=True)
+    mine = jnp.sum(rows.reshape(facets, row_count, 2, side), axis=0)
     along_y = jnp.stack(
         [jnp.stack([cosine, -sine], axis=1), jnp.stack([sine, cosine], axis=1)], axis=0
     )

time: 423 us -> 206 us (0.49)
  waiting for transfers between devices: 300 us -> 60.6 us
  Pallas kernels: 52.8 us -> 79 us
  starting transfers between devices: 12 us -> 25.9 us
  between operations: 13.5 us -> 0.16 us
    unnamed x2 -> x0, waiting for transfers between devices: 276 us -> none
    all_to_all x0 -> x2, waiting for transfers between devices: none -> 57.6 us  [the longest x1 50.1 us: body(): rows = lax.all_to_all(rows, 'chan', split_axis=0, concat_axis=0, tiled=True)]
    pallas_call x1, Pallas kernels: 52.8 us -> 79 us  [grid_blocks(): pl.pallas_call(grid_kernel, out_shape=jax.ShapeDtypeStruct((facets, side,...]
    all_to_all x1, waiting for transfers between devices: 24.3 us -> 3.02 us  [body(): lax.all_to_all(voltages, 'stn', split_axis=1, concat_axis=0, tiled=True)]
    all_to_all x0 -> x2, starting transfers between devices: none -> 14.1 us  [the longest x1 9.8 us: body(): rows = lax.all_to_all(rows, 'chan', split_axis=0, concat_axis=0, tiled=True)]
    transpose x2 -> x1, local copies, waits for them, and re-layouts: 13.7 us -> 0.64 us  [body(): rows = jnp.transpose(rows, (1, 0, 2)).reshape(facets * row_count * 2, side)]
    another operation x0 -> x1, local copies, waits for them, and re-layouts: none -> 8.56 us  [body(): jnp.stack([jnp.stack([cosine, sine], axis=2), jnp.stack([-sine, cosine],...]
  transfers between devices with their start and end apart: 2 -> 3, of which waited for: 2 -> 3; matrix products, arithmetic and copies ran while one was open for 1% -> 13% of each run, Pallas kernels for 0% -> 0%
where the time goes in v4:
time: 206 us; the launch traced here: 205 us
  Pallas kernels  79 us (38%)
  waiting for transfers between devices  60.6 us (29%)
  local copies, waits for them, and re-layouts  31.3 us (15%)
  starting transfers between devices  25.9 us (13%)
  other arithmetic  5.3 us (3%)
  matrix products  2.85 us (1%)
    pallas_call x1, Pallas kernels, grid_blocks(): pl.pallas_call(grid_kernel, out_shape=jax.ShapeDtypeStruct((facets, side,...  79 us
    all_to_all x1, waiting for transfers between devices, body(): rows = lax.all_to_all(rows, 'chan', split_axis=0, concat_axis=0, tiled=True)  50.1 us
    reshape x1, local copies, waits for them, and re-layouts, body(): along_x = jnp.stack([jnp.stack([cosine, sine], axis=2), jnp.stack([-sine,...  12.8 us
    all_to_all x1, starting transfers between devices, body(): lax.all_to_all(voltages, 'stn', split_axis=1, concat_axis=0, tiled=True)  11.8 us
    all_to_all x1, starting transfers between devices, body(): rows = lax.all_to_all(rows, 'chan', split_axis=0, concat_axis=0, tiled=True)  9.8 us
    another operation x1, local copies, waits for them, and re-layouts, body(): jnp.stack([jnp.stack([cosine, sine], axis=2), jnp.stack([-sine, cosine],...  8.56 us
    all_to_all x1, waiting for transfers between devices, body(): rows = lax.all_to_all(rows, 'stn', split_axis=0, concat_axis=0, tiled=True)  7.54 us
    all_to_all x1, starting transfers between devices, body(): rows = lax.all_to_all(rows, 'stn', split_axis=0, concat_axis=0, tiled=True)  4.26 us
  transfers between devices with their start and end apart: 3, of which 3 were waited for; matrix products, arithmetic and copies ran while one was open for 13% of the time, Pallas kernels for 0%

profile of v4, /device:TPU:1, one launch (start us, length us, event | category | flops | bytes accessed | tf_op | source)
XLA Modules:
  0.0 205.1 jit_solution(14631733117801012475)
XLA Ops:
  0.0 2.8 %copy.28 = bf16[16,64,512]{2,0,1:T(8,128)(2,1)} copy(bf16[16,64,512]{2,1,0:T(8,128)(2,1)} %param.5) | data formatting | bytes 2097152 | tf_op args[0]
  2.8 11.8 %all-to-all-start = ((bf16[16,64,512]{2,0,1:T(8,128)(2,1)}), bf16[16,64,512]{2,0,1:T(8,128)(2,1)S(1)}, u32[]{:S(2)}, u32[]{:S(2)}) async-start(bf16[16,64,512]{2,0,1:T(8,128)(2,1)} %copy.28), calls=%async_computation | async-start | bytes 2097152 | tf_op jit(solution)/shard_map/all_to_all | solution.py:93
  14.6 0.3 fusion.33
  14.9 0.3 fusion.31
  15.2 8.6 %copy.27 = f32[128,2,128,2]{3,2,1,0:T(8,128)} copy(f32[128,2,128,2]{2,0,3,1:T(8,128)S(1)} %pad_maximum_fusion) | data formatting | bytes 524288 | tf_op jit(solution)/shard_map/stack | solution.py:116
  23.8 12.8 %reshape.584 = f32[256,256,1]{1,0,2:T(8,128)S(1)} reshape(f32[128,2,128,2]{3,2,1,0:T(8,128)} %copy.27) | data formatting | bytes 524288 | tf_op jit(solution)/shard_map/reshape | solution.py:118
  36.6 0.6 add.103.seg_ref
  37.2 2.3 %add_select_fusion = (s32[2048,128]{1,0:T(8,128)}, s32[2048,128]{1,0:T(8,128)}) fusion(s32[1,1,2048,128]{3,2,1,0:T(8,128)S(1)} %copy-done), kind=kLoop, calls=%fused_computation.6 | loop fusion | flops 3145728 | bytes 3145728 | tf_op jit(solution)/shard_map/jit(remainder)/select_n | solution.py:110
  39.5 3.0 %all-to-all-done = bf16[16,64,512]{2,0,1:T(8,128)(2,1)S(1)} async-done(((bf16[16,64,512]{2,0,1:T(8,128)(2,1)}), bf16[16,64,512]{2,0,1:T(8,128)(2,1)S(1)}, u32[]{:S(2)}, u32[]{:S(2)}) %all-to-all-start) | async-done | bytes 1048608 | tf_op jit(solution)/shard_map/all_to_all | solution.py:93
  42.7 0.7 fusion
  43.4 0.2 fusion.12
  43.6 1.0 reshape.580.re_ref
  44.6 1.1 reshape.581.im_ref
  45.7 79.0 %shard_map.55 = f32[16,128,256]{2,1,0:T(8,128)} custom-call(s32[2048]{0:T(1024)} %add.103.seg_ref, s32[2048,128]{1,0:T(8,128)} %get-tuple-element.14.du_ref, s32[2048,128]{1,0:T(8,128)} %get-tuple-element.13.dv_ref, f32[2048,128]{1,0:T(8,128)} %reshape.580.re_ref, f32[2048,128]{1,0:T(8,128)} %reshape.581.im_ref), custom_call_target="tpu_custom_call" | custom-call | flops 4294967296 | bytes 6291456 | tf_op jit(solution)/shard_map/pallas_call | solution.py:56
  124.7 1.6 reshape.579
  126.3 1.9 fusion.48
  128.3 2.5 %copy.30 = f32[256,16,128]{2,1,0:T(8,128)} copy(f32[256,16,128]{2,0,1:T(8,128)S(1)} %fusion.48) | data formatting | bytes 4194304 | tf_op jit(solution)/shard_map/kc,fcv->kfv/dot_general | solution.py:119
  130.8 9.8 %all-to-all-start.1 = ((f32[32,128,128]{2,1,0:T(8,128)}), f32[32,128,128]{2,1,0:T(8,128)S(1)}, u32[]{:S(2)}, u32[]{:S(2)}) async-start(f32[32,128,128]{2,1,0:T(8,128)} %bitcast.70), calls=%async_computation.1 | async-start | bytes 4194304 | tf_op jit(solution)/shard_map/all_to_all | solution.py:121
  140.7 0.1 multiply_reduce_fusion.2
  140.7 0.3 fusion.34
  141.0 0.3 fusion.29
  141.3 50.1 %all-to-all-done.1 = f32[32,128,128]{2,1,0:T(8,128)S(1)} async-done(((f32[32,128,128]{2,1,0:T(8,128)}), f32[32,128,128]{2,1,0:T(8,128)S(1)}, u32[]{:S(2)}, u32[]{:S(2)}) %all-to-all-start.1) | async-done | bytes 2097184 | tf_op jit(solution)/shard_map/all_to_all | solution.py:121
  191.3 0.1 reduce_sum.58
  191.5 0.6 copy.31
  192.1 4.3 %all-to-all-start.2 = ((f32[16,8,128]{2,1,0:T(8,128)}), f32[16,8,128]{2,1,0:T(8,128)S(1)}, u32[]{:S(2)}, u32[]{:S(2)}) async-start(f32[16,8,128]{2,1,0:T(8,128)} %copy.31), calls=%async_computation.2 | async-start | bytes 131072 | tf_op jit(solution)/shard_map/all_to_all | solution.py:124
  196.4 0.1 multiply_reduce_fusion.3
  196.5 0.1 dynamic_slice.7
  196.5 0.1 dynamic_slice.6
  196.6 7.5 %all-to-all-done.2 = f32[16,8,128]{2,1,0:T(8,128)S(1)} async-done(((f32[16,8,128]{2,1,0:T(8,128)}), f32[16,8,128]{2,1,0:T(8,128)S(1)}, u32[]{:S(2)}, u32[]{:S(2)}) %all-to-all-start.2) | async-done | bytes 65568 | tf_op jit(solution)/shard_map/all_to_all | solution.py:124
  204.2 0.2 convolution_bitcast_fusion
  204.4 0.1 subtract_multiply_fusion
  204.5 0.6 pad_maximum_fusion.1
  (19 shorter events, 0.3 us)
Async XLA Ops:
  2.8 39.8 %all-to-all-start = ((bf16[16,64,512]{2,0,1:T(8,128)(2,1)}), bf16[16,64,512]{2,0,1:T(8,128)(2,1)S(1)}, u32[]{:S(2)}, u32[]{:S(2)}) async-start(bf16[16,64,512]{2,0,1:T(8,128)(2,1)} %copy.28), calls=%async_computation | async-start | bytes 2097152 | tf_op jit(solution)/shard_map/all_to_all | solution.py:93
  23.8 12.8 %copy-start.2 = (s32[1,1,2048,1]{2,3,1,0:T(1,128)S(1)}, s32[1,1,2048,1]{2,3,1,0:T(1,128)}, u32[]{:S(2)}) copy-start(s32[1,1,2048,1]{2,3,1,0:T(1,128)} %param.6) | copy-start | bytes 24580
  23.8 12.8 %copy-start.1 = (s32[1,1,2048]{2,1,0:T(1,128)S(1)}, s32[1,1,2048]{2,1,0:T(1,128)}, u32[]{:S(2)}) copy-start(s32[1,1,2048]{2,1,0:T(1,128)} %param.7) | copy-start | bytes 24580
  23.8 13.4 %copy-start = (s32[1,1,2048,128]{3,2,1,0:T(8,128)S(1)}, s32[1,1,2048,128]{3,2,1,0:T(8,128)}, u32[]{:S(2)}) copy-start(s32[1,1,2048,128]{3,2,1,0:T(8,128)} %param.8) | copy-start | bytes 3145732
  130.8 9.8 %copy-start.3 = (bf16[2,8]{1,0:T(2,128)(2,1)S(1)}, bf16[2,8]{1,0:T(2,128)(2,1)}, u32[]{:S(2)}) copy-start(bf16[2,8]{1,0:T(2,128)(2,1)} %param.9) | copy-start | bytes 100
  130.8 60.5 %all-to-all-start.1 = ((f32[32,128,128]{2,1,0:T(8,128)}), f32[32,128,128]{2,1,0:T(8,128)S(1)}, u32[]{:S(2)}, u32[]{:S(2)}) async-start(f32[32,128,128]{2,1,0:T(8,128)} %bitcast.70), calls=%async_computation.1 | async-start | bytes 4194304 | tf_op jit(solution)/shard_map/all_to_all | solution.py:121
  192.1 12.1 %all-to-all-start.2 = ((f32[16,8,128]{2,1,0:T(8,128)}), f32[16,8,128]{2,1,0:T(8,128)S(1)}, u32[]{:S(2)}, u32[]{:S(2)}) async-start(f32[16,8,128]{2,1,0:T(8,128)} %copy.31), calls=%async_computation.2 | async-start | bytes 131072 | tf_op jit(solution)/shard_map/all_to_all | solution.py:124

commit v5 on v4

--- a/solution.py
+++ b/solution.py
@@ -25,7 +25,6 @@
     def _():
         out_ref[...] = jnp.zeros_like(out_ref)
     cells = lax.broadcasted_iota(jnp.int32, (TILE, VB), 0)
-    lines = lax.broadcasted_iota(jnp.int32, (side, VB), 0)
     def one_block(b, carry):
         du = du_ref[pl.ds(b, 1), :]
         dv = dv_ref[pl.ds(b, 1), :]
@@ -35,12 +34,14 @@
         facet = seg // TT
         tile = seg % TT
         first_u = pl.multiple_of((tile // TS) * TILE, TILE)
-        first_v = (tile % TS) * TILE
+        tile_v = tile % TS
         along_u = (cells == du).astype(jnp.float32).astype(jnp.bfloat16)
-        hit_v = lines == (dv + first_v)
+        hit_v = cells == dv
+        parts = [jnp.where(hit_v, re, 0.0).astype(jnp.bfloat16), jnp.where(hit_v, im, 0.0).astype(jnp.bfloat16)]
+        empty = jnp.zeros((TILE, VB), jnp.bfloat16)
         spread = jnp.concatenate(
-            [jnp.where(hit_v, re, 0.0), jnp.where(hit_v, im, 0.0)], axis=0
-        ).astype(jnp.bfloat16)
+            [jnp.where(tile_v == t, part, empty) for part in parts for t in range(TS)], axis=0
+        )
         tile_sum = lax.dot_general(
             along_u, spread, (((1,), (1,)), ((), ())), preferred_element_type=jnp.float32
         )
@@ -116,15 +117,21 @@
     along_x = jnp.stack(
         [jnp.stack([cosine, sine], axis=2), jnp.stack([-sine, cosine], axis=2)], axis=1
     ).reshape(2 * side, 2 * side)
-    rows = jnp.einsum("kc,fcv->kfv", along_x, delta.reshape(facets, 2 * side, side), precision=high)
-    rows = rows.reshape(chan_count * row_count * 2 * facets, side)
+    used = jnp.arange(TS * OFFS, dtype=jnp.int32)
+    used = (used // OFFS) * TILE + used % OFFS
+    width = TS * OFFS
+    delta = delta.reshape(facets, 2 * side, TS, TILE)[..., :OFFS].reshape(facets, 2 * side, width)
+    rows = jnp.einsum("kc,fcv->kfv", along_x, delta, precision=high)
+    rows = rows.reshape(chan_count * row_count * 2 * facets * width // VB, VB)
     rows = lax.all_to_all(rows, "chan", split_axis=0, concat_axis=0, tiled=True)
-    rows = jnp.sum(rows.reshape(chan_count, row_count * 2, facets, side), axis=0)
-    rows = jnp.transpose(rows, (1, 0, 2)).reshape(facets * row_count * 2, side)
+    rows = jnp.sum(rows.reshape(chan_count, row_count * 2, facets, width), axis=0)
+    rows = jnp.transpose(rows, (1, 0, 2)).reshape(facets, row_count * 2 * width)
     rows = lax.all_to_all(rows, "stn", split_axis=0, concat_axis=0, tiled=True)
-    mine = jnp.sum(rows.reshape(facets, row_count, 2, side), axis=0)
+    mine = jnp.sum(rows.reshape(facets, row_count, 2, width), axis=0)
+    cos_used = cosine[used]
+    sin_used = sine[used]
     along_y = jnp.stack(
-        [jnp.stack([cosine, -sine], axis=1), jnp.stack([sine, cosine], axis=1)], axis=0
+        [jnp.stack([cos_used, -sin_used], axis=1), jnp.stack([sin_used, cos_used], axis=1)], axis=0
     )
     spectrum = jnp.einsum("rqv,qvsy->rsy", mine, along_y, precision=high)
     first_row = lax.axis_index("chan") * row_count

time: 206 us -> 216 us (1.049)
  local copies, waits for them, and re-layouts: 31.3 us -> 47.6 us
  waiting for transfers between devices: 60.6 us -> 49.8 us
    all_to_all x1, waiting for transfers between devices: 50.1 us -> 39.2 us  [body(): rows = lax.all_to_all(rows, 'chan', split_axis=0, concat_axis=0, tiled=True)]
    reshape x1, local copies, waits for them, and re-layouts: 1.63 us -> 7.28 us  [body(): delta.reshape(facets, 2 * side, TS, TILE)[..., :OFFS]]
    slice x0 -> x1, local copies, waits for them, and re-layouts: none -> 5.31 us  [body(): delta.reshape(facets, 2 * side, TS, TILE)[..., :OFFS]]
    all_to_all x0 -> x2, local copies, waits for them, and re-layouts: none -> 4.57 us  [the longest x1 3.82 us: body(): rows = lax.all_to_all(rows, 'chan', split_axis=0, concat_axis=0, tiled=True)]
where the time goes in v5:
time: 216 us; the launch traced here: 215 us
  Pallas kernels  80.6 us (37%)
  waiting for transfers between devices  49.8 us (23%)
  local copies, waits for them, and re-layouts  47.6 us (22%)
  starting transfers between devices  27 us (12%)
  other arithmetic  5.34 us (2%)
  matrix products  4.31 us (2%)
    pallas_call x1, Pallas kernels, grid_blocks(): pl.pallas_call(grid_kernel, out_shape=jax.ShapeDtypeStruct((facets, side,...  80.6 us
    all_to_all x1, waiting for transfers between devices, body(): rows = lax.all_to_all(rows, 'chan', split_axis=0, concat_axis=0, tiled=True)  39.2 us
    reshape x1, local copies, waits for them, and re-layouts, body(): along_x = jnp.stack([jnp.stack([cosine, sine], axis=2), jnp.stack([-sine,...  12.8 us
    all_to_all x1, starting transfers between devices, body(): lax.all_to_all(voltages, 'stn', split_axis=1, concat_axis=0, tiled=True)  11.8 us
    all_to_all x1, starting transfers between devices, body(): rows = lax.all_to_all(rows, 'chan', split_axis=0, concat_axis=0, tiled=True)  9.8 us
    another operation x1, local copies, waits for them, and re-layouts, body(): jnp.stack([jnp.stack([cosine, sine], axis=2), jnp.stack([-sine, cosine],...  8.6 us
    all_to_all x1, waiting for transfers between devices, body(): rows = lax.all_to_all(rows, 'stn', split_axis=0, concat_axis=0, tiled=True)  7.62 us
    reshape x1, local copies, waits for them, and re-layouts, body(): delta.reshape(facets, 2 * side, TS, TILE)[..., :OFFS]  7.28 us
  transfers between devices with their start and end apart: 3, of which 3 were waited for; matrix products, arithmetic and copies ran while one was open for 13% of the time, Pallas kernels for 0%

profile of v5, /device:TPU:1, one launch (start us, length us, event | category | flops | bytes accessed | tf_op | source)
XLA Modules:
  0.0 214.8 jit_solution(4607221326612644795)
XLA Ops:
  0.0 2.8 %copy.36 = bf16[16,64,512]{2,0,1:T(8,128)(2,1)} copy(bf16[16,64,512]{2,1,0:T(8,128)(2,1)} %param.5) | data formatting | bytes 2097152 | tf_op args[0]
  2.8 11.8 %all-to-all-start = ((bf16[16,64,512]{2,0,1:T(8,128)(2,1)}), bf16[16,64,512]{2,0,1:T(8,128)(2,1)S(1)}, u32[]{:S(2)}, u32[]{:S(2)}) async-start(bf16[16,64,512]{2,0,1:T(8,128)(2,1)} %copy.36), calls=%async_computation | async-start | bytes 2097152 | tf_op jit(solution)/shard_map/all_to_all | solution.py:94
  14.6 0.3 fusion.35
  14.9 0.3 fusion.33
  15.2 8.6 %copy.35 = f32[128,2,128,2]{3,2,1,0:T(8,128)} copy(f32[128,2,128,2]{2,0,3,1:T(8,128)S(1)} %pad_maximum_fusion) | data formatting | bytes 524288 | tf_op jit(solution)/shard_map/stack | solution.py:117
  23.8 12.8 %reshape.596 = f32[256,256,1]{1,0,2:T(8,128)S(1)} reshape(f32[128,2,128,2]{3,2,1,0:T(8,128)} %copy.35) | data formatting | bytes 524288 | tf_op jit(solution)/shard_map/reshape | solution.py:119
  36.6 0.6 add.132.seg_ref
  37.3 2.3 %add_select_fusion = (s32[2048,128]{1,0:T(8,128)}, s32[2048,128]{1,0:T(8,128)}) fusion(s32[1,1,2048,128]{3,2,1,0:T(8,128)S(1)} %copy-done), kind=kLoop, calls=%fused_computation.10 | loop fusion | flops 3145728 | bytes 3145728 | tf_op jit(solution)/shard_map/jit(remainder)/select_n | solution.py:111
  39.6 3.0 %all-to-all-done = bf16[16,64,512]{2,0,1:T(8,128)(2,1)S(1)} async-done(((bf16[16,64,512]{2,0,1:T(8,128)(2,1)}), bf16[16,64,512]{2,0,1:T(8,128)(2,1)S(1)}, u32[]{:S(2)}, u32[]{:S(2)}) %all-to-all-start) | async-done | bytes 1048608 | tf_op jit(solution)/shard_map/all_to_all | solution.py:94
  42.7 0.7 fusion
  43.4 0.2 fusion.14
  43.6 1.1 reshape.576.re_ref
  44.7 1.0 reshape.577.im_ref
  45.7 80.6 %shard_map.55 = f32[16,128,256]{2,1,0:T(8,128)} custom-call(s32[2048]{0:T(1024)} %add.132.seg_ref, s32[2048,128]{1,0:T(8,128)} %get-tuple-element.14.du_ref, s32[2048,128]{1,0:T(8,128)} %get-tuple-element.13.dv_ref, f32[2048,128]{1,0:T(8,128)} %reshape.576.re_ref, f32[2048,128]{1,0:T(8,128)} %reshape.577.im_ref), custom_call_target="tpu_custom_call" | custom-call | flops 4294967296 | bytes 6291456 | tf_op jit(solution)/shard_map/pallas_call | solution.py:57
  126.3 7.3 %reshape.574 = f32[16,256,4,32]{3,2,1,0:T(4,128)} reshape(f32[16,128,256]{2,1,0:T(8,128)} %shard_map.55) | data formatting | bytes 4194304 | tf_op jit(solution)/shard_map/reshape | solution.py:123
  133.6 5.3 %copy.38 = f32[16,256,4,25]{1,0,3,2:T(8,128)S(1)} copy(f32[16,256,4,25]{3,2,1,0:T(4,128)} %bitcast.72) | data formatting | bytes 3276800 | tf_op jit(solution)/shard_map/slice | solution.py:123
  138.9 3.4 %fusion.6 = f32[256,16,100]{0,2,1:T(8,128)} fusion(f32[256,256,1]{1,0,2:T(8,128)S(1)} %reshape.596, f32[16,256,100]{1,0,2:T(8,128)S(1)} %bitcast.73), kind=kOutput, calls=%fused_computation.8 | convolution fusion | flops 1258291200 | bytes 3538944 | tf_op jit(solution)/shard_map/kc,fcv->kfv/dot_general | solution.py:124
  142.3 2.4 %copy.40 = f32[256,16,100]{2,1,0:T(8,128)S(1)} copy(f32[256,16,100]{0,2,1:T(8,128)} %fusion.6) | data formatting | bytes 3276800 | tf_op jit(solution)/shard_map/kc,fcv->kfv/dot_general | solution.py:124
  144.7 3.8 %all_to_all.29 = f32[32,100,128]{2,1,0:T(8,128)} reshape(f32[256,16,100]{2,1,0:T(8,128)S(1)} %copy.40) | data formatting | bytes 3276800 | tf_op jit(solution)/shard_map/all_to_all | solution.py:126
  148.5 9.8 %all-to-all-start.1 = ((f32[32,100,128]{2,1,0:T(8,128)}), f32[32,100,128]{2,1,0:T(8,128)S(1)}, u32[]{:S(2)}, u32[]{:S(2)}) async-start(f32[32,100,128]{2,1,0:T(8,128)} %all_to_all.29), calls=%async_computation.1 | async-start | bytes 3407872 | tf_op jit(solution)/shard_map/all_to_all | solution.py:126
  158.4 0.3 fusion.31
  158.6 0.6 gather_fusion.1
  159.2 0.3 fusion.32
  159.5 0.6 gather_fusion
  160.5 39.2 %all-to-all-done.1 = f32[32,100,128]{2,1,0:T(8,128)S(1)} async-done(((f32[32,100,128]{2,1,0:T(8,128)}), f32[32,100,128]{2,1,0:T(8,128)S(1)}, u32[]{:S(2)}, u32[]{:S(2)}) %all-to-all-start.1) | async-done | bytes 1638432 | tf_op jit(solution)/shard_map/all_to_all | solution.py:126
  199.8 0.1 reduce_sum.59
  199.9 0.8 all_to_all.33
  200.7 5.4 %all-to-all-start.2 = ((f32[16,1,800]{2,1,0:T(1,128)}), f32[16,1,800]{2,1,0:T(1,128)S(1)}, u32[]{:S(2)}, u32[]{:S(2)}) async-start(f32[16,1,800]{2,1,0:T(1,128)} %all_to_all.33), calls=%async_computation.2 | async-start | bytes 114688 | tf_op jit(solution)/shard_map/all_to_all | solution.py:129
  206.1 7.6 %all-to-all-done.2 = f32[16,1,800]{2,1,0:T(1,128)S(1)} async-done(((f32[16,1,800]{2,1,0:T(1,128)}), f32[16,1,800]{2,1,0:T(1,128)S(1)}, u32[]{:S(2)}, u32[]{:S(2)}) %all-to-all-start.2) | async-done | bytes 51232 | tf_op jit(solution)/shard_map/all_to_all | solution.py:129
  213.9 0.2 convolution_bitcast_fusion
  214.0 0.1 subtract_multiply_fusion
  214.1 0.6 pad_maximum_fusion.1
  (29 shorter events, 0.8 us)
Async XLA Ops:
  2.8 39.8 %all-to-all-start = ((bf16[16,64,512]{2,0,1:T(8,128)(2,1)}), bf16[16,64,512]{2,0,1:T(8,128)(2,1)S(1)}, u32[]{:S(2)}, u32[]{:S(2)}) async-start(bf16[16,64,512]{2,0,1:T(8,128)(2,1)} %copy.36), calls=%async_computation | async-start | bytes 2097152 | tf_op jit(solution)/shard_map/all_to_all | solution.py:94
  23.8 12.8 %copy-start.2 = (s32[1,1,2048,1]{2,3,1,0:T(1,128)S(1)}, s32[1,1,2048,1]{2,3,1,0:T(1,128)}, u32[]{:S(2)}) copy-start(s32[1,1,2048,1]{2,3,1,0:T(1,128)} %param.6) | copy-start | bytes 24580
  23.8 12.8 %copy-start.1 = (s32[1,1,2048]{2,1,0:T(1,128)S(1)}, s32[1,1,2048]{2,1,0:T(1,128)}, u32[]{:S(2)}) copy-start(s32[1,1,2048]{2,1,0:T(1,128)} %param.7) | copy-start | bytes 24580
  23.8 13.4 %copy-start = (s32[1,1,2048,128]{3,2,1,0:T(8,128)S(1)}, s32[1,1,2048,128]{3,2,1,0:T(8,128)}, u32[]{:S(2)}) copy-start(s32[1,1,2048,128]{3,2,1,0:T(8,128)} %param.8) | copy-start | bytes 3145732
  148.5 11.6 %copy-start.3 = (bf16[2,8]{1,0:T(2,128)(2,1)S(1)}, bf16[2,8]{1,0:T(2,128)(2,1)}, u32[]{:S(2)}) copy-start(bf16[2,8]{1,0:T(2,128)(2,1)} %param.9) | copy-start | bytes 100
  148.5 51.2 %all-to-all-start.1 = ((f32[32,100,128]{2,1,0:T(8,128)}), f32[32,100,128]{2,1,0:T(8,128)S(1)}, u32[]{:S(2)}, u32[]{:S(2)}) async-start(f32[32,100,128]{2,1,0:T(8,128)} %all_to_all.29), calls=%async_computation.1 | async-start | bytes 3407872 | tf_op jit(solution)/shard_map/all_to_all | solution.py:126
  200.7 13.0 %all-to-all-start.2 = ((f32[16,1,800]{2,1,0:T(1,128)}), f32[16,1,800]{2,1,0:T(1,128)S(1)}, u32[]{:S(2)}, u32[]{:S(2)}) async-start(f32[16,1,800]{2,1,0:T(1,128)} %all_to_all.33), calls=%async_computation.2 | async-start | bytes 114688 | tf_op jit(solution)/shard_map/all_to_all | solution.py:129

commit v6 on v4

--- a/solution.py
+++ b/solution.py
@@ -14,25 +14,29 @@
 TS = 4
 TT = 16
 OFFS = 25
-CHUNK = 256
+GROUP = 8
 
 
-def grid_kernel(seg_ref, du_ref, dv_ref, re_ref, im_ref, out_ref):
-    step = pl.program_id(0)
+def grid_kernel(order_ref, seg_ref, bounds_ref, du_ref, dv_ref, re_ref, im_ref, out_ref):
     side = TS * TILE
-
-    @pl.when(step == 0)
-    def _():
-        out_ref[...] = jnp.zeros_like(out_ref)
+    half = out_ref.shape[0]
+    low = bounds_ref[2]
+    out_ref[...] = jnp.zeros_like(out_ref)
     cells = lax.broadcasted_iota(jnp.int32, (TILE, VB), 0)
     lines = lax.broadcasted_iota(jnp.int32, (side, VB), 0)
-    def one_block(b, carry):
+    first = bounds_ref[0]
+    last = bounds_ref[1]
+
+    def one_block(j):
+        valid = (j >= first) & (j < last)
+        place = jnp.minimum(j, du_ref.shape[0] - 1)
+        b = order_ref[place]
         du = du_ref[pl.ds(b, 1), :]
         dv = dv_ref[pl.ds(b, 1), :]
-        re = re_ref[pl.ds(b, 1), :]
-        im = im_ref[pl.ds(b, 1), :]
-        seg = seg_ref[step * CHUNK + b]
-        facet = seg // TT
+        re = jnp.where(valid, re_ref[pl.ds(b, 1), :], 0.0)
+        im = jnp.where(valid, im_ref[pl.ds(b, 1), :], 0.0)
+        seg = seg_ref[b]
+        facet = jnp.clip(seg // TT - low, 0, half - 1)
         tile = seg % TT
         first_u = pl.multiple_of((tile // TS) * TILE, TILE)
         first_v = (tile % TS) * TILE
@@ -45,29 +49,34 @@
             along_u, spread, (((1,), (1,)), ((), ())), preferred_element_type=jnp.float32
         )
         out_ref[facet, pl.ds(first_u, TILE), :] += tile_sum
+
+    def group(g, carry):
+        for i in range(GROUP):
+            one_block(g * GROUP + i)
         return carry
-    lax.fori_loop(0, CHUNK, one_block, 0, unroll=8)
+
+    lax.fori_loop(first // GROUP, (last + GROUP - 1) // GROUP, group, 0)
 
 
-def grid_blocks(seg_ids, du, dv, re, im, facets):
+def grid_blocks(order, seg_ids, bounds, du, dv, re, im, half):
     blocks = du.shape[0]
     side = TS * TILE
-    row_spec = pl.BlockSpec((CHUNK, VB), lambda i, seg: (i, 0))
+    row_spec = pl.BlockSpec((blocks, VB), lambda i, *_: (0, 0))
     return pl.pallas_call(
         grid_kernel,
-        out_shape=jax.ShapeDtypeStruct((facets, side, 2 * side), jnp.float32),
+        out_shape=jax.ShapeDtypeStruct((half, side, 2 * side), jnp.float32),
         grid_spec=pltpu.PrefetchScalarGridSpec(
-            num_scalar_prefetch=1,
-            grid=(blocks // CHUNK,),
+            num_scalar_prefetch=3,
+            grid=(1,),
             in_specs=[row_spec] * 4,
-            out_specs=pl.BlockSpec((facets, side, 2 * side), lambda i, seg: (0, 0, 0)),
+            out_specs=pl.BlockSpec((half, side, 2 * side), lambda i, *_: (0, 0, 0)),
         ),
         cost_estimate=pl.CostEstimate(
-            flops=blocks * TILE * VB * 2 * side * 2,
-            bytes_accessed=blocks * VB * 16 + facets * side * 2 * side * 4,
+            flops=blocks * TILE * VB * 2 * side,
+            bytes_accessed=blocks * VB * 16 + half * side * 2 * side * 4,
             transcendentals=0,
         ),
-    )(seg_ids, du, dv, re, im)
+    )(order, seg_ids, bounds, du, dv, re, im)
 
 
 def dft_tables(side):
@@ -109,17 +118,25 @@
     du = offsets // OFFS
     dv = offsets % OFFS
     seg_ids = block_facet.reshape(block_count) * TT + block_tile.reshape(block_count)
-    delta = grid_blocks(seg_ids, du, dv, re, im, facets)
+    half = facets // 2
+    later = (block_facet.reshape(block_count) >= half).astype(jnp.int32)
+    order = jnp.argsort(later, stable=True).astype(jnp.int32)
+    split = block_count - jnp.sum(later)
     side = TS * TILE
     row_count = side // chan_count
     cosine, sine = dft_tables(side)
     along_x = jnp.stack(
         [jnp.stack([cosine, sine], axis=2), jnp.stack([-sine, cosine], axis=2)], axis=1
     ).reshape(2 * side, 2 * side)
-    rows = jnp.einsum("kc,fcv->kfv", along_x, delta.reshape(facets, 2 * side, side), precision=high)
-    rows = rows.reshape(chan_count * row_count * 2 * facets, side)
-    rows = lax.all_to_all(rows, "chan", split_axis=0, concat_axis=0, tiled=True)
-    rows = jnp.sum(rows.reshape(chan_count, row_count * 2, facets, side), axis=0)
+    summed = []
+    for low, first, last in ((0, 0, split), (half, split, block_count)):
+        bounds = jnp.stack([first, last, low]).astype(jnp.int32)
+        delta = grid_blocks(order, seg_ids, bounds, du, dv, re, im, half)
+        rows = jnp.einsum("kc,fcv->kfv", along_x, delta.reshape(half, 2 * side, side), precision=high)
+        rows = rows.reshape(chan_count * row_count * 2 * half, side)
+        rows = lax.all_to_all(rows, "chan", split_axis=0, concat_axis=0, tiled=True)
+        summed.append(jnp.sum(rows.reshape(chan_count, row_count * 2, half, side), axis=0))
+    rows = jnp.concatenate(summed, axis=1)
     rows = jnp.transpose(rows, (1, 0, 2)).reshape(facets * row_count * 2, side)
     rows = lax.all_to_all(rows, "stn", split_axis=0, concat_axis=0, tiled=True)
     mine = jnp.sum(rows.reshape(facets, row_count, 2, side), axis=0)

time: 206 us -> 209 us (1.015)
  waiting for transfers between devices: 60.6 us -> 31.2 us
  starting transfers between devices: 25.9 us -> 44 us
  other arithmetic: 5.3 us -> 11.7 us
  Pallas kernels: 79 us -> 84.1 us
    all_to_all x1 -> x2, waiting for transfers between devices: 50.1 us -> 23.7 us  [body(): rows = lax.all_to_all(rows, 'chan', split_axis=0, concat_axis=0, tiled=True)]
    all_to_all x1 -> x2, starting transfers between devices: 9.8 us -> 21.1 us  [body(): rows = lax.all_to_all(rows, 'chan', split_axis=0, concat_axis=0, tiled=True)]
    all_to_all x1, starting transfers between devices: 4.26 us -> 11 us  [body(): rows = lax.all_to_all(rows, 'stn', split_axis=0, concat_axis=0, tiled=True)]
    pallas_call x1 -> x2, Pallas kernels: 79 us -> 84.1 us  [grid_blocks(): pl.pallas_call(grid_kernel, out_shape=jax.ShapeDtypeStruct((half, side, 2...]
    sort x0 -> x1, other arithmetic: none -> 5.05 us  [body(): order = jnp.argsort(later, stable=True).astype(jnp.int32)]
    all_to_all x1, waiting for transfers between devices: 3.02 us -> 0.01 us  [body(): lax.all_to_all(voltages, 'stn', split_axis=1, concat_axis=0, tiled=True)]
  transfers between devices with their start and end apart: 3 -> 4, of which waited for: 3 -> 2; matrix products, arithmetic and copies ran while one was open for 13% -> 17% of each run, Pallas kernels for 0% -> 20%
where the time goes in v6:
time: 209 us; the launch traced here: 208 us
  Pallas kernels  84.1 us (40%)
  starting transfers between devices  44 us (21%)
  local copies, waits for them, and re-layouts  33 us (16%)
  waiting for transfers between devices  31.2 us (15%)
  other arithmetic  11.7 us (6%)
  matrix products  2.99 us (1%)
    pallas_call x2, Pallas kernels, grid_blocks(): pl.pallas_call(grid_kernel, out_shape=jax.ShapeDtypeStruct((half, side, 2...  84.1 us
    all_to_all x2, waiting for transfers between devices, body(): rows = lax.all_to_all(rows, 'chan', split_axis=0, concat_axis=0, tiled=True)  23.7 us
    all_to_all x2, starting transfers between devices, body(): rows = lax.all_to_all(rows, 'chan', split_axis=0, concat_axis=0, tiled=True)  21.1 us
    reshape x1, local copies, waits for them, and re-layouts, body(): along_x = jnp.stack([jnp.stack([cosine, sine], axis=2), jnp.stack([-sine,...  12.8 us
    all_to_all x1, starting transfers between devices, body(): lax.all_to_all(voltages, 'stn', split_axis=1, concat_axis=0, tiled=True)  11.8 us
    all_to_all x1, starting transfers between devices, body(): rows = lax.all_to_all(rows, 'stn', split_axis=0, concat_axis=0, tiled=True)  11 us
    another operation x1, local copies, waits for them, and re-layouts, body(): jnp.stack([jnp.stack([cosine, sine], axis=2), jnp.stack([-sine, cosine],...  8.66 us
    all_to_all x1, waiting for transfers between devices, body(): rows = lax.all_to_all(rows, 'stn', split_axis=0, concat_axis=0, tiled=True)  7.54 us
  transfers between devices with their start and end apart: 4, of which 2 were waited for; matrix products, arithmetic and copies ran while one was open for 17% of the time, Pallas kernels for 20%

profile of v6, /device:TPU:1, one launch (start us, length us, event | category | flops | bytes accessed | tf_op | source)
XLA Modules:
  0.0 207.8 jit_solution(17948200232222528710)
XLA Ops:
  0.0 2.8 %copy.31 = bf16[16,64,512]{2,0,1:T(8,128)(2,1)} copy(bf16[16,64,512]{2,1,0:T(8,128)(2,1)} %param.5) | data formatting | bytes 2097152 | tf_op args[0]
  2.8 11.8 %all-to-all-start = ((bf16[16,64,512]{2,0,1:T(8,128)(2,1)}), bf16[16,64,512]{2,0,1:T(8,128)(2,1)S(1)}, u32[]{:S(2)}, u32[]{:S(2)}) async-start(bf16[16,64,512]{2,0,1:T(8,128)(2,1)} %copy.31), calls=%async_computation | async-start | bytes 2097152 | tf_op jit(solution)/shard_map/all_to_all | solution.py:102
  14.6 0.3 fusion.33
  14.9 0.3 fusion.31
  15.2 8.7 %copy.30 = f32[128,2,128,2]{3,2,1,0:T(8,128)} copy(f32[128,2,128,2]{2,0,3,1:T(8,128)S(1)} %pad_maximum_fusion) | data formatting | bytes 524288 | tf_op jit(solution)/shard_map/stack | solution.py:128
  23.9 12.8 %reshape.599 = f32[256,256,1]{1,0,2:T(8,128)S(1)} reshape(f32[128,2,128,2]{3,2,1,0:T(8,128)} %copy.30) | data formatting | bytes 524288 | tf_op jit(solution)/shard_map/reshape | solution.py:130
  36.7 5.1 %sort.17 = (s32[2048]{0:T(1024)}, s32[2048]{0:T(1024)}) sort(s32[2048]{0:T(1024)S(1)} %bitcast.82, s32[2048]{0:T(1024)S(1)} %iota.70), dimensions={0}, to_apply=%region_0.1 | sort | flops 22528 | bytes 32768 | tf_op jit(solution)/shard_map/jit(argsort)/sort | solution.py:123
  41.8 0.6 fusion.47
  42.4 0.6 add.103.seg_ref
  43.7 0.7 pad_add_fusion
  44.4 2.3 %add_select_fusion = (s32[2048,128]{1,0:T(8,128)}, s32[2048,128]{1,0:T(8,128)}) fusion(s32[1,1,2048,128]{3,2,1,0:T(8,128)S(1)} %copy-done), kind=kLoop, calls=%fused_computation.6 | loop fusion | flops 3145728 | bytes 3145728 | tf_op jit(solution)/shard_map/jit(remainder)/select_n | solution.py:119
  46.9 0.7 fusion
  47.8 1.1 reshape.595.re_ref
  48.8 1.0 reshape.596.im_ref
  49.9 43.4 %shard_map.56 = f32[8,128,256]{2,1,0:T(8,128)} custom-call(s32[2048]{0:T(1024)} %get-tuple-element.6.order_ref, s32[2048]{0:T(1024)} %add.103.seg_ref, s32[3]{0:T(128)} %get-tuple-element.32.bounds_ref, s32[2048,128]{1,0:T(8,128)} %get-tuple-element.16.du_ref, s32[2048,128]{1,0:T(8,128)} %get-tuple-element.15.dv_ref, f32[2048,128]{1,0:T(8,128)} %reshape.595.re_ref, ...), custom_call_target="tpu_custom_call" | custom-call | flops 2147483648 | bytes 5242880 | tf_op jit(solution)/shard_map/pallas_call | solution.py:65
  93.2 1.3 reshape.594
  94.5 1.0 fusion.50
  95.6 1.6 copy.34
  97.1 11.3 %all-to-all-start.2 = ((f32[32,64,128]{2,1,0:T(8,128)}), f32[32,64,128]{2,1,0:T(8,128)S(1)}, u32[]{:S(2)}, u32[]{:S(2)}) async-start(f32[32,64,128]{2,1,0:T(8,128)} %bitcast.15), calls=%async_computation.2 | async-start | bytes 2097152 | tf_op jit(solution)/shard_map/all_to_all | solution.py:137
  108.5 40.7 %shard_map.55 = f32[8,128,256]{2,1,0:T(8,128)} custom-call(s32[2048]{0:T(1024)} %get-tuple-element.6.order_ref, s32[2048]{0:T(1024)} %add.103.seg_ref, s32[3]{0:T(128)} %get-tuple-element.31.bounds_ref, s32[2048,128]{1,0:T(8,128)} %get-tuple-element.16.du_ref, s32[2048,128]{1,0:T(8,128)} %get-tuple-element.15.dv_ref, f32[2048,128]{1,0:T(8,128)} %reshape.595.re_ref, ...), custom_call_target="tpu_custom_call" | custom-call | flops 2147483648 | bytes 5242880 | tf_op jit(solution)/shard_map/pallas_call | solution.py:65
  149.2 1.3 reshape.593
  150.5 1.0 fusion.49
  151.6 1.6 copy.33
  153.2 9.8 %all-to-all-start.1 = ((f32[32,64,128]{2,1,0:T(8,128)}), f32[32,64,128]{2,1,0:T(8,128)S(1)}, u32[]{:S(2)}, u32[]{:S(2)}) async-start(f32[32,64,128]{2,1,0:T(8,128)} %bitcast.13), calls=%async_computation.1 | async-start | bytes 2097152 | tf_op jit(solution)/shard_map/all_to_all | solution.py:137
  163.1 0.3 fusion.34
  163.4 0.3 fusion.29
  163.7 23.7 %all-to-all-done.1 = f32[32,64,128]{2,1,0:T(8,128)S(1)} async-done(((f32[32,64,128]{2,1,0:T(8,128)}), f32[32,64,128]{2,1,0:T(8,128)S(1)}, u32[]{:S(2)}, u32[]{:S(2)}) %all-to-all-start.1) | async-done | bytes 1048608 | tf_op jit(solution)/shard_map/all_to_all | solution.py:137
  187.5 0.6 copy.35
  188.1 11.0 %all-to-all-start.3 = ((f32[16,8,128]{2,1,0:T(8,128)}), f32[16,8,128]{2,1,0:T(8,128)S(1)}, u32[]{:S(2)}, u32[]{:S(2)}) async-start(f32[16,8,128]{2,1,0:T(8,128)} %copy.35), calls=%async_computation.3 | async-start | bytes 131072 | tf_op jit(solution)/shard_map/all_to_all | solution.py:141
  199.4 7.5 %all-to-all-done.3 = f32[16,8,128]{2,1,0:T(8,128)S(1)} async-done(((f32[16,8,128]{2,1,0:T(8,128)}), f32[16,8,128]{2,1,0:T(8,128)S(1)}, u32[]{:S(2)}, u32[]{:S(2)}) %all-to-all-start.3) | async-done | bytes 65568 | tf_op jit(solution)/shard_map/all_to_all | solution.py:141
  206.9 0.2 convolution_bitcast_fusion
  207.2 0.6 pad_maximum_fusion.1
  (31 shorter events, 1.0 us)
Async XLA Ops:
  2.8 43.9 %all-to-all-start = ((bf16[16,64,512]{2,0,1:T(8,128)(2,1)}), bf16[16,64,512]{2,0,1:T(8,128)(2,1)S(1)}, u32[]{:S(2)}, u32[]{:S(2)}) async-start(bf16[16,64,512]{2,0,1:T(8,128)(2,1)} %copy.31), calls=%async_computation | async-start | bytes 2097152 | tf_op jit(solution)/shard_map/all_to_all | solution.py:102
  23.9 12.8 %copy-start.1 = (s32[1,1,2048,1]{2,3,1,0:T(1,128)S(1)}, s32[1,1,2048,1]{2,3,1,0:T(1,128)}, u32[]{:S(2)}) copy-start(s32[1,1,2048,1]{2,3,1,0:T(1,128)} %param.6) | copy-start | bytes 24580
  23.9 18.5 %copy-start.2 = (s32[1,1,2048]{2,1,0:T(1,128)S(1)}, s32[1,1,2048]{2,1,0:T(1,128)}, u32[]{:S(2)}) copy-start(s32[1,1,2048]{2,1,0:T(1,128)} %param.7) | copy-start | bytes 24580
  23.9 20.5 %copy-start = (s32[1,1,2048,128]{3,2,1,0:T(8,128)S(1)}, s32[1,1,2048,128]{3,2,1,0:T(8,128)}, u32[]{:S(2)}) copy-start(s32[1,1,2048,128]{3,2,1,0:T(8,128)} %param.8) | copy-start | bytes 3145732
  97.1 56.0 %all-to-all-start.2 = ((f32[32,64,128]{2,1,0:T(8,128)}), f32[32,64,128]{2,1,0:T(8,128)S(1)}, u32[]{:S(2)}, u32[]{:S(2)}) async-start(f32[32,64,128]{2,1,0:T(8,128)} %bitcast.15), calls=%async_computation.2 | async-start | bytes 2097152 | tf_op jit(solution)/shard_map/all_to_all | solution.py:137
  151.6 11.4 %copy-start.3 = (bf16[2,8]{1,0:T(2,128)(2,1)S(1)}, bf16[2,8]{1,0:T(2,128)(2,1)}, u32[]{:S(2)}) copy-start(bf16[2,8]{1,0:T(2,128)(2,1)} %param.9) | copy-start | bytes 100
  153.2 34.2 %all-to-all-start.1 = ((f32[32,64,128]{2,1,0:T(8,128)}), f32[32,64,128]{2,1,0:T(8,128)S(1)}, u32[]{:S(2)}, u32[]{:S(2)}) async-start(f32[32,64,128]{2,1,0:T(8,128)} %bitcast.13), calls=%async_computation.1 | async-start | bytes 2097152 | tf_op jit(solution)/shard_map/all_to_all | solution.py:137
  188.1 18.8 %all-to-all-start.3 = ((f32[16,8,128]{2,1,0:T(8,128)}), f32[16,8,128]{2,1,0:T(8,128)S(1)}, u32[]{:S(2)}, u32[]{:S(2)}) async-start(f32[16,8,128]{2,1,0:T(8,128)} %copy.35), calls=%async_computation.3 | async-start | bytes 131072 | tf_op jit(solution)/shard_map/all_to_all | solution.py:141

commit v7 on v4

--- a/solution.py
+++ b/solution.py
@@ -117,12 +117,10 @@
         [jnp.stack([cosine, sine], axis=2), jnp.stack([-sine, cosine], axis=2)], axis=1
     ).reshape(2 * side, 2 * side)
     rows = jnp.einsum("kc,fcv->kfv", along_x, delta.reshape(facets, 2 * side, side), precision=high)
-    rows = rows.reshape(chan_count * row_count * 2 * facets, side)
-    rows = lax.all_to_all(rows, "chan", split_axis=0, concat_axis=0, tiled=True)
-    rows = jnp.sum(rows.reshape(chan_count, row_count * 2, facets, side), axis=0)
-    rows = jnp.transpose(rows, (1, 0, 2)).reshape(facets * row_count * 2, side)
-    rows = lax.all_to_all(rows, "stn", split_axis=0, concat_axis=0, tiled=True)
-    mine = jnp.sum(rows.reshape(facets, row_count, 2, side), axis=0)
+    rows = rows.reshape(chan_count, row_count * 2, facets, side)
+    rows = jnp.transpose(rows, (2, 0, 1, 3)).reshape(facets * chan_count * row_count * 2, side)
+    rows = lax.all_to_all(rows, ("stn", "chan"), split_axis=0, concat_axis=0, tiled=True)
+    mine = jnp.sum(rows.reshape(facets * chan_count, row_count, 2, side), axis=0)
     along_y = jnp.stack(
         [jnp.stack([cosine, -sine], axis=1), jnp.stack([sine, cosine], axis=1)], axis=0
     )

time: 206 us -> 202 us (0.981)
  waiting for transfers between devices: 60.6 us -> 57.9 us
    reshape x1 -> x0, local copies, waits for them, and re-layouts: 12.8 us -> none  [body(): along_x = jnp.stack([jnp.stack([cosine, sine], axis=2), jnp.stack([-sine,...]
    dot_general x1, local copies, waits for them, and re-layouts: 2.55 us -> 12.8 us  [body(): jnp.einsum('kc,fcv->kfv', along_x, delta.reshape(facets, 2 * side, side),...]
    all_to_all x2 -> x1, waiting for transfers between devices: 57.6 us -> 54.9 us  [body(): lax.all_to_all(rows, ('stn', 'chan'), split_axis=0, concat_axis=0, tiled=...]
    all_to_all x2 -> x1, starting transfers between devices: 14.1 us -> 14.6 us  [body(): lax.all_to_all(rows, ('stn', 'chan'), split_axis=0, concat_axis=0, tiled=...]
  transfers between devices with their start and end apart: 3 -> 2, of which waited for: 3 -> 2; matrix products, arithmetic and copies ran while one was open for 13% -> 13% of each run, Pallas kernels for 0% -> 0%
where the time goes in v7:
time: 202 us
  Pallas kernels  79 us (39%)
  waiting for transfers between devices  57.9 us (29%)
  local copies, waits for them, and re-layouts  29.6 us (15%)
  starting transfers between devices  26.4 us (13%)
  other arithmetic  5.72 us (3%)
  matrix products  2.83 us (1%)
    pallas_call x1, Pallas kernels, grid_blocks(): pl.pallas_call(grid_kernel, out_shape=jax.ShapeDtypeStruct((facets, side,...  79 us
    all_to_all x1, waiting for transfers between devices, body(): lax.all_to_all(rows, ('stn', 'chan'), split_axis=0, concat_axis=0, tiled=...  54.9 us
    all_to_all x1, starting transfers between devices, body(): lax.all_to_all(rows, ('stn', 'chan'), split_axis=0, concat_axis=0, tiled=...  14.6 us
    dot_general x1, local copies, waits for them, and re-layouts, body(): jnp.einsum('kc,fcv->kfv', along_x, delta.reshape(facets, 2 * side, side),...  12.8 us
    all_to_all x1, starting transfers between devices, body(): lax.all_to_all(voltages, 'stn', split_axis=1, concat_axis=0, tiled=True)  11.8 us
    another operation x1, local copies, waits for them, and re-layouts, body(): jnp.stack([jnp.stack([cosine, sine], axis=2), jnp.stack([-sine, cosine],...  8.56 us
  transfers between devices with their start and end apart: 2, of which 2 were waited for; matrix products, arithmetic and copies ran while one was open for 13% of the time, Pallas kernels for 0%

profile of v7, /device:TPU:1, one launch (start us, length us, event | category | flops | bytes accessed | tf_op | source)
XLA Modules:
  0.0 201.7 jit_solution(13616624064382418008)
XLA Ops:
  0.0 2.8 %copy.21 = bf16[16,64,512]{2,0,1:T(8,128)(2,1)} copy(bf16[16,64,512]{2,1,0:T(8,128)(2,1)} %param.5) | data formatting | bytes 2097152 | tf_op args[0]
  2.8 11.8 %all-to-all-start = ((bf16[16,64,512]{2,0,1:T(8,128)(2,1)}), bf16[16,64,512]{2,0,1:T(8,128)(2,1)S(1)}, u32[]{:S(2)}, u32[]{:S(2)}) async-start(bf16[16,64,512]{2,0,1:T(8,128)(2,1)} %copy.21), calls=%async_computation | async-start | bytes 2097152 | tf_op jit(solution)/shard_map/all_to_all | solution.py:93
  14.6 0.3 fusion.34
  14.9 0.3 fusion.32
  15.2 8.6 %copy.20 = f32[128,2,128,2]{3,2,1,0:T(8,128)} copy(f32[128,2,128,2]{2,0,3,1:T(8,128)S(1)} %pad_maximum_fusion) | data formatting | bytes 524288 | tf_op jit(solution)/shard_map/stack | solution.py:116
  23.8 12.8 %reshape.577 = f32[32,8,256,1]{2,1,0,3:T(8,128)S(1)} reshape(f32[128,2,128,2]{3,2,1,0:T(8,128)} %copy.20) | data formatting | bytes 524288 | tf_op jit(solution)/shard_map/kc,fcv->kfv/dot_general | solution.py:119
  36.6 0.0 copy-done.1
  36.6 0.6 add.103.seg_ref
  37.2 2.3 %add_select_fusion = (s32[2048,128]{1,0:T(8,128)}, s32[2048,128]{1,0:T(8,128)}) fusion(s32[1,1,2048,128]{3,2,1,0:T(8,128)S(1)} %copy-done), kind=kLoop, calls=%fused_computation.7 | loop fusion | flops 3145728 | bytes 3145728 | tf_op jit(solution)/shard_map/jit(remainder)/select_n | solution.py:110
  39.5 3.0 %all-to-all-done = bf16[16,64,512]{2,0,1:T(8,128)(2,1)S(1)} async-done(((bf16[16,64,512]{2,0,1:T(8,128)(2,1)}), bf16[16,64,512]{2,0,1:T(8,128)(2,1)S(1)}, u32[]{:S(2)}, u32[]{:S(2)}) %all-to-all-start) | async-done | bytes 1048608 | tf_op jit(solution)/shard_map/all_to_all | solution.py:93
  42.5 0.1 copy.22
  42.6 0.1 fusion.48
  42.7 0.7 fusion
  43.4 0.2 fusion.12
  43.6 1.1 reshape.573.re_ref
  44.6 1.1 reshape.574.im_ref
  45.7 79.0 %shard_map.55 = f32[16,128,256]{2,1,0:T(8,128)} custom-call(s32[2048]{0:T(1024)} %add.103.seg_ref, s32[2048,128]{1,0:T(8,128)} %get-tuple-element.14.du_ref, s32[2048,128]{1,0:T(8,128)} %get-tuple-element.13.dv_ref, f32[2048,128]{1,0:T(8,128)} %reshape.573.re_ref, f32[2048,128]{1,0:T(8,128)} %reshape.574.im_ref), custom_call_target="tpu_custom_call" | custom-call | flops 4294967296 | bytes 6291456 | tf_op jit(solution)/shard_map/pallas_call | solution.py:56
  124.7 1.6 reshape.578
  126.3 1.9 convolution_bitcast_fusion
  128.3 1.5 copy.23
  129.8 14.6 %all-to-all-start.1 = ((f32[512,8,128]{2,1,0:T(8,128)}), f32[512,8,128]{2,1,0:T(8,128)S(1)}, u32[]{:S(2)}, u32[]{:S(2)}) async-start(f32[512,8,128]{2,1,0:T(8,128)} %bitcast.71), calls=%async_computation.1 | async-start | bytes 4194304 | tf_op jit(solution)/shard_map/all_to_all | solution.py:122
  144.4 0.1 multiply_reduce_fusion.3
  144.5 0.1 dynamic_slice.7
  144.6 0.1 dynamic_slice.6
  144.6 0.1 multiply_reduce_fusion.2
  144.7 0.3 fusion.35
  145.0 0.3 fusion.30
  145.3 54.9 %all-to-all-done.1 = f32[512,8,128]{2,1,0:T(8,128)S(1)} async-done(((f32[512,8,128]{2,1,0:T(8,128)}), f32[512,8,128]{2,1,0:T(8,128)S(1)}, u32[]{:S(2)}, u32[]{:S(2)}) %all-to-all-start.1) | async-done | bytes 2097184 | tf_op jit(solution)/shard_map/all_to_all | solution.py:122
  200.2 0.5 reduce_sum.47
  200.8 0.2 convolution_bitcast_fusion.1
  200.9 0.1 subtract_multiply_fusion
  201.1 0.6 pad_maximum_fusion.1
  (15 shorter events, 0.1 us)
Async XLA Ops:
  2.8 39.8 %all-to-all-start = ((bf16[16,64,512]{2,0,1:T(8,128)(2,1)}), bf16[16,64,512]{2,0,1:T(8,128)(2,1)S(1)}, u32[]{:S(2)}, u32[]{:S(2)}) async-start(bf16[16,64,512]{2,0,1:T(8,128)(2,1)} %copy.21), calls=%async_computation | async-start | bytes 2097152 | tf_op jit(solution)/shard_map/all_to_all | solution.py:93
  23.8 12.8 %copy-start.2 = (s32[1,1,2048,1]{2,3,1,0:T(1,128)S(1)}, s32[1,1,2048,1]{2,3,1,0:T(1,128)}, u32[]{:S(2)}) copy-start(s32[1,1,2048,1]{2,3,1,0:T(1,128)} %param.6) | copy-start | bytes 24580
  23.8 12.8 %copy-start.1 = (s32[1,1,2048]{2,1,0:T(1,128)S(1)}, s32[1,1,2048]{2,1,0:T(1,128)}, u32[]{:S(2)}) copy-start(s32[1,1,2048]{2,1,0:T(1,128)} %param.7) | copy-start | bytes 24580
  23.8 13.4 %copy-start = (s32[1,1,2048,128]{3,2,1,0:T(8,128)S(1)}, s32[1,1,2048,128]{3,2,1,0:T(8,128)}, u32[]{:S(2)}) copy-start(s32[1,1,2048,128]{3,2,1,0:T(8,128)} %param.8) | copy-start | bytes 3145732
  129.8 14.6 %copy-start.3 = (bf16[2,8]{1,0:T(2,128)(2,1)S(1)}, bf16[2,8]{1,0:T(2,128)(2,1)}, u32[]{:S(2)}) copy-start(bf16[2,8]{1,0:T(2,128)(2,1)} %param.9) | copy-start | bytes 100
  129.8 70.4 %all-to-all-start.1 = ((f32[512,8,128]{2,1,0:T(8,128)}), f32[512,8,128]{2,1,0:T(8,128)S(1)}, u32[]{:S(2)}, u32[]{:S(2)}) async-start(f32[512,8,128]{2,1,0:T(8,128)} %bitcast.71), calls=%async_computation.1 | async-start | bytes 4194304 | tf_op jit(solution)/shard_map/all_to_all | solution.py:122

commit v8 on v7

--- a/solution.py
+++ b/solution.py
@@ -15,18 +15,21 @@
 TT = 16
 OFFS = 25
 CHUNK = 256
+SPARE = 3
 
 
-def grid_kernel(seg_ref, du_ref, dv_ref, re_ref, im_ref, out_ref):
+def grid_kernel(seg_ref, du_ref, dv_ref, re_ref, im_ref, out_ref, spare_ref):
     step = pl.program_id(0)
     side = TS * TILE
+    sums = [out_ref] + [spare_ref.at[i] for i in range(spare_ref.shape[0])]
 
     @pl.when(step == 0)
     def _():
         out_ref[...] = jnp.zeros_like(out_ref)
+        spare_ref[...] = jnp.zeros_like(spare_ref)
     cells = lax.broadcasted_iota(jnp.int32, (TILE, VB), 0)
     lines = lax.broadcasted_iota(jnp.int32, (side, VB), 0)
-    def one_block(b, carry):
+    def one_block(b, total):
         du = du_ref[pl.ds(b, 1), :]
         dv = dv_ref[pl.ds(b, 1), :]
         re = re_ref[pl.ds(b, 1), :]
@@ -44,9 +47,18 @@
         tile_sum = lax.dot_general(
             along_u, spread, (((1,), (1,)), ((), ())), preferred_element_type=jnp.float32
         )
-        out_ref[facet, pl.ds(first_u, TILE), :] += tile_sum
+        total[facet, pl.ds(first_u, TILE), :] += tile_sum
+
+    def blocks(g, carry):
+        for i, total in enumerate(sums):
+            one_block(g * len(sums) + i, total)
         return carry
-    lax.fori_loop(0, CHUNK, one_block, 0, unroll=8)
+
+    lax.fori_loop(0, CHUNK // len(sums), blocks, 0, unroll=2)
+
+    @pl.when(step == pl.num_programs(0) - 1)
+    def _():
+        out_ref[...] += jnp.sum(spare_ref[...], axis=0)
 
 
 def grid_blocks(seg_ids, du, dv, re, im, facets):
@@ -61,6 +73,7 @@
             grid=(blocks // CHUNK,),
             in_specs=[row_spec] * 4,
             out_specs=pl.BlockSpec((facets, side, 2 * side), lambda i, seg: (0, 0, 0)),
+            scratch_shapes=[pltpu.VMEM((SPARE, facets, side, 2 * side), jnp.float32)],
         ),
         cost_estimate=pl.CostEstimate(
             flops=blocks * TILE * VB * 2 * side * 2,

time: 202 us -> 202 us (level)
  no operation moved by 1% of the time
where the time goes in v8:
time: 202 us
  Pallas kernels  79 us (39%)
  waiting for transfers between devices  57.9 us (29%)
  local copies, waits for them, and re-layouts  29.6 us (15%)
  starting transfers between devices  26.4 us (13%)
  other arithmetic  5.72 us (3%)
  matrix products  2.83 us (1%)
    pallas_call x1, Pallas kernels, grid_blocks(): pl.pallas_call(grid_kernel, out_shape=jax.ShapeDtypeStruct((facets, side,...  79 us
    all_to_all x1, waiting for transfers between devices, body(): lax.all_to_all(rows, ('stn', 'chan'), split_axis=0, concat_axis=0, tiled=...  54.9 us
    all_to_all x1, starting transfers between devices, body(): lax.all_to_all(rows, ('stn', 'chan'), split_axis=0, concat_axis=0, tiled=...  14.5 us
    dot_general x1, local copies, waits for them, and re-layouts, body(): jnp.einsum('kc,fcv->kfv', along_x, delta.reshape(facets, 2 * side, side),...  12.8 us
    all_to_all x1, starting transfers between devices, body(): lax.all_to_all(voltages, 'stn', split_axis=1, concat_axis=0, tiled=True)  11.8 us
    another operation x1, local copies, waits for them, and re-layouts, body(): jnp.stack([jnp.stack([cosine, sine], axis=2), jnp.stack([-sine, cosine],...  8.56 us
  transfers between devices with their start and end apart: 2, of which 2 were waited for; matrix products, arithmetic and copies ran while one was open for 13% of the time, Pallas kernels for 0%

profile of v8, /device:TPU:1, one launch (start us, length us, event | category | flops | bytes accessed | tf_op | source)
XLA Modules:
  0.0 201.7 jit_solution(3702311209883290159)
XLA Ops:
  0.0 2.8 %copy.21 = bf16[16,64,512]{2,0,1:T(8,128)(2,1)} copy(bf16[16,64,512]{2,1,0:T(8,128)(2,1)} %param.5) | data formatting | bytes 2097152 | tf_op args[0]
  2.8 11.8 %all-to-all-start = ((bf16[16,64,512]{2,0,1:T(8,128)(2,1)}), bf16[16,64,512]{2,0,1:T(8,128)(2,1)S(1)}, u32[]{:S(2)}, u32[]{:S(2)}) async-start(bf16[16,64,512]{2,0,1:T(8,128)(2,1)} %copy.21), calls=%async_computation | async-start | bytes 2097152 | tf_op jit(solution)/shard_map/all_to_all | solution.py:106
  14.6 0.3 fusion.34
  14.9 0.3 fusion.32
  15.2 8.6 %copy.20 = f32[128,2,128,2]{3,2,1,0:T(8,128)} copy(f32[128,2,128,2]{2,0,3,1:T(8,128)S(1)} %pad_maximum_fusion) | data formatting | bytes 524288 | tf_op jit(solution)/shard_map/stack | solution.py:129
  23.8 12.8 %reshape.577 = f32[32,8,256,1]{2,1,0,3:T(8,128)S(1)} reshape(f32[128,2,128,2]{3,2,1,0:T(8,128)} %copy.20) | data formatting | bytes 524288 | tf_op jit(solution)/shard_map/kc,fcv->kfv/dot_general | solution.py:132
  36.6 0.0 copy-done.1
  36.6 0.6 add.103.seg_ref
  37.2 2.3 %add_select_fusion = (s32[2048,128]{1,0:T(8,128)}, s32[2048,128]{1,0:T(8,128)}) fusion(s32[1,1,2048,128]{3,2,1,0:T(8,128)S(1)} %copy-done), kind=kLoop, calls=%fused_computation.7 | loop fusion | flops 3145728 | bytes 3145728 | tf_op jit(solution)/shard_map/jit(remainder)/select_n | solution.py:123
  39.5 3.0 %all-to-all-done = bf16[16,64,512]{2,0,1:T(8,128)(2,1)S(1)} async-done(((bf16[16,64,512]{2,0,1:T(8,128)(2,1)}), bf16[16,64,512]{2,0,1:T(8,128)(2,1)S(1)}, u32[]{:S(2)}, u32[]{:S(2)}) %all-to-all-start) | async-done | bytes 1048608 | tf_op jit(solution)/shard_map/all_to_all | solution.py:106
  42.5 0.1 copy.22
  42.6 0.1 fusion.48
  42.7 0.7 fusion
  43.4 0.2 fusion.12
  43.6 1.1 reshape.573.re_ref
  44.6 1.1 reshape.574.im_ref
  45.7 79.0 %shard_map.55 = f32[16,128,256]{2,1,0:T(8,128)} custom-call(s32[2048]{0:T(1024)} %add.103.seg_ref, s32[2048,128]{1,0:T(8,128)} %get-tuple-element.14.du_ref, s32[2048,128]{1,0:T(8,128)} %get-tuple-element.13.dv_ref, f32[2048,128]{1,0:T(8,128)} %reshape.573.re_ref, f32[2048,128]{1,0:T(8,128)} %reshape.574.im_ref), custom_call_target="tpu_custom_call" | custom-call | flops 4294967296 | bytes 6291456 | tf_op jit(solution)/shard_map/pallas_call | solution.py:68
  124.8 1.6 reshape.578
  126.4 1.9 convolution_bitcast_fusion
  128.3 1.5 copy.23
  129.9 14.5 %all-to-all-start.1 = ((f32[512,8,128]{2,1,0:T(8,128)}), f32[512,8,128]{2,1,0:T(8,128)S(1)}, u32[]{:S(2)}, u32[]{:S(2)}) async-start(f32[512,8,128]{2,1,0:T(8,128)} %bitcast.71), calls=%async_computation.1 | async-start | bytes 4194304 | tf_op jit(solution)/shard_map/all_to_all | solution.py:135
  144.4 0.1 multiply_reduce_fusion.3
  144.5 0.1 dynamic_slice.7
  144.6 0.1 dynamic_slice.6
  144.7 0.1 multiply_reduce_fusion.2
  144.8 0.3 fusion.35
  145.0 0.3 fusion.30
  145.3 54.9 %all-to-all-done.1 = f32[512,8,128]{2,1,0:T(8,128)S(1)} async-done(((f32[512,8,128]{2,1,0:T(8,128)}), f32[512,8,128]{2,1,0:T(8,128)S(1)}, u32[]{:S(2)}, u32[]{:S(2)}) %all-to-all-start.1) | async-done | bytes 2097184 | tf_op jit(solution)/shard_map/all_to_all | solution.py:135
  200.3 0.5 reduce_sum.47
  200.8 0.2 convolution_bitcast_fusion.1
  201.0 0.1 subtract_multiply_fusion
  201.1 0.6 pad_maximum_fusion.1
  (15 shorter events, 0.1 us)
Async XLA Ops:
  2.8 39.8 %all-to-all-start = ((bf16[16,64,512]{2,0,1:T(8,128)(2,1)}), bf16[16,64,512]{2,0,1:T(8,128)(2,1)S(1)}, u32[]{:S(2)}, u32[]{:S(2)}) async-start(bf16[16,64,512]{2,0,1:T(8,128)(2,1)} %copy.21), calls=%async_computation | async-start | bytes 2097152 | tf_op jit(solution)/shard_map/all_to_all | solution.py:106
  23.8 12.8 %copy-start.2 = (s32[1,1,2048,1]{2,3,1,0:T(1,128)S(1)}, s32[1,1,2048,1]{2,3,1,0:T(1,128)}, u32[]{:S(2)}) copy-start(s32[1,1,2048,1]{2,3,1,0:T(1,128)} %param.6) | copy-start | bytes 24580
  23.8 12.8 %copy-start.1 = (s32[1,1,2048]{2,1,0:T(1,128)S(1)}, s32[1,1,2048]{2,1,0:T(1,128)}, u32[]{:S(2)}) copy-start(s32[1,1,2048]{2,1,0:T(1,128)} %param.7) | copy-start | bytes 24580
  23.8 13.4 %copy-start = (s32[1,1,2048,128]{3,2,1,0:T(8,128)S(1)}, s32[1,1,2048,128]{3,2,1,0:T(8,128)}, u32[]{:S(2)}) copy-start(s32[1,1,2048,128]{3,2,1,0:T(8,128)} %param.8) | copy-start | bytes 3145732
  129.9 14.6 %copy-start.3 = (bf16[2,8]{1,0:T(2,128)(2,1)S(1)}, bf16[2,8]{1,0:T(2,128)(2,1)}, u32[]{:S(2)}) copy-start(bf16[2,8]{1,0:T(2,128)(2,1)} %param.9) | copy-start | bytes 100
  129.9 70.4 %all-to-all-start.1 = ((f32[512,8,128]{2,1,0:T(8,128)}), f32[512,8,128]{2,1,0:T(8,128)S(1)}, u32[]{:S(2)}, u32[]{:S(2)}) async-start(f32[512,8,128]{2,1,0:T(8,128)} %bitcast.71), calls=%async_computation.1 | async-start | bytes 4194304 | tf_op jit(solution)/shard_map/all_to_all | solution.py:135

commit v9 on v8

--- a/solution.py
+++ b/solution.py
@@ -90,6 +90,18 @@
     return (jnp.cos(angles), jnp.sin(angles))
 
 
+def complex_table(side, row_major, sign):
+    shape = (side, 2, side, 2) if row_major else (2, side, 2, side)
+    axes = (0, 1, 2, 3) if row_major else (1, 0, 3, 2)
+    first = lax.broadcasted_iota(jnp.int32, shape, axes[0])
+    part_in = lax.broadcasted_iota(jnp.int32, shape, axes[1])
+    second = lax.broadcasted_iota(jnp.int32, shape, axes[2])
+    part_out = lax.broadcasted_iota(jnp.int32, shape, axes[3])
+    angles = (first * second % side).astype(jnp.float32) * (2.0 * math.pi / side)
+    cross = jnp.where(part_in == 0, sign, -sign) * jnp.sin(angles)
+    return jnp.where(part_in == part_out, jnp.cos(angles), cross)
+
+
 def taps_transform(taps_row, side):
     index_ids = jnp.arange(side, dtype=jnp.int32)
     tap_ids = jnp.arange(KT, dtype=jnp.int32)
@@ -125,18 +137,13 @@
     delta = grid_blocks(seg_ids, du, dv, re, im, facets)
     side = TS * TILE
     row_count = side // chan_count
-    cosine, sine = dft_tables(side)
-    along_x = jnp.stack(
-        [jnp.stack([cosine, sine], axis=2), jnp.stack([-sine, cosine], axis=2)], axis=1
-    ).reshape(2 * side, 2 * side)
+    along_x = complex_table(side, True, 1.0).reshape(2 * side, 2 * side)
     rows = jnp.einsum("kc,fcv->kfv", along_x, delta.reshape(facets, 2 * side, side), precision=high)
     rows = rows.reshape(chan_count, row_count * 2, facets, side)
     rows = jnp.transpose(rows, (2, 0, 1, 3)).reshape(facets * chan_count * row_count * 2, side)
     rows = lax.all_to_all(rows, ("stn", "chan"), split_axis=0, concat_axis=0, tiled=True)
     mine = jnp.sum(rows.reshape(facets * chan_count, row_count, 2, side), axis=0)
-    along_y = jnp.stack(
-        [jnp.stack([cosine, -sine], axis=1), jnp.stack([sine, cosine], axis=1)], axis=0
-    )
+    along_y = complex_table(side, False, -1.0)
     spectrum = jnp.einsum("rqv,qvsy->rsy", mine, along_y, precision=high)
     first_row = lax.axis_index("chan") * row_count
     u_re, u_im = taps_transform(kernel_taps[0], side)

time: 202 us -> 203 us (level)
  waiting for transfers between devices: 57.9 us -> 79.9 us
  local copies, waits for them, and re-layouts: 29.6 us -> 8.96 us
    all_to_all x1, waiting for transfers between devices: 3.02 us -> 24.4 us  [body(): lax.all_to_all(voltages, 'stn', split_axis=1, concat_axis=0, tiled=True)]
    dot_general x1 -> x0, local copies, waits for them, and re-layouts: 12.8 us -> none  [body(): jnp.einsum('kc,fcv->kfv', along_x, delta.reshape(facets, 2 * side, side),...]
    another operation x1 -> x0, local copies, waits for them, and re-layouts: 8.56 us -> none  [body(): jnp.stack([jnp.stack([cosine, sine], axis=2), jnp.stack([-sine, cosine],...]
  transfers between devices with their start and end apart: 2 -> 2, of which waited for: 2 -> 2; matrix products, arithmetic and copies ran while one was open for 13% -> 2% of each run, Pallas kernels for 0% -> 0%
where the time goes in v9:
time: 203 us
  waiting for transfers between devices  79.9 us (39%)
  Pallas kernels  79.1 us (39%)
  starting transfers between devices  25.7 us (13%)
  local copies, waits for them, and re-layouts  8.96 us (4%)
  matrix products  4.71 us (2%)
  other arithmetic  4.53 us (2%)
    pallas_call x1, Pallas kernels, grid_blocks(): pl.pallas_call(grid_kernel, out_shape=jax.ShapeDtypeStruct((facets, side,...  79.1 us
    all_to_all x1, waiting for transfers between devices, body(): lax.all_to_all(rows, ('stn', 'chan'), split_axis=0, concat_axis=0, tiled=...  55.5 us
    all_to_all x1, waiting for transfers between devices, body(): lax.all_to_all(voltages, 'stn', split_axis=1, concat_axis=0, tiled=True)  24.4 us
    all_to_all x1, starting transfers between devices, body(): lax.all_to_all(rows, ('stn', 'chan'), split_axis=0, concat_axis=0, tiled=...  13.9 us
    all_to_all x1, starting transfers between devices, body(): lax.all_to_all(voltages, 'stn', split_axis=1, concat_axis=0, tiled=True)  11.8 us
  transfers between devices with their start and end apart: 2, of which 2 were waited for; matrix products, arithmetic and copies ran while one was open for 2% of the time, Pallas kernels for 0%

profile of v9, /device:TPU:1, one launch (start us, length us, event | category | flops | bytes accessed | tf_op | source)
XLA Modules:
  0.0 203.0 jit_solution(2674928311780076651)
XLA Ops:
  0.0 2.9 %copy.14 = bf16[16,64,512]{2,0,1:T(8,128)(2,1)} copy(bf16[16,64,512]{2,1,0:T(8,128)(2,1)} %param.5) | data formatting | bytes 2097152 | tf_op args[0]
  2.9 11.8 %all-to-all-start = ((bf16[16,64,512]{2,0,1:T(8,128)(2,1)}), bf16[16,64,512]{2,0,1:T(8,128)(2,1)S(1)}, u32[]{:S(2)}, u32[]{:S(2)}) async-start(bf16[16,64,512]{2,0,1:T(8,128)(2,1)} %copy.14), calls=%async_computation | async-start | bytes 2097152 | tf_op jit(solution)/shard_map/all_to_all | solution.py:118
  14.7 0.1 iota.105
  14.8 0.1 iota.99
  14.9 0.1 iota.102
  15.1 0.1 iota.108
  15.2 0.1 iota.112
  15.3 0.0 copy-done.2
  15.3 0.6 add.71.seg_ref
  16.0 2.3 %add_select_fusion = (s32[2048,128]{1,0:T(8,128)}, s32[2048,128]{1,0:T(8,128)}) fusion(s32[1,1,2048,128]{3,2,1,0:T(8,128)S(1)} %copy-done), kind=kLoop, calls=%fused_computation.7 | loop fusion | flops 3145728 | bytes 3145728 | tf_op jit(solution)/shard_map/jit(remainder)/select_n | solution.py:135
  18.2 24.4 %all-to-all-done = bf16[16,64,512]{2,0,1:T(8,128)(2,1)S(1)} async-done(((bf16[16,64,512]{2,0,1:T(8,128)(2,1)}), bf16[16,64,512]{2,0,1:T(8,128)(2,1)S(1)}, u32[]{:S(2)}, u32[]{:S(2)}) %all-to-all-start) | async-done | bytes 1048608 | tf_op jit(solution)/shard_map/all_to_all | solution.py:118
  42.7 0.1 copy.15
  42.7 0.1 fusion.72
  42.8 0.7 fusion
  43.6 0.2 fusion.12
  43.7 1.0 reshape.473.re_ref
  44.8 1.1 reshape.474.im_ref
  45.8 79.1 %shard_map.55 = f32[16,128,256]{2,1,0:T(8,128)} custom-call(s32[2048]{0:T(1024)} %add.71.seg_ref, s32[2048,128]{1,0:T(8,128)} %get-tuple-element.14.du_ref, s32[2048,128]{1,0:T(8,128)} %get-tuple-element.13.dv_ref, f32[2048,128]{1,0:T(8,128)} %reshape.473.re_ref, f32[2048,128]{1,0:T(8,128)} %reshape.474.im_ref), custom_call_target="tpu_custom_call" | custom-call | flops 4294967296 | bytes 6291456 | tf_op jit(solution)/shard_map/pallas_call | solution.py:68
  124.9 1.6 reshape.478
  126.5 3.0 %convolution_bitcast_fusion = f32[16,32,8,128]{3,2,0,1:T(8,128)S(1)} fusion(f32[16,256,128,1]{2,1,0,3:T(8,128)S(1)} %reshape.478, f32[8]{0:T(128)S(1)} %iota.112, s32[256]{0:T(256)S(1)} %iota.108, s32[32,8]{1,0:T(8,128)S(1)} %iota.105, s32[256]{0:T(256)S(1)} %iota.102, s32[32,8]{1,0:T(8,128)S(1)} %iota.99), kind=kOutput, calls=%fused_computation.6 | convolution fusion | flops 1611726848 | bytes 4198432 | tf_op jit(solution)/shard_map/kc,fcv->kfv/dot_general | solution.py:141
  129.6 1.6 copy.16
  131.1 13.9 %all-to-all-start.1 = ((f32[512,8,128]{2,1,0:T(8,128)}), f32[512,8,128]{2,1,0:T(8,128)S(1)}, u32[]{:S(2)}, u32[]{:S(2)}) async-start(f32[512,8,128]{2,1,0:T(8,128)} %bitcast.61), calls=%async_computation.1 | async-start | bytes 4194304 | tf_op jit(solution)/shard_map/all_to_all | solution.py:144
  145.0 0.0 copy-done.3
  145.0 0.1 multiply_reduce_fusion.3
  145.1 0.1 dynamic_slice.7
  145.2 0.1 dynamic_slice.6
  145.2 0.1 multiply_reduce_fusion.2
  145.3 55.5 %all-to-all-done.1 = f32[512,8,128]{2,1,0:T(8,128)S(1)} async-done(((f32[512,8,128]{2,1,0:T(8,128)}), f32[512,8,128]{2,1,0:T(8,128)S(1)}, u32[]{:S(2)}, u32[]{:S(2)}) %all-to-all-start.1) | async-done | bytes 2097184 | tf_op jit(solution)/shard_map/all_to_all | solution.py:144
  200.8 0.5 reduce_sum.47
  201.4 0.9 convolution_bitcast_fusion.1
  202.3 0.1 subtract_multiply_fusion
  202.4 0.6 pad_maximum_fusion
  (18 shorter events, 0.1 us)
Async XLA Ops:
  0.0 15.3 %copy-start.2 = (s32[1,1,2048,1]{2,3,1,0:T(1,128)S(1)}, s32[1,1,2048,1]{2,3,1,0:T(1,128)}, u32[]{:S(2)}) copy-start(s32[1,1,2048,1]{2,3,1,0:T(1,128)} %param.6) | copy-start | bytes 24580
  0.0 15.3 %copy-start.1 = (s32[1,1,2048]{2,1,0:T(1,128)S(1)}, s32[1,1,2048]{2,1,0:T(1,128)}, u32[]{:S(2)}) copy-start(s32[1,1,2048]{2,1,0:T(1,128)} %param.7) | copy-start | bytes 24580
  0.0 15.9 %copy-start = (s32[1,1,2048,128]{3,2,1,0:T(8,128)S(1)}, s32[1,1,2048,128]{3,2,1,0:T(8,128)}, u32[]{:S(2)}) copy-start(s32[1,1,2048,128]{3,2,1,0:T(8,128)} %param.8) | copy-start | bytes 3145732
  2.9 39.8 %all-to-all-start = ((bf16[16,64,512]{2,0,1:T(8,128)(2,1)}), bf16[16,64,512]{2,0,1:T(8,128)(2,1)S(1)}, u32[]{:S(2)}, u32[]{:S(2)}) async-start(bf16[16,64,512]{2,0,1:T(8,128)(2,1)} %copy.14), calls=%async_computation | async-start | bytes 2097152 | tf_op jit(solution)/shard_map/all_to_all | solution.py:118
  131.1 13.9 %copy-start.3 = (bf16[2,8]{1,0:T(2,128)(2,1)S(1)}, bf16[2,8]{1,0:T(2,128)(2,1)}, u32[]{:S(2)}) copy-start(bf16[2,8]{1,0:T(2,128)(2,1)} %param.9) | copy-start | bytes 100
  131.1 69.7 %all-to-all-start.1 = ((f32[512,8,128]{2,1,0:T(8,128)}), f32[512,8,128]{2,1,0:T(8,128)S(1)}, u32[]{:S(2)}, u32[]{:S(2)}) async-start(f32[512,8,128]{2,1,0:T(8,128)} %bitcast.61), calls=%async_computation.1 | async-start | bytes 4194304 | tf_op jit(solution)/shard_map/all_to_all | solution.py:144

commit v10 on v7

--- a/solution.py
+++ b/solution.py
@@ -24,7 +24,6 @@
     @pl.when(step == 0)
     def _():
         out_ref[...] = jnp.zeros_like(out_ref)
-    cells = lax.broadcasted_iota(jnp.int32, (TILE, VB), 0)
     lines = lax.broadcasted_iota(jnp.int32, (side, VB), 0)
     def one_block(b, carry):
         du = du_ref[pl.ds(b, 1), :]
@@ -34,9 +33,9 @@
         seg = seg_ref[step * CHUNK + b]
         facet = seg // TT
         tile = seg % TT
-        first_u = pl.multiple_of((tile // TS) * TILE, TILE)
+        first_u = (tile // TS) * TILE
         first_v = (tile % TS) * TILE
-        along_u = (cells == du).astype(jnp.float32).astype(jnp.bfloat16)
+        along_u = (lines == du + first_u).astype(jnp.float32).astype(jnp.bfloat16)
         hit_v = lines == (dv + first_v)
         spread = jnp.concatenate(
             [jnp.where(hit_v, re, 0.0), jnp.where(hit_v, im, 0.0)], axis=0
@@ -44,7 +43,7 @@
         tile_sum = lax.dot_general(
             along_u, spread, (((1,), (1,)), ((), ())), preferred_element_type=jnp.float32
         )
-        out_ref[facet, pl.ds(first_u, TILE), :] += tile_sum
+        out_ref[facet] += tile_sum
         return carry
     lax.fori_loop(0, CHUNK, one_block, 0, unroll=8)
 

time: 202 us -> 215 us (1.064)
  Pallas kernels: 79 us -> 92 us
    pallas_call x1, Pallas kernels: 79 us -> 92 us  [grid_blocks(): pl.pallas_call(grid_kernel, out_shape=jax.ShapeDtypeStruct((facets, side,...]
  transfers between devices with their start and end apart: 2 -> 2, of which waited for: 2 -> 2; matrix products, arithmetic and copies ran while one was open for 13% -> 12% of each run, Pallas kernels for 0% -> 0%
where the time goes in v10:
time: 215 us
  Pallas kernels  92 us (43%)
  waiting for transfers between devices  57.9 us (27%)
  local copies, waits for them, and re-layouts  29.6 us (14%)
  starting transfers between devices  26.4 us (12%)
  other arithmetic  5.72 us (3%)
  matrix products  2.83 us (1%)
    pallas_call x1, Pallas kernels, grid_blocks(): pl.pallas_call(grid_kernel, out_shape=jax.ShapeDtypeStruct((facets, side,...  92 us
    all_to_all x1, waiting for transfers between devices, body(): lax.all_to_all(rows, ('stn', 'chan'), split_axis=0, concat_axis=0, tiled=...  54.9 us
    all_to_all x1, starting transfers between devices, body(): lax.all_to_all(rows, ('stn', 'chan'), split_axis=0, concat_axis=0, tiled=...  14.5 us
    dot_general x1, local copies, waits for them, and re-layouts, body(): jnp.einsum('kc,fcv->kfv', along_x, delta.reshape(facets, 2 * side, side),...  12.8 us
    all_to_all x1, starting transfers between devices, body(): lax.all_to_all(voltages, 'stn', split_axis=1, concat_axis=0, tiled=True)  11.8 us
    another operation x1, local copies, waits for them, and re-layouts, body(): jnp.stack([jnp.stack([cosine, sine], axis=2), jnp.stack([-sine, cosine],...  8.56 us
  transfers between devices with their start and end apart: 2, of which 2 were waited for; matrix products, arithmetic and copies ran while one was open for 12% of the time, Pallas kernels for 0%

profile of v10, /device:TPU:1, one launch (start us, length us, event | category | flops | bytes accessed | tf_op | source)
XLA Modules:
  0.0 214.7 jit_solution(13684518470224332480)
XLA Ops:
  0.0 2.8 %copy.21 = bf16[16,64,512]{2,0,1:T(8,128)(2,1)} copy(bf16[16,64,512]{2,1,0:T(8,128)(2,1)} %param.5) | data formatting | bytes 2097152 | tf_op args[0]
  2.8 11.8 %all-to-all-start = ((bf16[16,64,512]{2,0,1:T(8,128)(2,1)}), bf16[16,64,512]{2,0,1:T(8,128)(2,1)S(1)}, u32[]{:S(2)}, u32[]{:S(2)}) async-start(bf16[16,64,512]{2,0,1:T(8,128)(2,1)} %copy.21), calls=%async_computation | async-start | bytes 2097152 | tf_op jit(solution)/shard_map/all_to_all | solution.py:92
  14.6 0.3 fusion.34
  14.9 0.3 fusion.32
  15.2 8.6 %copy.20 = f32[128,2,128,2]{3,2,1,0:T(8,128)} copy(f32[128,2,128,2]{2,0,3,1:T(8,128)S(1)} %pad_maximum_fusion) | data formatting | bytes 524288 | tf_op jit(solution)/shard_map/stack | solution.py:115
  23.8 12.8 %reshape.577 = f32[32,8,256,1]{2,1,0,3:T(8,128)S(1)} reshape(f32[128,2,128,2]{3,2,1,0:T(8,128)} %copy.20) | data formatting | bytes 524288 | tf_op jit(solution)/shard_map/kc,fcv->kfv/dot_general | solution.py:118
  36.6 0.0 copy-done.1
  36.6 0.6 add.103.seg_ref
  37.2 2.3 %add_select_fusion = (s32[2048,128]{1,0:T(8,128)}, s32[2048,128]{1,0:T(8,128)}) fusion(s32[1,1,2048,128]{3,2,1,0:T(8,128)S(1)} %copy-done), kind=kLoop, calls=%fused_computation.7 | loop fusion | flops 3145728 | bytes 3145728 | tf_op jit(solution)/shard_map/jit(remainder)/select_n | solution.py:109
  39.5 3.0 %all-to-all-done = bf16[16,64,512]{2,0,1:T(8,128)(2,1)S(1)} async-done(((bf16[16,64,512]{2,0,1:T(8,128)(2,1)}), bf16[16,64,512]{2,0,1:T(8,128)(2,1)S(1)}, u32[]{:S(2)}, u32[]{:S(2)}) %all-to-all-start) | async-done | bytes 1048608 | tf_op jit(solution)/shard_map/all_to_all | solution.py:92
  42.5 0.1 copy.22
  42.6 0.1 fusion.48
  42.7 0.7 fusion
  43.4 0.2 fusion.12
  43.6 1.1 reshape.573.re_ref
  44.6 1.1 reshape.574.im_ref
  45.7 92.0 %shard_map.55 = f32[16,128,256]{2,1,0:T(8,128)} custom-call(s32[2048]{0:T(1024)} %add.103.seg_ref, s32[2048,128]{1,0:T(8,128)} %get-tuple-element.14.du_ref, s32[2048,128]{1,0:T(8,128)} %get-tuple-element.13.dv_ref, f32[2048,128]{1,0:T(8,128)} %reshape.573.re_ref, f32[2048,128]{1,0:T(8,128)} %reshape.574.im_ref), custom_call_target="tpu_custom_call" | custom-call | flops 4294967296 | bytes 6291456 | tf_op jit(solution)/shard_map/pallas_call | solution.py:55
  137.8 1.6 reshape.578
  139.4 1.9 convolution_bitcast_fusion
  141.3 1.5 copy.23
  142.9 14.5 %all-to-all-start.1 = ((f32[512,8,128]{2,1,0:T(8,128)}), f32[512,8,128]{2,1,0:T(8,128)S(1)}, u32[]{:S(2)}, u32[]{:S(2)}) async-start(f32[512,8,128]{2,1,0:T(8,128)} %bitcast.71), calls=%async_computation.1 | async-start | bytes 4194304 | tf_op jit(solution)/shard_map/all_to_all | solution.py:121
  157.4 0.1 multiply_reduce_fusion.3
  157.5 0.1 dynamic_slice.7
  157.6 0.1 dynamic_slice.6
  157.7 0.1 multiply_reduce_fusion.2
  157.8 0.3 fusion.35
  158.0 0.3 fusion.30
  158.3 54.9 %all-to-all-done.1 = f32[512,8,128]{2,1,0:T(8,128)S(1)} async-done(((f32[512,8,128]{2,1,0:T(8,128)}), f32[512,8,128]{2,1,0:T(8,128)S(1)}, u32[]{:S(2)}, u32[]{:S(2)}) %all-to-all-start.1) | async-done | bytes 2097184 | tf_op jit(solution)/shard_map/all_to_all | solution.py:121
  213.3 0.5 reduce_sum.47
  213.8 0.2 convolution_bitcast_fusion.1
  214.0 0.1 subtract_multiply_fusion
  214.1 0.6 pad_maximum_fusion.1
  (15 shorter events, 0.1 us)
Async XLA Ops:
  2.8 39.8 %all-to-all-start = ((bf16[16,64,512]{2,0,1:T(8,128)(2,1)}), bf16[16,64,512]{2,0,1:T(8,128)(2,1)S(1)}, u32[]{:S(2)}, u32[]{:S(2)}) async-start(bf16[16,64,512]{2,0,1:T(8,128)(2,1)} %copy.21), calls=%async_computation | async-start | bytes 2097152 | tf_op jit(solution)/shard_map/all_to_all | solution.py:92
  23.8 12.8 %copy-start.2 = (s32[1,1,2048,1]{2,3,1,0:T(1,128)S(1)}, s32[1,1,2048,1]{2,3,1,0:T(1,128)}, u32[]{:S(2)}) copy-start(s32[1,1,2048,1]{2,3,1,0:T(1,128)} %param.6) | copy-start | bytes 24580
  23.8 12.8 %copy-start.1 = (s32[1,1,2048]{2,1,0:T(1,128)S(1)}, s32[1,1,2048]{2,1,0:T(1,128)}, u32[]{:S(2)}) copy-start(s32[1,1,2048]{2,1,0:T(1,128)} %param.7) | copy-start | bytes 24580
  23.8 13.4 %copy-start = (s32[1,1,2048,128]{3,2,1,0:T(8,128)S(1)}, s32[1,1,2048,128]{3,2,1,0:T(8,128)}, u32[]{:S(2)}) copy-start(s32[1,1,2048,128]{3,2,1,0:T(8,128)} %param.8) | copy-start | bytes 3145732
  142.9 14.6 %copy-start.3 = (bf16[2,8]{1,0:T(2,128)(2,1)S(1)}, bf16[2,8]{1,0:T(2,128)(2,1)}, u32[]{:S(2)}) copy-start(bf16[2,8]{1,0:T(2,128)(2,1)} %param.9) | copy-start | bytes 100
  142.9 70.4 %all-to-all-start.1 = ((f32[512,8,128]{2,1,0:T(8,128)}), f32[512,8,128]{2,1,0:T(8,128)S(1)}, u32[]{:S(2)}, u32[]{:S(2)}) async-start(f32[512,8,128]{2,1,0:T(8,128)} %bitcast.71), calls=%async_computation.1 | async-start | bytes 4194304 | tf_op jit(solution)/shard_map/all_to_all | solution.py:121

commit v11 on v7

--- a/solution.py
+++ b/solution.py
@@ -17,15 +17,16 @@
 CHUNK = 256
 
 
-def grid_kernel(seg_ref, du_ref, dv_ref, re_ref, im_ref, out_ref):
+def grid_kernel(seg_ref, du_ref, dv_ref, re_ref, im_ref, out_ref, acc_ref):
     step = pl.program_id(0)
     side = TS * TILE
 
     @pl.when(step == 0)
     def _():
-        out_ref[...] = jnp.zeros_like(out_ref)
+        acc_ref[...] = jnp.zeros_like(acc_ref)
+
     cells = lax.broadcasted_iota(jnp.int32, (TILE, VB), 0)
-    lines = lax.broadcasted_iota(jnp.int32, (side, VB), 0)
+
     def one_block(b, carry):
         du = du_ref[pl.ds(b, 1), :]
         dv = dv_ref[pl.ds(b, 1), :]
@@ -35,18 +36,40 @@
         facet = seg // TT
         tile = seg % TT
         first_u = pl.multiple_of((tile // TS) * TILE, TILE)
-        first_v = (tile % TS) * TILE
         along_u = (cells == du).astype(jnp.float32).astype(jnp.bfloat16)
-        hit_v = lines == (dv + first_v)
+        hit_v = cells == dv
         spread = jnp.concatenate(
             [jnp.where(hit_v, re, 0.0), jnp.where(hit_v, im, 0.0)], axis=0
         ).astype(jnp.bfloat16)
         tile_sum = lax.dot_general(
             along_u, spread, (((1,), (1,)), ((), ())), preferred_element_type=jnp.float32
         )
-        out_ref[facet, pl.ds(first_u, TILE), :] += tile_sum
+        acc_ref[facet, tile % TS, pl.ds(first_u, TILE), :] += tile_sum
         return carry
+
     lax.fori_loop(0, CHUNK, one_block, 0, unroll=8)
+
+    @pl.when(step == pl.num_programs(0) - 1)
+    def _():
+        rows = lax.broadcasted_iota(jnp.int32, (2 * TILE, 2 * side), 0)
+        cols = lax.broadcasted_iota(jnp.int32, (2 * TILE, 2 * side), 1)
+        places = [
+            (cols == (rows // TILE) * side + tv * TILE + rows % TILE).astype(jnp.float32).astype(jnp.bfloat16)
+            for tv in range(TS)
+        ]
+
+        def one_facet(f, carry):
+            total = jnp.zeros((side, 2 * side), jnp.float32)
+            for tv in range(TS):
+                part = acc_ref[f, tv]
+                high = part.astype(jnp.bfloat16)
+                low = (part - high.astype(jnp.float32)).astype(jnp.bfloat16)
+                total = total + jnp.dot(high, places[tv], preferred_element_type=jnp.float32)
+                total = total + jnp.dot(low, places[tv], preferred_element_type=jnp.float32)
+            out_ref[f] = total
+            return carry
+
+        lax.fori_loop(0, out_ref.shape[0], one_facet, 0)
 
 
 def grid_blocks(seg_ids, du, dv, re, im, facets):
@@ -61,9 +84,10 @@
             grid=(blocks // CHUNK,),
             in_specs=[row_spec] * 4,
             out_specs=pl.BlockSpec((facets, side, 2 * side), lambda i, seg: (0, 0, 0)),
+            scratch_shapes=[pltpu.VMEM((facets, TS, side, 2 * TILE), jnp.float32)],
         ),
         cost_estimate=pl.CostEstimate(
-            flops=blocks * TILE * VB * 2 * side * 2,
+            flops=blocks * TILE * VB * 2 * TILE * 2,
             bytes_accessed=blocks * VB * 16 + facets * side * 2 * side * 4,
             transcendentals=0,
         ),

time: 202 us -> 180 us (0.89)
  Pallas kernels: 79 us -> 56.7 us
    pallas_call x1, Pallas kernels: 79 us -> 56.7 us  [grid_blocks(): pl.pallas_call(grid_kernel, out_shape=jax.ShapeDtypeStruct((facets, side,...]
  transfers between devices with their start and end apart: 2 -> 2, of which waited for: 2 -> 2; matrix products, arithmetic and copies ran while one was open for 13% -> 14% of each run, Pallas kernels for 0% -> 0%
where the time goes in v11:
time: 180 us; the launch traced here: 179 us
  waiting for transfers between devices  57.9 us (32%)
  Pallas kernels  56.7 us (32%)
  local copies, waits for them, and re-layouts  29.6 us (16%)
  starting transfers between devices  26.4 us (15%)
  other arithmetic  5.72 us (3%)
  matrix products  2.83 us (2%)
    pallas_call x1, Pallas kernels, grid_blocks(): pl.pallas_call(grid_kernel, out_shape=jax.ShapeDtypeStruct((facets, side,...  56.7 us
    all_to_all x1, waiting for transfers between devices, body(): lax.all_to_all(rows, ('stn', 'chan'), split_axis=0, concat_axis=0, tiled=...  54.9 us
    all_to_all x1, starting transfers between devices, body(): lax.all_to_all(rows, ('stn', 'chan'), split_axis=0, concat_axis=0, tiled=...  14.5 us
    dot_general x1, local copies, waits for them, and re-layouts, body(): jnp.einsum('kc,fcv->kfv', along_x, delta.reshape(facets, 2 * side, side),...  12.8 us
    all_to_all x1, starting transfers between devices, body(): lax.all_to_all(voltages, 'stn', split_axis=1, concat_axis=0, tiled=True)  11.8 us
    another operation x1, local copies, waits for them, and re-layouts, body(): jnp.stack([jnp.stack([cosine, sine], axis=2), jnp.stack([-sine, cosine],...  8.56 us
  transfers between devices with their start and end apart: 2, of which 2 were waited for; matrix products, arithmetic and copies ran while one was open for 14% of the time, Pallas kernels for 0%

profile of v11, /device:TPU:1, one launch (start us, length us, event | category | flops | bytes accessed | tf_op | source)
XLA Modules:
  0.0 179.4 jit_solution(3619067167880142858)
XLA Ops:
  0.0 2.8 %copy.21 = bf16[16,64,512]{2,0,1:T(8,128)(2,1)} copy(bf16[16,64,512]{2,1,0:T(8,128)(2,1)} %param.5) | data formatting | bytes 2097152 | tf_op args[0]
  2.8 11.8 %all-to-all-start = ((bf16[16,64,512]{2,0,1:T(8,128)(2,1)}), bf16[16,64,512]{2,0,1:T(8,128)(2,1)S(1)}, u32[]{:S(2)}, u32[]{:S(2)}) async-start(bf16[16,64,512]{2,0,1:T(8,128)(2,1)} %copy.21), calls=%async_computation | async-start | bytes 2097152 | tf_op jit(solution)/shard_map/all_to_all | solution.py:117
  14.6 0.3 fusion.34
  14.9 0.3 fusion.32
  15.2 8.6 %copy.20 = f32[128,2,128,2]{3,2,1,0:T(8,128)} copy(f32[128,2,128,2]{2,0,3,1:T(8,128)S(1)} %pad_maximum_fusion) | data formatting | bytes 524288 | tf_op jit(solution)/shard_map/stack | solution.py:140
  23.8 12.8 %reshape.577 = f32[32,8,256,1]{2,1,0,3:T(8,128)S(1)} reshape(f32[128,2,128,2]{3,2,1,0:T(8,128)} %copy.20) | data formatting | bytes 524288 | tf_op jit(solution)/shard_map/kc,fcv->kfv/dot_general | solution.py:143
  36.6 0.0 copy-done.1
  36.6 0.6 add.103.seg_ref
  37.2 2.3 %add_select_fusion = (s32[2048,128]{1,0:T(8,128)}, s32[2048,128]{1,0:T(8,128)}) fusion(s32[1,1,2048,128]{3,2,1,0:T(8,128)S(1)} %copy-done), kind=kLoop, calls=%fused_computation.7 | loop fusion | flops 3145728 | bytes 3145728 | tf_op jit(solution)/shard_map/jit(remainder)/select_n | solution.py:134
  39.5 3.0 %all-to-all-done = bf16[16,64,512]{2,0,1:T(8,128)(2,1)S(1)} async-done(((bf16[16,64,512]{2,0,1:T(8,128)(2,1)}), bf16[16,64,512]{2,0,1:T(8,128)(2,1)S(1)}, u32[]{:S(2)}, u32[]{:S(2)}) %all-to-all-start) | async-done | bytes 1048608 | tf_op jit(solution)/shard_map/all_to_all | solution.py:117
  42.5 0.1 copy.22
  42.6 0.1 fusion.48
  42.7 0.7 fusion
  43.4 0.2 fusion.12
  43.6 1.1 reshape.573.re_ref
  44.6 1.1 reshape.574.im_ref
  45.7 56.7 %shard_map.55 = f32[16,128,256]{2,1,0:T(8,128)} custom-call(s32[2048]{0:T(1024)} %add.103.seg_ref, s32[2048,128]{1,0:T(8,128)} %get-tuple-element.14.du_ref, s32[2048,128]{1,0:T(8,128)} %get-tuple-element.13.dv_ref, f32[2048,128]{1,0:T(8,128)} %reshape.573.re_ref, f32[2048,128]{1,0:T(8,128)} %reshape.574.im_ref), custom_call_target="tpu_custom_call" | custom-call | flops 1073741824 | bytes 6291456 | tf_op jit(solution)/shard_map/pallas_call | solution.py:79
  102.4 1.6 reshape.578
  104.1 1.9 %convolution_bitcast_fusion = f32[16,32,8,128]{3,2,0,1:T(8,128)S(1)} fusion(f32[16,256,128,1]{2,1,0,3:T(8,128)S(1)} %reshape.578, f32[32,8,256,1]{2,1,0,3:T(8,128)S(1)} %reshape.577), kind=kOutput, calls=%fused_computation.6 | convolution fusion | flops 1610612736 | bytes 4456448 | tf_op jit(solution)/shard_map/kc,fcv->kfv/dot_general | solution.py:143
  106.0 1.5 copy.23
  107.5 14.5 %all-to-all-start.1 = ((f32[512,8,128]{2,1,0:T(8,128)}), f32[512,8,128]{2,1,0:T(8,128)S(1)}, u32[]{:S(2)}, u32[]{:S(2)}) async-start(f32[512,8,128]{2,1,0:T(8,128)} %bitcast.71), calls=%async_computation.1 | async-start | bytes 4194304 | tf_op jit(solution)/shard_map/all_to_all | solution.py:146
  122.1 0.1 multiply_reduce_fusion.3
  122.2 0.1 dynamic_slice.7
  122.3 0.1 dynamic_slice.6
  122.3 0.1 multiply_reduce_fusion.2
  122.4 0.3 fusion.35
  122.7 0.3 fusion.30
  123.0 54.9 %all-to-all-done.1 = f32[512,8,128]{2,1,0:T(8,128)S(1)} async-done(((f32[512,8,128]{2,1,0:T(8,128)}), f32[512,8,128]{2,1,0:T(8,128)S(1)}, u32[]{:S(2)}, u32[]{:S(2)}) %all-to-all-start.1) | async-done | bytes 2097184 | tf_op jit(solution)/shard_map/all_to_all | solution.py:146
  177.9 0.5 reduce_sum.47
  178.5 0.2 convolution_bitcast_fusion.1
  178.7 0.1 subtract_multiply_fusion
  178.8 0.6 pad_maximum_fusion.1
  (15 shorter events, 0.1 us)
Async XLA Ops:
  2.8 39.8 %all-to-all-start = ((bf16[16,64,512]{2,0,1:T(8,128)(2,1)}), bf16[16,64,512]{2,0,1:T(8,128)(2,1)S(1)}, u32[]{:S(2)}, u32[]{:S(2)}) async-start(bf16[16,64,512]{2,0,1:T(8,128)(2,1)} %copy.21), calls=%async_computation | async-start | bytes 2097152 | tf_op jit(solution)/shard_map/all_to_all | solution.py:117
  23.8 12.8 %copy-start.2 = (s32[1,1,2048,1]{2,3,1,0:T(1,128)S(1)}, s32[1,1,2048,1]{2,3,1,0:T(1,128)}, u32[]{:S(2)}) copy-start(s32[1,1,2048,1]{2,3,1,0:T(1,128)} %param.6) | copy-start | bytes 24580
  23.8 12.8 %copy-start.1 = (s32[1,1,2048]{2,1,0:T(1,128)S(1)}, s32[1,1,2048]{2,1,0:T(1,128)}, u32[]{:S(2)}) copy-start(s32[1,1,2048]{2,1,0:T(1,128)} %param.7) | copy-start | bytes 24580
  23.8 13.4 %copy-start = (s32[1,1,2048,128]{3,2,1,0:T(8,128)S(1)}, s32[1,1,2048,128]{3,2,1,0:T(8,128)}, u32[]{:S(2)}) copy-start(s32[1,1,2048,128]{3,2,1,0:T(8,128)} %param.8) | copy-start | bytes 3145732
  107.5 14.6 %copy-start.3 = (bf16[2,8]{1,0:T(2,128)(2,1)S(1)}, bf16[2,8]{1,0:T(2,128)(2,1)}, u32[]{:S(2)}) copy-start(bf16[2,8]{1,0:T(2,128)(2,1)} %param.9) | copy-start | bytes 100
  107.5 70.4 %all-to-all-start.1 = ((f32[512,8,128]{2,1,0:T(8,128)}), f32[512,8,128]{2,1,0:T(8,128)S(1)}, u32[]{:S(2)}, u32[]{:S(2)}) async-start(f32[512,8,128]{2,1,0:T(8,128)} %bitcast.71), calls=%async_computation.1 | async-start | bytes 4194304 | tf_op jit(solution)/shard_map/all_to_all | solution.py:146

commit v12 on v11

--- a/solution.py
+++ b/solution.py
@@ -14,7 +14,7 @@
 TS = 4
 TT = 16
 OFFS = 25
-CHUNK = 256
+CHUNK = 512
 
 
 def grid_kernel(seg_ref, du_ref, dv_ref, re_ref, im_ref, out_ref, acc_ref):
@@ -47,7 +47,7 @@
         acc_ref[facet, tile % TS, pl.ds(first_u, TILE), :] += tile_sum
         return carry
 
-    lax.fori_loop(0, CHUNK, one_block, 0, unroll=8)
+    lax.fori_loop(0, CHUNK, one_block, 0, unroll=16)
 
     @pl.when(step == pl.num_programs(0) - 1)
     def _():

time: 180 us -> 169 us (0.939)
  Pallas kernels: 56.7 us -> 45.9 us
    pallas_call x1, Pallas kernels: 56.7 us -> 45.9 us  [grid_blocks(): pl.pallas_call(grid_kernel, out_shape=jax.ShapeDtypeStruct((facets, side,...]
  transfers between devices with their start and end apart: 2 -> 2, of which waited for: 2 -> 2; matrix products, arithmetic and copies ran while one was open for 14% -> 15% of each run, Pallas kernels for 0% -> 0%
where the time goes in v12:
time: 169 us
  waiting for transfers between devices  57.9 us (34%)
  Pallas kernels  45.9 us (27%)
  local copies, waits for them, and re-layouts  29.6 us (18%)
  starting transfers between devices  26.4 us (16%)
  other arithmetic  5.72 us (3%)
  matrix products  2.83 us (2%)
    all_to_all x1, waiting for transfers between devices, body(): lax.all_to_all(rows, ('stn', 'chan'), split_axis=0, concat_axis=0, tiled=...  54.9 us
    pallas_call x1, Pallas kernels, grid_blocks(): pl.pallas_call(grid_kernel, out_shape=jax.ShapeDtypeStruct((facets, side,...  45.9 us
    all_to_all x1, starting transfers between devices, body(): lax.all_to_all(rows, ('stn', 'chan'), split_axis=0, concat_axis=0, tiled=...  14.6 us
    dot_general x1, local copies, waits for them, and re-layouts, body(): jnp.einsum('kc,fcv->kfv', along_x, delta.reshape(facets, 2 * side, side),...  12.8 us
    all_to_all x1, starting transfers between devices, body(): lax.all_to_all(voltages, 'stn', split_axis=1, concat_axis=0, tiled=True)  11.8 us
    another operation x1, local copies, waits for them, and re-layouts, body(): jnp.stack([jnp.stack([cosine, sine], axis=2), jnp.stack([-sine, cosine],...  8.56 us
  transfers between devices with their start and end apart: 2, of which 2 were waited for; matrix products, arithmetic and copies ran while one was open for 15% of the time, Pallas kernels for 0%

profile of v12, /device:TPU:1, one launch (start us, length us, event | category | flops | bytes accessed | tf_op | source)
XLA Modules:
  0.0 168.5 jit_solution(14582643127872247303)
XLA Ops:
  0.0 2.8 %copy.21 = bf16[16,64,512]{2,0,1:T(8,128)(2,1)} copy(bf16[16,64,512]{2,1,0:T(8,128)(2,1)} %param.5) | data formatting | bytes 2097152 | tf_op args[0]
  2.8 11.8 %all-to-all-start = ((bf16[16,64,512]{2,0,1:T(8,128)(2,1)}), bf16[16,64,512]{2,0,1:T(8,128)(2,1)S(1)}, u32[]{:S(2)}, u32[]{:S(2)}) async-start(bf16[16,64,512]{2,0,1:T(8,128)(2,1)} %copy.21), calls=%async_computation | async-start | bytes 2097152 | tf_op jit(solution)/shard_map/all_to_all | solution.py:117
  14.6 0.3 fusion.34
  14.9 0.3 fusion.32
  15.2 8.6 %copy.20 = f32[128,2,128,2]{3,2,1,0:T(8,128)} copy(f32[128,2,128,2]{2,0,3,1:T(8,128)S(1)} %pad_maximum_fusion) | data formatting | bytes 524288 | tf_op jit(solution)/shard_map/stack | solution.py:140
  23.8 12.8 %reshape.577 = f32[32,8,256,1]{2,1,0,3:T(8,128)S(1)} reshape(f32[128,2,128,2]{3,2,1,0:T(8,128)} %copy.20) | data formatting | bytes 524288 | tf_op jit(solution)/shard_map/kc,fcv->kfv/dot_general | solution.py:143
  36.6 0.0 copy-done.1
  36.6 0.6 add.103.seg_ref
  37.2 2.3 %add_select_fusion = (s32[2048,128]{1,0:T(8,128)}, s32[2048,128]{1,0:T(8,128)}) fusion(s32[1,1,2048,128]{3,2,1,0:T(8,128)S(1)} %copy-done), kind=kLoop, calls=%fused_computation.7 | loop fusion | flops 3145728 | bytes 3145728 | tf_op jit(solution)/shard_map/jit(remainder)/select_n | solution.py:134
  39.5 3.0 %all-to-all-done = bf16[16,64,512]{2,0,1:T(8,128)(2,1)S(1)} async-done(((bf16[16,64,512]{2,0,1:T(8,128)(2,1)}), bf16[16,64,512]{2,0,1:T(8,128)(2,1)S(1)}, u32[]{:S(2)}, u32[]{:S(2)}) %all-to-all-start) | async-done | bytes 1048608 | tf_op jit(solution)/shard_map/all_to_all | solution.py:117
  42.5 0.1 copy.22
  42.6 0.1 fusion.48
  42.7 0.7 fusion
  43.4 0.2 fusion.12
  43.6 1.1 reshape.573.re_ref
  44.6 1.1 reshape.574.im_ref
  45.7 45.9 %shard_map.55 = f32[16,128,256]{2,1,0:T(8,128)} custom-call(s32[2048]{0:T(1024)} %add.103.seg_ref, s32[2048,128]{1,0:T(8,128)} %get-tuple-element.14.du_ref, s32[2048,128]{1,0:T(8,128)} %get-tuple-element.13.dv_ref, f32[2048,128]{1,0:T(8,128)} %reshape.573.re_ref, f32[2048,128]{1,0:T(8,128)} %reshape.574.im_ref), custom_call_target="tpu_custom_call" | custom-call | flops 1073741824 | bytes 6291456 | tf_op jit(solution)/shard_map/pallas_call | solution.py:79
  91.6 1.6 reshape.578
  93.2 1.9 %convolution_bitcast_fusion = f32[16,32,8,128]{3,2,0,1:T(8,128)S(1)} fusion(f32[16,256,128,1]{2,1,0,3:T(8,128)S(1)} %reshape.578, f32[32,8,256,1]{2,1,0,3:T(8,128)S(1)} %reshape.577), kind=kOutput, calls=%fused_computation.6 | convolution fusion | flops 1610612736 | bytes 4456448 | tf_op jit(solution)/shard_map/kc,fcv->kfv/dot_general | solution.py:143
  95.1 1.5 copy.23
  96.7 14.6 %all-to-all-start.1 = ((f32[512,8,128]{2,1,0:T(8,128)}), f32[512,8,128]{2,1,0:T(8,128)S(1)}, u32[]{:S(2)}, u32[]{:S(2)}) async-start(f32[512,8,128]{2,1,0:T(8,128)} %bitcast.71), calls=%async_computation.1 | async-start | bytes 4194304 | tf_op jit(solution)/shard_map/all_to_all | solution.py:146
  111.3 0.1 multiply_reduce_fusion.3
  111.3 0.1 dynamic_slice.7
  111.4 0.1 dynamic_slice.6
  111.5 0.1 multiply_reduce_fusion.2
  111.6 0.3 fusion.35
  111.9 0.3 fusion.30
  112.2 54.9 %all-to-all-done.1 = f32[512,8,128]{2,1,0:T(8,128)S(1)} async-done(((f32[512,8,128]{2,1,0:T(8,128)}), f32[512,8,128]{2,1,0:T(8,128)S(1)}, u32[]{:S(2)}, u32[]{:S(2)}) %all-to-all-start.1) | async-done | bytes 2097184 | tf_op jit(solution)/shard_map/all_to_all | solution.py:146
  167.1 0.5 reduce_sum.47
  167.6 0.2 convolution_bitcast_fusion.1
  167.8 0.1 subtract_multiply_fusion
  167.9 0.6 pad_maximum_fusion.1
  (15 shorter events, 0.1 us)
Async XLA Ops:
  2.8 39.8 %all-to-all-start = ((bf16[16,64,512]{2,0,1:T(8,128)(2,1)}), bf16[16,64,512]{2,0,1:T(8,128)(2,1)S(1)}, u32[]{:S(2)}, u32[]{:S(2)}) async-start(bf16[16,64,512]{2,0,1:T(8,128)(2,1)} %copy.21), calls=%async_computation | async-start | bytes 2097152 | tf_op jit(solution)/shard_map/all_to_all | solution.py:117
  23.8 12.8 %copy-start.2 = (s32[1,1,2048,1]{2,3,1,0:T(1,128)S(1)}, s32[1,1,2048,1]{2,3,1,0:T(1,128)}, u32[]{:S(2)}) copy-start(s32[1,1,2048,1]{2,3,1,0:T(1,128)} %param.6) | copy-start | bytes 24580
  23.8 12.8 %copy-start.1 = (s32[1,1,2048]{2,1,0:T(1,128)S(1)}, s32[1,1,2048]{2,1,0:T(1,128)}, u32[]{:S(2)}) copy-start(s32[1,1,2048]{2,1,0:T(1,128)} %param.7) | copy-start | bytes 24580
  23.8 13.4 %copy-start = (s32[1,1,2048,128]{3,2,1,0:T(8,128)S(1)}, s32[1,1,2048,128]{3,2,1,0:T(8,128)}, u32[]{:S(2)}) copy-start(s32[1,1,2048,128]{3,2,1,0:T(8,128)} %param.8) | copy-start | bytes 3145732
  96.7 14.6 %copy-start.3 = (bf16[2,8]{1,0:T(2,128)(2,1)S(1)}, bf16[2,8]{1,0:T(2,128)(2,1)}, u32[]{:S(2)}) copy-start(bf16[2,8]{1,0:T(2,128)(2,1)} %param.9) | copy-start | bytes 100
  96.7 70.4 %all-to-all-start.1 = ((f32[512,8,128]{2,1,0:T(8,128)}), f32[512,8,128]{2,1,0:T(8,128)S(1)}, u32[]{:S(2)}, u32[]{:S(2)}) async-start(f32[512,8,128]{2,1,0:T(8,128)} %bitcast.71), calls=%async_computation.1 | async-start | bytes 4194304 | tf_op jit(solution)/shard_map/all_to_all | solution.py:146

commit v13 on v12

--- a/solution.py
+++ b/solution.py
@@ -14,7 +14,7 @@
 TS = 4
 TT = 16
 OFFS = 25
-CHUNK = 512
+CHUNK = 1024
 
 
 def grid_kernel(seg_ref, du_ref, dv_ref, re_ref, im_ref, out_ref, acc_ref):
@@ -47,7 +47,7 @@
         acc_ref[facet, tile % TS, pl.ds(first_u, TILE), :] += tile_sum
         return carry
 
-    lax.fori_loop(0, CHUNK, one_block, 0, unroll=16)
+    lax.fori_loop(0, CHUNK, one_block, 0, unroll=32)
 
     @pl.when(step == pl.num_programs(0) - 1)
     def _():

time: 169 us -> 166 us (0.982)
  Pallas kernels: 45.9 us -> 42.8 us
    pallas_call x1, Pallas kernels: 45.9 us -> 42.8 us  [grid_blocks(): pl.pallas_call(grid_kernel, out_shape=jax.ShapeDtypeStruct((facets, side,...]
  transfers between devices with their start and end apart: 2 -> 2, of which waited for: 2 -> 2; matrix products, arithmetic and copies ran while one was open for 15% -> 16% of each run, Pallas kernels for 0% -> 0%
where the time goes in v13:
time: 166 us; the launch traced here: 165 us
  waiting for transfers between devices  57.9 us (35%)
  Pallas kernels  42.8 us (26%)
  local copies, waits for them, and re-layouts  29.6 us (18%)
  starting transfers between devices  26.4 us (16%)
  other arithmetic  5.72 us (3%)
  matrix products  2.83 us (2%)
    all_to_all x1, waiting for transfers between devices, body(): lax.all_to_all(rows, ('stn', 'chan'), split_axis=0, concat_axis=0, tiled=...  54.9 us
    pallas_call x1, Pallas kernels, grid_blocks(): pl.pallas_call(grid_kernel, out_shape=jax.ShapeDtypeStruct((facets, side,...  42.8 us
    all_to_all x1, starting transfers between devices, body(): lax.all_to_all(rows, ('stn', 'chan'), split_axis=0, concat_axis=0, tiled=...  14.6 us
    dot_general x1, local copies, waits for them, and re-layouts, body(): jnp.einsum('kc,fcv->kfv', along_x, delta.reshape(facets, 2 * side, side),...  12.8 us
    all_to_all x1, starting transfers between devices, body(): lax.all_to_all(voltages, 'stn', split_axis=1, concat_axis=0, tiled=True)  11.8 us
    another operation x1, local copies, waits for them, and re-layouts, body(): jnp.stack([jnp.stack([cosine, sine], axis=2), jnp.stack([-sine, cosine],...  8.56 us
  transfers between devices with their start and end apart: 2, of which 2 were waited for; matrix products, arithmetic and copies ran while one was open for 16% of the time, Pallas kernels for 0%

profile of v13, /device:TPU:1, one launch (start us, length us, event | category | flops | bytes accessed | tf_op | source)
XLA Modules:
  0.0 165.5 jit_solution(6284890106545386022)
XLA Ops:
  0.0 2.8 %copy.21 = bf16[16,64,512]{2,0,1:T(8,128)(2,1)} copy(bf16[16,64,512]{2,1,0:T(8,128)(2,1)} %param.5) | data formatting | bytes 2097152 | tf_op args[0]
  2.8 11.8 %all-to-all-start = ((bf16[16,64,512]{2,0,1:T(8,128)(2,1)}), bf16[16,64,512]{2,0,1:T(8,128)(2,1)S(1)}, u32[]{:S(2)}, u32[]{:S(2)}) async-start(bf16[16,64,512]{2,0,1:T(8,128)(2,1)} %copy.21), calls=%async_computation | async-start | bytes 2097152 | tf_op jit(solution)/shard_map/all_to_all | solution.py:117
  14.6 0.3 fusion.34
  14.9 0.3 fusion.32
  15.2 8.6 %copy.20 = f32[128,2,128,2]{3,2,1,0:T(8,128)} copy(f32[128,2,128,2]{2,0,3,1:T(8,128)S(1)} %pad_maximum_fusion) | data formatting | bytes 524288 | tf_op jit(solution)/shard_map/stack | solution.py:140
  23.8 12.8 %reshape.577 = f32[32,8,256,1]{2,1,0,3:T(8,128)S(1)} reshape(f32[128,2,128,2]{3,2,1,0:T(8,128)} %copy.20) | data formatting | bytes 524288 | tf_op jit(solution)/shard_map/kc,fcv->kfv/dot_general | solution.py:143
  36.6 0.0 copy-done.1
  36.6 0.6 add.103.seg_ref
  37.2 2.3 %add_select_fusion = (s32[2048,128]{1,0:T(8,128)}, s32[2048,128]{1,0:T(8,128)}) fusion(s32[1,1,2048,128]{3,2,1,0:T(8,128)S(1)} %copy-done), kind=kLoop, calls=%fused_computation.7 | loop fusion | flops 3145728 | bytes 3145728 | tf_op jit(solution)/shard_map/jit(remainder)/select_n | solution.py:134
  39.5 3.0 %all-to-all-done = bf16[16,64,512]{2,0,1:T(8,128)(2,1)S(1)} async-done(((bf16[16,64,512]{2,0,1:T(8,128)(2,1)}), bf16[16,64,512]{2,0,1:T(8,128)(2,1)S(1)}, u32[]{:S(2)}, u32[]{:S(2)}) %all-to-all-start) | async-done | bytes 1048608 | tf_op jit(solution)/shard_map/all_to_all | solution.py:117
  42.5 0.1 copy.22
  42.6 0.1 fusion.48
  42.7 0.7 fusion
  43.4 0.2 fusion.12
  43.6 1.1 reshape.573.re_ref
  44.6 1.1 reshape.574.im_ref
  45.7 42.8 %shard_map.55 = f32[16,128,256]{2,1,0:T(8,128)} custom-call(s32[2048]{0:T(1024)} %add.103.seg_ref, s32[2048,128]{1,0:T(8,128)} %get-tuple-element.14.du_ref, s32[2048,128]{1,0:T(8,128)} %get-tuple-element.13.dv_ref, f32[2048,128]{1,0:T(8,128)} %reshape.573.re_ref, f32[2048,128]{1,0:T(8,128)} %reshape.574.im_ref), custom_call_target="tpu_custom_call" | custom-call | flops 1073741824 | bytes 6291456 | tf_op jit(solution)/shard_map/pallas_call | solution.py:79
  88.5 1.6 reshape.578
  90.2 1.9 %convolution_bitcast_fusion = f32[16,32,8,128]{3,2,0,1:T(8,128)S(1)} fusion(f32[16,256,128,1]{2,1,0,3:T(8,128)S(1)} %reshape.578, f32[32,8,256,1]{2,1,0,3:T(8,128)S(1)} %reshape.577), kind=kOutput, calls=%fused_computation.6 | convolution fusion | flops 1610612736 | bytes 4456448 | tf_op jit(solution)/shard_map/kc,fcv->kfv/dot_general | solution.py:143
  92.1 1.5 copy.23
  93.6 14.6 %all-to-all-start.1 = ((f32[512,8,128]{2,1,0:T(8,128)}), f32[512,8,128]{2,1,0:T(8,128)S(1)}, u32[]{:S(2)}, u32[]{:S(2)}) async-start(f32[512,8,128]{2,1,0:T(8,128)} %bitcast.71), calls=%async_computation.1 | async-start | bytes 4194304 | tf_op jit(solution)/shard_map/all_to_all | solution.py:146
  108.2 0.1 multiply_reduce_fusion.3
  108.3 0.1 dynamic_slice.7
  108.4 0.1 dynamic_slice.6
  108.5 0.1 multiply_reduce_fusion.2
  108.5 0.3 fusion.35
  108.8 0.3 fusion.30
  109.1 54.9 %all-to-all-done.1 = f32[512,8,128]{2,1,0:T(8,128)S(1)} async-done(((f32[512,8,128]{2,1,0:T(8,128)}), f32[512,8,128]{2,1,0:T(8,128)S(1)}, u32[]{:S(2)}, u32[]{:S(2)}) %all-to-all-start.1) | async-done | bytes 2097184 | tf_op jit(solution)/shard_map/all_to_all | solution.py:146
  164.0 0.5 reduce_sum.47
  164.6 0.2 convolution_bitcast_fusion.1
  164.8 0.1 subtract_multiply_fusion
  164.9 0.6 pad_maximum_fusion.1
  (15 shorter events, 0.1 us)
Async XLA Ops:
  2.8 39.8 %all-to-all-start = ((bf16[16,64,512]{2,0,1:T(8,128)(2,1)}), bf16[16,64,512]{2,0,1:T(8,128)(2,1)S(1)}, u32[]{:S(2)}, u32[]{:S(2)}) async-start(bf16[16,64,512]{2,0,1:T(8,128)(2,1)} %copy.21), calls=%async_computation | async-start | bytes 2097152 | tf_op jit(solution)/shard_map/all_to_all | solution.py:117
  23.8 12.8 %copy-start.2 = (s32[1,1,2048,1]{2,3,1,0:T(1,128)S(1)}, s32[1,1,2048,1]{2,3,1,0:T(1,128)}, u32[]{:S(2)}) copy-start(s32[1,1,2048,1]{2,3,1,0:T(1,128)} %param.6) | copy-start | bytes 24580
  23.8 12.8 %copy-start.1 = (s32[1,1,2048]{2,1,0:T(1,128)S(1)}, s32[1,1,2048]{2,1,0:T(1,128)}, u32[]{:S(2)}) copy-start(s32[1,1,2048]{2,1,0:T(1,128)} %param.7) | copy-start | bytes 24580
  23.8 13.4 %copy-start = (s32[1,1,2048,128]{3,2,1,0:T(8,128)S(1)}, s32[1,1,2048,128]{3,2,1,0:T(8,128)}, u32[]{:S(2)}) copy-start(s32[1,1,2048,128]{3,2,1,0:T(8,128)} %param.8) | copy-start | bytes 3145732
  93.6 14.6 %copy-start.3 = (bf16[2,8]{1,0:T(2,128)(2,1)S(1)}, bf16[2,8]{1,0:T(2,128)(2,1)}, u32[]{:S(2)}) copy-start(bf16[2,8]{1,0:T(2,128)(2,1)} %param.9) | copy-start | bytes 100
  93.6 70.4 %all-to-all-start.1 = ((f32[512,8,128]{2,1,0:T(8,128)}), f32[512,8,128]{2,1,0:T(8,128)S(1)}, u32[]{:S(2)}, u32[]{:S(2)}) async-start(f32[512,8,128]{2,1,0:T(8,128)} %bitcast.71), calls=%async_computation.1 | async-start | bytes 4194304 | tf_op jit(solution)/shard_map/all_to_all | solution.py:146

commit v14 on v13

--- a/solution.py
+++ b/solution.py
@@ -14,7 +14,7 @@
 TS = 4
 TT = 16
 OFFS = 25
-CHUNK = 1024
+CHUNK = 2048
 
 
 def grid_kernel(seg_ref, du_ref, dv_ref, re_ref, im_ref, out_ref, acc_ref):
@@ -47,7 +47,7 @@
         acc_ref[facet, tile % TS, pl.ds(first_u, TILE), :] += tile_sum
         return carry
 
-    lax.fori_loop(0, CHUNK, one_block, 0, unroll=32)
+    lax.fori_loop(0, CHUNK, one_block, 0, unroll=64)
 
     @pl.when(step == pl.num_programs(0) - 1)
     def _():

time: 166 us -> 161 us (0.970)
  Pallas kernels: 42.8 us -> 37.6 us
    pallas_call x1, Pallas kernels: 42.8 us -> 37.6 us  [grid_blocks(): pl.pallas_call(grid_kernel, out_shape=jax.ShapeDtypeStruct((facets, side,...]
where the time goes in v14:
time: 161 us; the launch traced here: 160 us
  waiting for transfers between devices  57.9 us (36%)
  Pallas kernels  37.6 us (23%)
  local copies, waits for them, and re-layouts  29.6 us (18%)
  starting transfers between devices  26.4 us (16%)
  other arithmetic  5.72 us (4%)
  matrix products  2.83 us (2%)
    all_to_all x1, waiting for transfers between devices, body(): lax.all_to_all(rows, ('stn', 'chan'), split_axis=0, concat_axis=0, tiled=...  54.9 us
    pallas_call x1, Pallas kernels, grid_blocks(): pl.pallas_call(grid_kernel, out_shape=jax.ShapeDtypeStruct((facets, side,...  37.6 us
    all_to_all x1, starting transfers between devices, body(): lax.all_to_all(rows, ('stn', 'chan'), split_axis=0, concat_axis=0, tiled=...  14.6 us
    dot_general x1, local copies, waits for them, and re-layouts, body(): jnp.einsum('kc,fcv->kfv', along_x, delta.reshape(facets, 2 * side, side),...  12.8 us
    all_to_all x1, starting transfers between devices, body(): lax.all_to_all(voltages, 'stn', split_axis=1, concat_axis=0, tiled=True)  11.8 us
    another operation x1, local copies, waits for them, and re-layouts, body(): jnp.stack([jnp.stack([cosine, sine], axis=2), jnp.stack([-sine, cosine],...  8.56 us
  transfers between devices with their start and end apart: 2, of which 2 were waited for; matrix products, arithmetic and copies ran while one was open for 16% of the time, Pallas kernels for 0%

profile of v14, /device:TPU:1, one launch (start us, length us, event | category | flops | bytes accessed | tf_op | source)
XLA Modules:
  0.0 160.3 jit_solution(591039836971869849)
XLA Ops:
  0.0 2.8 %copy.21 = bf16[16,64,512]{2,0,1:T(8,128)(2,1)} copy(bf16[16,64,512]{2,1,0:T(8,128)(2,1)} %param.5) | data formatting | bytes 2097152 | tf_op args[0]
  2.8 11.8 %all-to-all-start = ((bf16[16,64,512]{2,0,1:T(8,128)(2,1)}), bf16[16,64,512]{2,0,1:T(8,128)(2,1)S(1)}, u32[]{:S(2)}, u32[]{:S(2)}) async-start(bf16[16,64,512]{2,0,1:T(8,128)(2,1)} %copy.21), calls=%async_computation | async-start | bytes 2097152 | tf_op jit(solution)/shard_map/all_to_all | solution.py:117
  14.6 0.3 fusion.34
  14.9 0.3 fusion.32
  15.2 8.6 %copy.20 = f32[128,2,128,2]{3,2,1,0:T(8,128)} copy(f32[128,2,128,2]{2,0,3,1:T(8,128)S(1)} %pad_maximum_fusion) | data formatting | bytes 524288 | tf_op jit(solution)/shard_map/stack | solution.py:140
  23.8 12.8 %reshape.577 = f32[32,8,256,1]{2,1,0,3:T(8,128)S(1)} reshape(f32[128,2,128,2]{3,2,1,0:T(8,128)} %copy.20) | data formatting | bytes 524288 | tf_op jit(solution)/shard_map/kc,fcv->kfv/dot_general | solution.py:143
  36.6 0.0 copy-done.1
  36.6 0.6 add.103.seg_ref
  37.2 2.3 %add_select_fusion = (s32[2048,128]{1,0:T(8,128)}, s32[2048,128]{1,0:T(8,128)}) fusion(s32[1,1,2048,128]{3,2,1,0:T(8,128)S(1)} %copy-done), kind=kLoop, calls=%fused_computation.7 | loop fusion | flops 3145728 | bytes 3145728 | tf_op jit(solution)/shard_map/jit(remainder)/select_n | solution.py:134
  39.5 3.0 %all-to-all-done = bf16[16,64,512]{2,0,1:T(8,128)(2,1)S(1)} async-done(((bf16[16,64,512]{2,0,1:T(8,128)(2,1)}), bf16[16,64,512]{2,0,1:T(8,128)(2,1)S(1)}, u32[]{:S(2)}, u32[]{:S(2)}) %all-to-all-start) | async-done | bytes 1048608 | tf_op jit(solution)/shard_map/all_to_all | solution.py:117
  42.5 0.1 copy.22
  42.6 0.1 fusion.48
  42.7 0.7 fusion
  43.4 0.2 fusion.12
  43.6 1.1 reshape.573.re_ref
  44.6 1.1 reshape.574.im_ref
  45.7 37.6 %shard_map.55 = f32[16,128,256]{2,1,0:T(8,128)} custom-call(s32[2048]{0:T(1024)} %add.103.seg_ref, s32[2048,128]{1,0:T(8,128)} %get-tuple-element.14.du_ref, s32[2048,128]{1,0:T(8,128)} %get-tuple-element.13.dv_ref, f32[2048,128]{1,0:T(8,128)} %reshape.573.re_ref, f32[2048,128]{1,0:T(8,128)} %reshape.574.im_ref), custom_call_target="tpu_custom_call" | custom-call | flops 1073741824 | bytes 6291456 | tf_op jit(solution)/shard_map/pallas_call | solution.py:79
  83.3 1.6 %reshape.578 = f32[16,256,128,1]{2,1,0,3:T(8,128)S(1)} reshape(f32[16,128,256]{2,1,0:T(8,128)} %shard_map.55) | data formatting | bytes 4194304 | tf_op jit(solution)/shard_map/reshape | solution.py:143
  84.9 1.9 %convolution_bitcast_fusion = f32[16,32,8,128]{3,2,0,1:T(8,128)S(1)} fusion(f32[16,256,128,1]{2,1,0,3:T(8,128)S(1)} %reshape.578, f32[32,8,256,1]{2,1,0,3:T(8,128)S(1)} %reshape.577), kind=kOutput, calls=%fused_computation.6 | convolution fusion | flops 1610612736 | bytes 4456448 | tf_op jit(solution)/shard_map/kc,fcv->kfv/dot_general | solution.py:143
  86.9 1.5 copy.23
  88.4 14.6 %all-to-all-start.1 = ((f32[512,8,128]{2,1,0:T(8,128)}), f32[512,8,128]{2,1,0:T(8,128)S(1)}, u32[]{:S(2)}, u32[]{:S(2)}) async-start(f32[512,8,128]{2,1,0:T(8,128)} %bitcast.71), calls=%async_computation.1 | async-start | bytes 4194304 | tf_op jit(solution)/shard_map/all_to_all | solution.py:146
  103.0 0.1 multiply_reduce_fusion.3
  103.1 0.1 dynamic_slice.7
  103.2 0.1 dynamic_slice.6
  103.2 0.1 multiply_reduce_fusion.2
  103.3 0.3 fusion.35
  103.6 0.3 fusion.30
  103.9 54.9 %all-to-all-done.1 = f32[512,8,128]{2,1,0:T(8,128)S(1)} async-done(((f32[512,8,128]{2,1,0:T(8,128)}), f32[512,8,128]{2,1,0:T(8,128)S(1)}, u32[]{:S(2)}, u32[]{:S(2)}) %all-to-all-start.1) | async-done | bytes 2097184 | tf_op jit(solution)/shard_map/all_to_all | solution.py:146
  158.8 0.5 reduce_sum.47
  159.4 0.2 convolution_bitcast_fusion.1
  159.5 0.1 subtract_multiply_fusion
  159.7 0.6 pad_maximum_fusion.1
  (15 shorter events, 0.1 us)
Async XLA Ops:
  2.8 39.8 %all-to-all-start = ((bf16[16,64,512]{2,0,1:T(8,128)(2,1)}), bf16[16,64,512]{2,0,1:T(8,128)(2,1)S(1)}, u32[]{:S(2)}, u32[]{:S(2)}) async-start(bf16[16,64,512]{2,0,1:T(8,128)(2,1)} %copy.21), calls=%async_computation | async-start | bytes 2097152 | tf_op jit(solution)/shard_map/all_to_all | solution.py:117
  23.8 12.8 %copy-start.2 = (s32[1,1,2048,1]{2,3,1,0:T(1,128)S(1)}, s32[1,1,2048,1]{2,3,1,0:T(1,128)}, u32[]{:S(2)}) copy-start(s32[1,1,2048,1]{2,3,1,0:T(1,128)} %param.6) | copy-start | bytes 24580
  23.8 12.8 %copy-start.1 = (s32[1,1,2048]{2,1,0:T(1,128)S(1)}, s32[1,1,2048]{2,1,0:T(1,128)}, u32[]{:S(2)}) copy-start(s32[1,1,2048]{2,1,0:T(1,128)} %param.7) | copy-start | bytes 24580
  23.8 13.4 %copy-start = (s32[1,1,2048,128]{3,2,1,0:T(8,128)S(1)}, s32[1,1,2048,128]{3,2,1,0:T(8,128)}, u32[]{:S(2)}) copy-start(s32[1,1,2048,128]{3,2,1,0:T(8,128)} %param.8) | copy-start | bytes 3145732
  88.4 14.6 %copy-start.3 = (bf16[2,8]{1,0:T(2,128)(2,1)S(1)}, bf16[2,8]{1,0:T(2,128)(2,1)}, u32[]{:S(2)}) copy-start(bf16[2,8]{1,0:T(2,128)(2,1)} %param.9) | copy-start | bytes 100
  88.4 70.4 %all-to-all-start.1 = ((f32[512,8,128]{2,1,0:T(8,128)}), f32[512,8,128]{2,1,0:T(8,128)S(1)}, u32[]{:S(2)}, u32[]{:S(2)}) async-start(f32[512,8,128]{2,1,0:T(8,128)} %bitcast.71), calls=%async_computation.1 | async-start | bytes 4194304 | tf_op jit(solution)/shard_map/all_to_all | solution.py:146

commit v15 on v14

--- a/solution.py
+++ b/solution.py
@@ -47,7 +47,7 @@
         acc_ref[facet, tile % TS, pl.ds(first_u, TILE), :] += tile_sum
         return carry
 
-    lax.fori_loop(0, CHUNK, one_block, 0, unroll=64)
+    lax.fori_loop(0, CHUNK, one_block, 0, unroll=128)
 
     @pl.when(step == pl.num_programs(0) - 1)
     def _():

time: 161 us -> 160 us (level)
  no operation moved by 1% of the time
where the time goes in v15:
time: 160 us
  waiting for transfers between devices  57.9 us (36%)
  Pallas kernels  37.2 us (23%)
  local copies, waits for them, and re-layouts  29.6 us (18%)
  starting transfers between devices  26.4 us (16%)
  other arithmetic  5.72 us (4%)
  matrix products  2.84 us (2%)
    all_to_all x1, waiting for transfers between devices, body(): lax.all_to_all(rows, ('stn', 'chan'), split_axis=0, concat_axis=0, tiled=...  54.9 us
    pallas_call x1, Pallas kernels, grid_blocks(): pl.pallas_call(grid_kernel, out_shape=jax.ShapeDtypeStruct((facets, side,...  37.2 us
    all_to_all x1, starting transfers between devices, body(): lax.all_to_all(rows, ('stn', 'chan'), split_axis=0, concat_axis=0, tiled=...  14.5 us
    dot_general x1, local copies, waits for them, and re-layouts, body(): jnp.einsum('kc,fcv->kfv', along_x, delta.reshape(facets, 2 * side, side),...  12.8 us
    all_to_all x1, starting transfers between devices, body(): lax.all_to_all(voltages, 'stn', split_axis=1, concat_axis=0, tiled=True)  11.8 us
    another operation x1, local copies, waits for them, and re-layouts, body(): jnp.stack([jnp.stack([cosine, sine], axis=2), jnp.stack([-sine, cosine],...  8.56 us
  transfers between devices with their start and end apart: 2, of which 2 were waited for; matrix products, arithmetic and copies ran while one was open for 16% of the time, Pallas kernels for 0%

profile of v15, /device:TPU:1, one launch (start us, length us, event | category | flops | bytes accessed | tf_op | source)
XLA Modules:
  0.0 159.9 jit_solution(11323615762135769562)
XLA Ops:
  0.0 2.8 %copy.21 = bf16[16,64,512]{2,0,1:T(8,128)(2,1)} copy(bf16[16,64,512]{2,1,0:T(8,128)(2,1)} %param.5) | data formatting | bytes 2097152 | tf_op args[0]
  2.8 11.8 %all-to-all-start = ((bf16[16,64,512]{2,0,1:T(8,128)(2,1)}), bf16[16,64,512]{2,0,1:T(8,128)(2,1)S(1)}, u32[]{:S(2)}, u32[]{:S(2)}) async-start(bf16[16,64,512]{2,0,1:T(8,128)(2,1)} %copy.21), calls=%async_computation | async-start | bytes 2097152 | tf_op jit(solution)/shard_map/all_to_all | solution.py:117
  14.6 0.3 fusion.34
  14.9 0.3 fusion.32
  15.2 8.6 %copy.20 = f32[128,2,128,2]{3,2,1,0:T(8,128)} copy(f32[128,2,128,2]{2,0,3,1:T(8,128)S(1)} %pad_maximum_fusion) | data formatting | bytes 524288 | tf_op jit(solution)/shard_map/stack | solution.py:140
  23.8 12.8 %reshape.577 = f32[32,8,256,1]{2,1,0,3:T(8,128)S(1)} reshape(f32[128,2,128,2]{3,2,1,0:T(8,128)} %copy.20) | data formatting | bytes 524288 | tf_op jit(solution)/shard_map/kc,fcv->kfv/dot_general | solution.py:143
  36.6 0.6 add.103.seg_ref
  37.2 2.3 %add_select_fusion = (s32[2048,128]{1,0:T(8,128)}, s32[2048,128]{1,0:T(8,128)}) fusion(s32[1,1,2048,128]{3,2,1,0:T(8,128)S(1)} %copy-done), kind=kLoop, calls=%fused_computation.7 | loop fusion | flops 3145728 | bytes 3145728 | tf_op jit(solution)/shard_map/jit(remainder)/select_n | solution.py:134
  39.5 3.0 %all-to-all-done = bf16[16,64,512]{2,0,1:T(8,128)(2,1)S(1)} async-done(((bf16[16,64,512]{2,0,1:T(8,128)(2,1)}), bf16[16,64,512]{2,0,1:T(8,128)(2,1)S(1)}, u32[]{:S(2)}, u32[]{:S(2)}) %all-to-all-start) | async-done | bytes 1048608 | tf_op jit(solution)/shard_map/all_to_all | solution.py:117
  42.5 0.1 copy.22
  42.6 0.1 fusion.48
  42.7 0.7 fusion
  43.4 0.2 fusion.12
  43.6 1.1 reshape.573.re_ref
  44.6 1.1 reshape.574.im_ref
  45.7 37.2 %shard_map.55 = f32[16,128,256]{2,1,0:T(8,128)} custom-call(s32[2048]{0:T(1024)} %add.103.seg_ref, s32[2048,128]{1,0:T(8,128)} %get-tuple-element.14.du_ref, s32[2048,128]{1,0:T(8,128)} %get-tuple-element.13.dv_ref, f32[2048,128]{1,0:T(8,128)} %reshape.573.re_ref, f32[2048,128]{1,0:T(8,128)} %reshape.574.im_ref), custom_call_target="tpu_custom_call" | custom-call | flops 1073741824 | bytes 6291456 | tf_op jit(solution)/shard_map/pallas_call | solution.py:79
  83.0 1.6 %reshape.578 = f32[16,256,128,1]{2,1,0,3:T(8,128)S(1)} reshape(f32[16,128,256]{2,1,0:T(8,128)} %shard_map.55) | data formatting | bytes 4194304 | tf_op jit(solution)/shard_map/reshape | solution.py:143
  84.6 1.9 %convolution_bitcast_fusion = f32[16,32,8,128]{3,2,0,1:T(8,128)S(1)} fusion(f32[16,256,128,1]{2,1,0,3:T(8,128)S(1)} %reshape.578, f32[32,8,256,1]{2,1,0,3:T(8,128)S(1)} %reshape.577), kind=kOutput, calls=%fused_computation.6 | convolution fusion | flops 1610612736 | bytes 4456448 | tf_op jit(solution)/shard_map/kc,fcv->kfv/dot_general | solution.py:143
  86.5 1.5 copy.23
  88.1 14.5 %all-to-all-start.1 = ((f32[512,8,128]{2,1,0:T(8,128)}), f32[512,8,128]{2,1,0:T(8,128)S(1)}, u32[]{:S(2)}, u32[]{:S(2)}) async-start(f32[512,8,128]{2,1,0:T(8,128)} %bitcast.71), calls=%async_computation.1 | async-start | bytes 4194304 | tf_op jit(solution)/shard_map/all_to_all | solution.py:146
  102.6 0.0 copy-done.3
  102.6 0.1 multiply_reduce_fusion.3
  102.7 0.1 dynamic_slice.7
  102.8 0.1 dynamic_slice.6
  102.9 0.1 multiply_reduce_fusion.2
  103.0 0.3 fusion.35
  103.2 0.3 fusion.30
  103.5 54.9 %all-to-all-done.1 = f32[512,8,128]{2,1,0:T(8,128)S(1)} async-done(((f32[512,8,128]{2,1,0:T(8,128)}), f32[512,8,128]{2,1,0:T(8,128)S(1)}, u32[]{:S(2)}, u32[]{:S(2)}) %all-to-all-start.1) | async-done | bytes 2097184 | tf_op jit(solution)/shard_map/all_to_all | solution.py:146
  158.5 0.5 reduce_sum.47
  159.0 0.2 convolution_bitcast_fusion.1
  159.2 0.1 subtract_multiply_fusion
  159.3 0.6 pad_maximum_fusion.1
  (15 shorter events, 0.1 us)
Async XLA Ops:
  2.8 39.8 %all-to-all-start = ((bf16[16,64,512]{2,0,1:T(8,128)(2,1)}), bf16[16,64,512]{2,0,1:T(8,128)(2,1)S(1)}, u32[]{:S(2)}, u32[]{:S(2)}) async-start(bf16[16,64,512]{2,0,1:T(8,128)(2,1)} %copy.21), calls=%async_computation | async-start | bytes 2097152 | tf_op jit(solution)/shard_map/all_to_all | solution.py:117
  23.8 12.8 %copy-start.2 = (s32[1,1,2048,1]{2,3,1,0:T(1,128)S(1)}, s32[1,1,2048,1]{2,3,1,0:T(1,128)}, u32[]{:S(2)}) copy-start(s32[1,1,2048,1]{2,3,1,0:T(1,128)} %param.6) | copy-start | bytes 24580
  23.8 12.8 %copy-start.1 = (s32[1,1,2048]{2,1,0:T(1,128)S(1)}, s32[1,1,2048]{2,1,0:T(1,128)}, u32[]{:S(2)}) copy-start(s32[1,1,2048]{2,1,0:T(1,128)} %param.7) | copy-start | bytes 24580
  23.8 13.4 %copy-start = (s32[1,1,2048,128]{3,2,1,0:T(8,128)S(1)}, s32[1,1,2048,128]{3,2,1,0:T(8,128)}, u32[]{:S(2)}) copy-start(s32[1,1,2048,128]{3,2,1,0:T(8,128)} %param.8) | copy-start | bytes 3145732
  88.1 14.6 %copy-start.3 = (bf16[2,8]{1,0:T(2,128)(2,1)S(1)}, bf16[2,8]{1,0:T(2,128)(2,1)}, u32[]{:S(2)}) copy-start(bf16[2,8]{1,0:T(2,128)(2,1)} %param.9) | copy-start | bytes 100
  88.1 70.4 %all-to-all-start.1 = ((f32[512,8,128]{2,1,0:T(8,128)}), f32[512,8,128]{2,1,0:T(8,128)S(1)}, u32[]{:S(2)}, u32[]{:S(2)}) async-start(f32[512,8,128]{2,1,0:T(8,128)} %bitcast.71), calls=%async_computation.1 | async-start | bytes 4194304 | tf_op jit(solution)/shard_map/all_to_all | solution.py:146

commit v16 on v15

--- a/solution.py
+++ b/solution.py
@@ -17,7 +17,7 @@
 CHUNK = 2048
 
 
-def grid_kernel(seg_ref, du_ref, dv_ref, re_ref, im_ref, out_ref, acc_ref):
+def grid_kernel(seg_ref, du_ref, re_ref, im_ref, out_ref, acc_ref):
     step = pl.program_id(0)
     side = TS * TILE
 
@@ -28,8 +28,9 @@
     cells = lax.broadcasted_iota(jnp.int32, (TILE, VB), 0)
 
     def one_block(b, carry):
-        du = du_ref[pl.ds(b, 1), :]
-        dv = dv_ref[pl.ds(b, 1), :]
+        code = du_ref[pl.ds(b, 1), :]
+        du = code // TILE
+        dv = code % TILE
         re = re_ref[pl.ds(b, 1), :]
         im = im_ref[pl.ds(b, 1), :]
         seg = seg_ref[step * CHUNK + b]
@@ -72,7 +73,7 @@
         lax.fori_loop(0, out_ref.shape[0], one_facet, 0)
 
 
-def grid_blocks(seg_ids, du, dv, re, im, facets):
+def grid_blocks(seg_ids, du, re, im, facets):
     blocks = du.shape[0]
     side = TS * TILE
     row_spec = pl.BlockSpec((CHUNK, VB), lambda i, seg: (i, 0))
@@ -82,7 +83,7 @@
         grid_spec=pltpu.PrefetchScalarGridSpec(
             num_scalar_prefetch=1,
             grid=(blocks // CHUNK,),
-            in_specs=[row_spec] * 4,
+            in_specs=[row_spec] * 3,
             out_specs=pl.BlockSpec((facets, side, 2 * side), lambda i, seg: (0, 0, 0)),
             scratch_shapes=[pltpu.VMEM((facets, TS, side, 2 * TILE), jnp.float32)],
         ),
@@ -91,7 +92,7 @@
             bytes_accessed=blocks * VB * 16 + facets * side * 2 * side * 4,
             transcendentals=0,
         ),
-    )(seg_ids, du, dv, re, im)
+    )(seg_ids, du, re, im)
 
 
 def dft_tables(side):
@@ -133,7 +134,7 @@
     du = offsets // OFFS
     dv = offsets % OFFS
     seg_ids = block_facet.reshape(block_count) * TT + block_tile.reshape(block_count)
-    delta = grid_blocks(seg_ids, du, dv, re, im, facets)
+    delta = grid_blocks(seg_ids, du * TILE + dv, re, im, facets)
     side = TS * TILE
     row_count = side // chan_count
     cosine, sine = dft_tables(side)

time: 160 us -> 160 us (level)
    select_n x1 -> x0, other arithmetic: 2.29 us -> none  [body(): dv = offsets % OFFS]
    add x0 -> x1, other arithmetic: none -> 2.05 us  [body(): delta = grid_blocks(seg_ids, du * TILE + dv, re, im, facets)]
where the time goes in v16:
time: 160 us; the launch traced here: 159 us
  waiting for transfers between devices  58.2 us (36%)
  Pallas kernels  37 us (23%)
  local copies, waits for them, and re-layouts  29.6 us (18%)
  starting transfers between devices  26.1 us (16%)
  other arithmetic  5.47 us (3%)
  matrix products  2.83 us (2%)
    all_to_all x1, waiting for transfers between devices, body(): lax.all_to_all(rows, ('stn', 'chan'), split_axis=0, concat_axis=0, tiled=...  54.9 us
    pallas_call x1, Pallas kernels, grid_blocks(): pl.pallas_call(grid_kernel, out_shape=jax.ShapeDtypeStruct((facets, side,...  37 us
    all_to_all x1, starting transfers between devices, body(): lax.all_to_all(rows, ('stn', 'chan'), split_axis=0, concat_axis=0, tiled=...  14.3 us
    dot_general x1, local copies, waits for them, and re-layouts, body(): jnp.einsum('kc,fcv->kfv', along_x, delta.reshape(facets, 2 * side, side),...  12.8 us
    all_to_all x1, starting transfers between devices, body(): lax.all_to_all(voltages, 'stn', split_axis=1, concat_axis=0, tiled=True)  11.8 us
    another operation x1, local copies, waits for them, and re-layouts, body(): jnp.stack([jnp.stack([cosine, sine], axis=2), jnp.stack([-sine, cosine],...  8.56 us
    all_to_all x1, waiting for transfers between devices, body(): lax.all_to_all(voltages, 'stn', split_axis=1, concat_axis=0, tiled=True)  3.27 us
  transfers between devices with their start and end apart: 2, of which 2 were waited for; matrix products, arithmetic and copies ran while one was open for 16% of the time, Pallas kernels for 0%

profile of v16, /device:TPU:1, one launch (start us, length us, event | category | flops | bytes accessed | tf_op | source)
XLA Modules:
  0.0 159.4 jit_solution(12038987904982500994)
XLA Ops:
  0.0 2.8 %copy.21 = bf16[16,64,512]{2,0,1:T(8,128)(2,1)} copy(bf16[16,64,512]{2,1,0:T(8,128)(2,1)} %param.5) | data formatting | bytes 2097152 | tf_op args[0]
  2.8 11.8 %all-to-all-start = ((bf16[16,64,512]{2,0,1:T(8,128)(2,1)}), bf16[16,64,512]{2,0,1:T(8,128)(2,1)S(1)}, u32[]{:S(2)}, u32[]{:S(2)}) async-start(bf16[16,64,512]{2,0,1:T(8,128)(2,1)} %copy.21), calls=%async_computation | async-start | bytes 2097152 | tf_op jit(solution)/shard_map/all_to_all | solution.py:118
  14.6 0.3 fusion.36
  14.9 0.3 fusion.34
  15.2 8.6 %copy.20 = f32[128,2,128,2]{3,2,1,0:T(8,128)} copy(f32[128,2,128,2]{2,0,3,1:T(8,128)S(1)} %pad_maximum_fusion) | data formatting | bytes 524288 | tf_op jit(solution)/shard_map/stack | solution.py:141
  23.8 12.8 %reshape.577 = f32[32,8,256,1]{2,1,0,3:T(8,128)S(1)} reshape(f32[128,2,128,2]{3,2,1,0:T(8,128)} %copy.20) | data formatting | bytes 524288 | tf_op jit(solution)/shard_map/kc,fcv->kfv/dot_general | solution.py:144
  36.6 0.6 add.106.seg_ref
  37.2 0.0 copy-done
  37.2 2.0 %fusion.7.du_ref = s32[2048,128]{1,0:T(8,128)} fusion(s32[1,1,2048,128]{3,2,1,0:T(8,128)S(1)} %copy-done), kind=kLoop, calls=%fused_computation.11 | loop fusion | flops 3670016 | bytes 2097152 | tf_op jit(solution)/shard_map/add | solution.py:137
  39.3 3.3 %all-to-all-done = bf16[16,64,512]{2,0,1:T(8,128)(2,1)S(1)} async-done(((bf16[16,64,512]{2,0,1:T(8,128)(2,1)}), bf16[16,64,512]{2,0,1:T(8,128)(2,1)S(1)}, u32[]{:S(2)}, u32[]{:S(2)}) %all-to-all-start) | async-done | bytes 1048608 | tf_op jit(solution)/shard_map/all_to_all | solution.py:118
  42.5 0.1 copy.22
  42.6 0.1 fusion.50
  42.7 0.7 fusion
  43.4 0.2 fusion.14
  43.6 1.1 reshape.573.re_ref
  44.6 1.0 reshape.574.im_ref
  45.7 37.0 %shard_map.55 = f32[16,128,256]{2,1,0:T(8,128)} custom-call(s32[2048]{0:T(1024)} %add.106.seg_ref, s32[2048,128]{1,0:T(8,128)} %fusion.7.du_ref, f32[2048,128]{1,0:T(8,128)} %reshape.573.re_ref, f32[2048,128]{1,0:T(8,128)} %reshape.574.im_ref), custom_call_target="tpu_custom_call" | custom-call | flops 1073741824 | bytes 6291456 | tf_op jit(solution)/shard_map/pallas_call | solution.py:80
  82.7 1.6 %reshape.578 = f32[16,256,128,1]{2,1,0,3:T(8,128)S(1)} reshape(f32[16,128,256]{2,1,0:T(8,128)} %shard_map.55) | data formatting | bytes 4194304 | tf_op jit(solution)/shard_map/reshape | solution.py:144
  84.4 1.9 %convolution_bitcast_fusion = f32[16,32,8,128]{3,2,0,1:T(8,128)S(1)} fusion(f32[16,256,128,1]{2,1,0,3:T(8,128)S(1)} %reshape.578, f32[32,8,256,1]{2,1,0,3:T(8,128)S(1)} %reshape.577), kind=kOutput, calls=%fused_computation.6 | convolution fusion | flops 1610612736 | bytes 4456448 | tf_op jit(solution)/shard_map/kc,fcv->kfv/dot_general | solution.py:144
  86.3 1.5 copy.23
  87.8 14.3 %all-to-all-start.1 = ((f32[512,8,128]{2,1,0:T(8,128)}), f32[512,8,128]{2,1,0:T(8,128)S(1)}, u32[]{:S(2)}, u32[]{:S(2)}) async-start(f32[512,8,128]{2,1,0:T(8,128)} %bitcast.69), calls=%async_computation.1 | async-start | bytes 4194304 | tf_op jit(solution)/shard_map/all_to_all | solution.py:147
  102.2 0.1 multiply_reduce_fusion.3
  102.3 0.1 dynamic_slice.7
  102.3 0.1 dynamic_slice.6
  102.4 0.1 multiply_reduce_fusion.2
  102.5 0.3 fusion.37
  102.8 0.3 fusion.32
  103.1 54.9 %all-to-all-done.1 = f32[512,8,128]{2,1,0:T(8,128)S(1)} async-done(((f32[512,8,128]{2,1,0:T(8,128)}), f32[512,8,128]{2,1,0:T(8,128)S(1)}, u32[]{:S(2)}, u32[]{:S(2)}) %all-to-all-start.1) | async-done | bytes 2097184 | tf_op jit(solution)/shard_map/all_to_all | solution.py:147
  158.0 0.5 reduce_sum.47
  158.5 0.2 convolution_bitcast_fusion.1
  158.7 0.1 subtract_multiply_fusion
  158.8 0.6 pad_maximum_fusion.1
  (15 shorter events, 0.1 us)
Async XLA Ops:
  2.8 39.8 %all-to-all-start = ((bf16[16,64,512]{2,0,1:T(8,128)(2,1)}), bf16[16,64,512]{2,0,1:T(8,128)(2,1)S(1)}, u32[]{:S(2)}, u32[]{:S(2)}) async-start(bf16[16,64,512]{2,0,1:T(8,128)(2,1)} %copy.21), calls=%async_computation | async-start | bytes 2097152 | tf_op jit(solution)/shard_map/all_to_all | solution.py:118
  23.8 12.8 %copy-start.2 = (s32[1,1,2048,1]{2,3,1,0:T(1,128)S(1)}, s32[1,1,2048,1]{2,3,1,0:T(1,128)}, u32[]{:S(2)}) copy-start(s32[1,1,2048,1]{2,3,1,0:T(1,128)} %param.6) | copy-start | bytes 24580
  23.8 12.8 %copy-start.1 = (s32[1,1,2048]{2,1,0:T(1,128)S(1)}, s32[1,1,2048]{2,1,0:T(1,128)}, u32[]{:S(2)}) copy-start(s32[1,1,2048]{2,1,0:T(1,128)} %param.7) | copy-start | bytes 24580
  23.8 13.4 %copy-start = (s32[1,1,2048,128]{3,2,1,0:T(8,128)S(1)}, s32[1,1,2048,128]{3,2,1,0:T(8,128)}, u32[]{:S(2)}) copy-start(s32[1,1,2048,128]{3,2,1,0:T(8,128)} %param.8) | copy-start | bytes 3145732
  87.8 14.3 %copy-start.3 = (bf16[2,8]{1,0:T(2,128)(2,1)S(1)}, bf16[2,8]{1,0:T(2,128)(2,1)}, u32[]{:S(2)}) copy-start(bf16[2,8]{1,0:T(2,128)(2,1)} %param.9) | copy-start | bytes 100
  87.8 70.2 %all-to-all-start.1 = ((f32[512,8,128]{2,1,0:T(8,128)}), f32[512,8,128]{2,1,0:T(8,128)S(1)}, u32[]{:S(2)}, u32[]{:S(2)}) async-start(f32[512,8,128]{2,1,0:T(8,128)} %bitcast.69), calls=%async_computation.1 | async-start | bytes 4194304 | tf_op jit(solution)/shard_map/all_to_all | solution.py:147
